TPU v7x, 32 devices: a whole 2x2x4 slice. The times are simulated.
32 devices in a mesh: dp: 2 (over x), ctx: 4 (over y, core), tensor: 4 (over z).
Axes of the slice: x: 2, y: 2, z: 4, core: 2. Of those that a mesh axis runs over, the one named last changes fastest.
Arguments:
- hidden: bfloat16 [2, 8, 1024, 768], P(None, ('dp', 'tensor'), 'ctx'), may hold values from -6 to 6
- segment_ids: int32 [2, 8, 1024], P(None, ('dp', 'tensor')), may hold values from 0 to 3, never falling along the last dimension, each value on 1 to 512 neighbouring positions
- w_in: bfloat16 [768, 1536], P('dp'), may hold values from -0.21875 to 0.21875
- w_depth: bfloat16 [768, 9], P('dp'), may hold values from -2 to 2
- w_point: bfloat16 [768, 384], P('dp'), may hold values from -0.21875 to 0.21875
- w_kernel: bfloat16 [384, 54], P('dp'), may hold values from -0.3125 to 0.3125
- w_out: bfloat16 [768, 768], P('dp'), may hold values from -2 to 2
- norm1_gain: bfloat16 [768], P('dp'), may hold values from 0.5 to 1.5
- norm1_bias: bfloat16 [768], P('dp'), may hold values from -3 to 3
- norm2_gain: bfloat16 [768], P('dp'), may hold values from 0.5 to 1.5
- norm2_bias: bfloat16 [768], P('dp'), may hold values from -3 to 3
- w_up: bfloat16 [384, 2, 1536], P('dp', None, 'tensor'), may hold values from -0.3125 to 0.3125
- w_down: bfloat16 [384, 2, 1536], P('dp', None, 'tensor'), may hold values from -0.15625 to 0.15625
- out_grad: bfloat16 [2, 8, 1024, 768], P(None, ('dp', 'tensor'), 'ctx'), may hold values from -6 to 6
Outputs:
- output: bfloat16 [2, 8, 1024, 768], P(None, ('dp', 'tensor'), 'ctx')
- input_grad: bfloat16 [2, 8, 1024, 768], P(None, ('dp', 'tensor'), 'ctx')
- w_in_grad: float32 [768, 1536], P('dp')
- w_depth_grad: float32 [768, 9], P('dp')
- w_point_grad: float32 [768, 384], P('dp')
- w_kernel_grad: float32 [384, 54], P('dp')
- w_out_grad: float32 [768, 768], P('dp')
- norm1_gain_grad: float32 [768], P('dp')
- norm1_bias_grad: float32 [768], P('dp')
- norm2_gain_grad: float32 [768], P('dp')
- norm2_bias_grad: float32 [768], P('dp')
- w_up_grad: float32 [384, 2, 1536], P('dp', None, 'tensor')
- w_down_grad: float32 [384, 2, 1536], P('dp', None, 'tensor')
Inputs may be any that keep to these rules, and one draw needn't show every extreme that they name: `segment_ids`: along each sequence the numbers never fall; every document has 1 to 512 positions, and one has exactly 512.
All inputs are finite; a program needn't handle non-finite values.
Results may differ from a plain program's by a relative error of at most 0.017.
Values may be sent and summed in bfloat16 or wider, within the bound.
No kernel may reach another device: no remote copies, remote signals or barrier semaphores. Data moves between devices by JAX's collectives and lax.ppermute only.
A program may use at most 256 MiB of HBM per device.

v0:
```python
import math

import jax
import jax.numpy as jnp
from jax import lax
from jax.sharding import PartitionSpec as P

D = 768
HEADS = 6
HEAD_DIM = 64
KERNEL = 9
GROUPS = 2
MICRO = 2


NORM_EPS = 1e-05
NEG_FILL = -1e30
HIGHEST = lax.Precision.HIGHEST


def padded(block, sides, width):
    for axis, dim in sides:
        count = lax.axis_size(axis)
        forward = [(i, i + 1) for i in range(count - 1)]
        backward = [(target, source) for source, target in forward]
        low = lax.ppermute(
            lax.slice_in_dim(block, block.shape[dim] - width, None, axis=dim), axis, forward
        )
        high = lax.ppermute(lax.slice_in_dim(block, 0, width, axis=dim), axis, backward)
        block = jnp.concatenate([low, block, high], axis=dim)
    return block


def gelu_exact(values):
    return 0.5 * values * (1.0 + jax.scipy.special.erf(values * 0.7071067811865476))


def softmax_last(values):
    shifted = values - jnp.max(values, axis=-1, keepdims=True)
    expo_vals = jnp.exp(shifted)
    return expo_vals / jnp.sum(expo_vals, axis=-1, keepdims=True)


def rows_product(left, right):
    return lax.dot_general(
        left, right, (((0,), (0,)), ((), ())), preferred_element_type=jnp.float32
    )


def times_transposed(left, right):
    return lax.dot_general(
        left, right, (((1,), (1,)), ((), ())), preferred_element_type=jnp.float32
    )


def norm_forward(values, gain_vec, bias_vec):
    average = jnp.mean(values, axis=-1, keepdims=True)
    centred = values - average
    inverse = lax.rsqrt(jnp.mean(centred * centred, axis=-1, keepdims=True) + NORM_EPS)
    normalized = centred * inverse
    return (normalized * gain_vec + bias_vec, normalized, inverse)


def norm_backward(grad_out, normalized, inverse, gain_vec):
    scaled = grad_out * gain_vec
    inner = (
        scaled
        - jnp.mean(scaled, axis=-1, keepdims=True)
        - normalized * jnp.mean(scaled * normalized, axis=-1, keepdims=True)
    )
    return (inner * inverse, jnp.sum(grad_out * normalized, axis=0), jnp.sum(grad_out, axis=0))


def meets(query_ids, key_ids):
    return jnp.logical_and(key_ids[0] <= query_ids[-1], key_ids[-1] >= query_ids[0])


def block_scores(heads_q, key_block, query_ids, key_ids, score_scale):
    raw_scores = (
        jnp.einsum("qhd,khd->hqk", heads_q, key_block, preferred_element_type=jnp.float32)
        * score_scale
    )
    return jnp.where((query_ids[:, None] == key_ids[None, :])[None], raw_scores, NEG_FILL)


def keep_state(state):
    return state


def log_totals(heads_q, key_blocks, query_ids, id_blocks, score_scale):
    head_count = heads_q.shape[1]
    row_count = heads_q.shape[0]

    def log_scan_step(carried, inputs):

        def log_visit(state):
            running, summed = state
            scores = block_scores(heads_q, inputs[0], query_ids, inputs[1], score_scale)
            highest = jnp.maximum(running, jnp.max(scores, axis=-1))
            summed = summed * jnp.exp(running - highest) + jnp.sum(
                jnp.exp(scores - highest[..., None]), axis=-1
            )
            return (highest, summed)

        return (lax.cond(meets(query_ids, inputs[1]), log_visit, keep_state, carried), None)

    start_state = (
        jnp.full((head_count, row_count), NEG_FILL, jnp.float32),
        jnp.zeros((head_count, row_count), jnp.float32),
    )
    final_state, unused = lax.scan(log_scan_step, start_state, (key_blocks, id_blocks))
    return final_state[0] + jnp.log(final_state[1])


def attend(heads_q, key_blocks, value_blocks, query_ids, id_blocks, log_total, score_scale):

    def attend_scan_step(carried, inputs):

        def attend_visit(state):
            scores = block_scores(heads_q, inputs[0], query_ids, inputs[2], score_scale)
            weights = jnp.exp(scores - log_total[..., None]).astype(jnp.bfloat16)
            return state + jnp.einsum(
                "hqk,khd->qhd", weights, inputs[1], preferred_element_type=jnp.float32
            )

        return (lax.cond(meets(query_ids, inputs[2]), attend_visit, keep_state, carried), None)

    result, unused = lax.scan(
        attend_scan_step,
        jnp.zeros(heads_q.shape, jnp.float32),
        (key_blocks, value_blocks, id_blocks),
    )
    return result


def delta_pass(
    heads_q, grad_heads, key_blocks, value_blocks, query_ids, id_blocks, log_total, score_scale
):

    def delta_scan_step(carried, inputs):

        def delta_visit(state):
            scores = block_scores(heads_q, inputs[0], query_ids, inputs[2], score_scale)
            attn_probs = jnp.exp(scores - log_total[..., None])
            grad_probs = jnp.einsum(
                "qhd,khd->hqk", grad_heads, inputs[1], preferred_element_type=jnp.float32
            )
            return state + jnp.sum(attn_probs * grad_probs, axis=-1)

        return (lax.cond(meets(query_ids, inputs[2]), delta_visit, keep_state, carried), None)

    result, unused = lax.scan(
        delta_scan_step,
        jnp.zeros(log_total.shape, jnp.float32),
        (key_blocks, value_blocks, id_blocks),
    )
    return result


def score_grads(
    heads_q, grad_heads, key_block, value_block, query_ids, key_ids, log_total, delta, score_scale
):
    scores = block_scores(heads_q, key_block, query_ids, key_ids, score_scale)
    attn_probs = jnp.exp(scores - log_total[..., None])
    grad_probs = jnp.einsum(
        "qhd,khd->hqk", grad_heads, value_block, preferred_element_type=jnp.float32
    )
    grad_scores = (attn_probs * (grad_probs - delta[..., None])).astype(jnp.bfloat16)
    return (grad_scores, attn_probs.astype(jnp.bfloat16))


def full_grad_pass(
    heads_q,
    grad_heads,
    key_blocks,
    value_blocks,
    query_ids,
    id_blocks,
    log_total,
    delta,
    score_scale,
):

    def full_scan_step(carried, inputs):
        key_block, value_block, key_ids = inputs
        block_len = key_block.shape[0]
        pair_width = 2 * key_block.shape[1] * key_block.shape[2]

        def full_visit(grad_query):
            grad_scores, probs_low = score_grads(
                heads_q,
                grad_heads,
                key_block,
                value_block,
                query_ids,
                key_ids,
                log_total,
                delta,
                score_scale,
            )
            grad_query = (
                grad_query
                + jnp.einsum(
                    "hqk,khd->qhd", grad_scores, key_block, preferred_element_type=jnp.float32
                )
                * score_scale
            )
            key_grad = (
                jnp.einsum("hqk,qhd->khd", grad_scores, heads_q, preferred_element_type=jnp.float32)
                * score_scale
            )
            value_grad = jnp.einsum(
                "hqk,qhd->khd", probs_low, grad_heads, preferred_element_type=jnp.float32
            )
            return (
                grad_query,
                jnp.concatenate(
                    [key_grad.reshape(block_len, -1), value_grad.reshape(block_len, -1)], axis=1
                ),
            )

        def skip_block(grad_query):
            return (grad_query, jnp.zeros((block_len, pair_width), jnp.float32))

        return lax.cond(meets(query_ids, key_ids), full_visit, skip_block, carried)

    grad_query, stacked = lax.scan(
        full_scan_step, jnp.zeros(heads_q.shape, jnp.float32), (key_blocks, value_blocks, id_blocks)
    )
    return (grad_query, stacked.reshape(-1, stacked.shape[-1]))


def body(
    hidden,
    segment_ids,
    w_in,
    w_depth,
    w_point,
    w_kernel,
    w_out,
    norm1_gain,
    norm1_bias,
    norm2_gain,
    norm2_bias,
    w_up,
    w_down,
    out_grad,
):
    (
        full_in,
        full_depth,
        full_point,
        full_kernel,
        full_out,
        gain_one,
        bias_one,
        gain_two,
        bias_two,
        full_up,
        full_down,
    ) = (
        lax.all_gather(w_in, "dp", axis=0, tiled=True),
        lax.all_gather(w_depth, "dp", axis=0, tiled=True),
        lax.all_gather(w_point, "dp", axis=0, tiled=True),
        lax.all_gather(w_kernel, "dp", axis=0, tiled=True),
        lax.all_gather(w_out, "dp", axis=0, tiled=True),
        lax.all_gather(norm1_gain, "dp", axis=0, tiled=True),
        lax.all_gather(norm1_bias, "dp", axis=0, tiled=True),
        lax.all_gather(norm2_gain, "dp", axis=0, tiled=True),
        lax.all_gather(norm2_bias, "dp", axis=0, tiled=True),
        lax.all_gather(w_up, "dp", axis=0, tiled=True),
        lax.all_gather(w_down, "dp", axis=0, tiled=True),
    )
    full_up, full_down = (
        lax.all_gather(full_up, "tensor", axis=2, tiled=True),
        lax.all_gather(full_down, "tensor", axis=2, tiled=True),
    )
    piece_rows = hidden.shape[2]
    seq_len = segment_ids.shape[2]
    attn_width = HEADS * HEAD_DIM
    radius = KERNEL // 2
    group_width = D // GROUPS
    block_rows = math.gcd(seq_len, 1024)
    block_count = seq_len // block_rows
    score_scale = HEAD_DIM ** (-0.5)
    row_offset = lax.axis_index("ctx") * piece_rows
    depth_table = full_depth.astype(jnp.float32)
    kernel_table = full_kernel.astype(jnp.float32)
    gain_one_f = gain_one.astype(jnp.float32)
    bias_one_f = bias_one.astype(jnp.float32)
    gain_two_f = gain_two.astype(jnp.float32)
    bias_two_f = bias_two.astype(jnp.float32)
    grad_totals = [
        jnp.zeros(weight_arr.shape, jnp.float32)
        for weight_arr in (
            full_in,
            full_depth,
            full_point,
            full_kernel,
            full_out,
            gain_one,
            bias_one,
            gain_two,
            bias_two,
            full_up,
            full_down,
        )
    ]
    outputs_list = []
    input_grads = []
    for micro_index in range(MICRO):
        tokens = hidden[micro_index, 0]
        cotangent = out_grad[micro_index, 0].astype(jnp.float32)
        seq_ids = segment_ids[micro_index, 0]
        own_ids = lax.dynamic_slice_in_dim(seq_ids, row_offset, piece_rows)
        window_ids = lax.dynamic_slice_in_dim(
            jnp.pad(seq_ids, radius, constant_values=-1), row_offset, piece_rows + 2 * radius
        )
        tap_mask = jnp.stack(
            [window_ids[j : j + piece_rows] == own_ids for j in range(KERNEL)], axis=1
        ).astype(jnp.float32)
        projected = jnp.dot(tokens, full_in, preferred_element_type=jnp.float32).astype(
            jnp.bfloat16
        )
        queries = projected[:, :attn_width]
        key_rows = projected[:, attn_width : 2 * attn_width]
        value_rows = projected[:, 2 * attn_width : 3 * attn_width]
        conv_rows = projected[:, 3 * attn_width :]
        extended = padded(jnp.concatenate([tokens, conv_rows], axis=1), (("ctx", 0),), radius)
        ext_tokens = extended[:, :D].astype(jnp.float32)
        ext_conv = (
            extended[:, D:].astype(jnp.float32).reshape(piece_rows + 2 * radius, HEADS, HEAD_DIM)
        )
        pre_key = sum(
            (
                ext_tokens[j : j + piece_rows] * depth_table[:, j] * tap_mask[:, j : j + 1]
                for j in range(KERNEL)
            )
        )
        pre_key_low = pre_key.astype(jnp.bfloat16)
        conv_key = jnp.dot(pre_key_low, full_point, preferred_element_type=jnp.float32)
        query_f = queries.astype(jnp.float32)
        mixed_low = (conv_key * query_f).astype(jnp.bfloat16)
        logits = jnp.dot(mixed_low, full_kernel, preferred_element_type=jnp.float32).reshape(
            piece_rows, HEADS, KERNEL
        )
        kernels = softmax_last(logits)
        conv_out = sum(
            (
                kernels[:, :, j : j + 1] * tap_mask[:, j, None, None] * ext_conv[j : j + piece_rows]
                for j in range(KERNEL)
            )
        )
        whole_keys, whole_values = (
            lax.all_gather(key_rows, "ctx", axis=0, tiled=True),
            lax.all_gather(value_rows, "ctx", axis=0, tiled=True),
        )
        heads_q = queries.reshape(piece_rows, HEADS, HEAD_DIM)
        key_blocks = whole_keys.reshape(block_count, block_rows, HEADS, HEAD_DIM)
        value_blocks = whole_values.reshape(block_count, block_rows, HEADS, HEAD_DIM)
        id_blocks = seq_ids.reshape(block_count, block_rows)
        log_total = log_totals(heads_q, key_blocks, own_ids, id_blocks, score_scale)
        attn_out = attend(
            heads_q, key_blocks, value_blocks, own_ids, id_blocks, log_total, score_scale
        )
        context = jnp.concatenate(
            [attn_out.reshape(piece_rows, attn_width), conv_out.reshape(piece_rows, attn_width)],
            axis=1,
        ).astype(jnp.bfloat16)
        mixed_out = jnp.dot(context, full_out, preferred_element_type=jnp.float32)
        normed_one, normal_one, inverse_one = norm_forward(
            tokens.astype(jnp.float32) + mixed_out, gain_one_f, bias_one_f
        )
        ffn_in = normed_one.astype(jnp.bfloat16)
        rows_grouped = ffn_in.reshape(-1, GROUPS, group_width)
        up_proj = jnp.einsum(
            "rgi,igj->rgj", rows_grouped, full_up, preferred_element_type=jnp.float32
        )
        activated = gelu_exact(up_proj).astype(jnp.bfloat16)
        down_proj = jnp.einsum(
            "rgj,igj->rgi", activated, full_down, preferred_element_type=jnp.float32
        ).reshape(piece_rows, D)
        final_rows, normal_two, inverse_two = norm_forward(
            normed_one + down_proj, gain_two_f, bias_two_f
        )
        outputs_list.append(final_rows.astype(jnp.bfloat16))
        grad_z, gain_two_grad, bias_two_grad = norm_backward(
            cotangent, normal_two, inverse_two, gain_two_f
        )
        grad_down = grad_z.astype(jnp.bfloat16)
        grad_grouped = grad_down.reshape(-1, GROUPS, group_width)
        grad_act = jnp.einsum(
            "rgi,igj->rgj", grad_grouped, full_down, preferred_element_type=jnp.float32
        )
        gelu_pull = jax.vjp(gelu_exact, up_proj)[1]
        grad_up = gelu_pull(grad_act)[0].astype(jnp.bfloat16)
        down_weight_grad = jnp.einsum(
            "rgi,rgj->igj", grad_grouped, activated, preferred_element_type=jnp.float32
        )
        up_weight_grad = jnp.einsum(
            "rgi,rgj->igj", rows_grouped, grad_up, preferred_element_type=jnp.float32
        )
        ffn_back = jnp.einsum(
            "rgj,igj->rgi", grad_up, full_up, preferred_element_type=jnp.float32
        ).reshape(piece_rows, D)
        grad_normed = grad_z + ffn_back
        grad_pre, gain_one_grad, bias_one_grad = norm_backward(
            grad_normed, normal_one, inverse_one, gain_one_f
        )
        grad_mix_low = grad_pre.astype(jnp.bfloat16)
        out_weight_grad = rows_product(context, grad_mix_low)
        grad_context = times_transposed(grad_mix_low, full_out).astype(jnp.bfloat16)
        grad_attn = grad_context[:, :attn_width]
        grad_heads = grad_attn.reshape(piece_rows, HEADS, HEAD_DIM)
        delta = delta_pass(
            heads_q,
            grad_heads,
            key_blocks,
            value_blocks,
            own_ids,
            id_blocks,
            log_total,
            score_scale,
        )
        grad_q_attn, all_kv_grads = full_grad_pass(
            heads_q,
            grad_heads,
            key_blocks,
            value_blocks,
            own_ids,
            id_blocks,
            log_total,
            delta,
            score_scale,
        )
        own_kv_grads = lax.psum_scatter(
            all_kv_grads.astype(jnp.bfloat16), "ctx", scatter_dimension=0, tiled=True
        ).astype(jnp.float32)
        grad_conv = (
            grad_context[:, attn_width:].astype(jnp.float32).reshape(piece_rows, HEADS, HEAD_DIM)
        )
        grad_taps = jnp.stack(
            [
                jnp.sum(grad_conv * ext_conv[j : j + piece_rows], axis=-1) * tap_mask[:, j : j + 1]
                for j in range(KERNEL)
            ],
            axis=-1,
        )
        grad_logits = (
            kernels * (grad_taps - jnp.sum(kernels * grad_taps, axis=-1, keepdims=True))
        ).reshape(piece_rows, HEADS * KERNEL)
        grad_conv_ext = sum(
            (
                jnp.pad(
                    kernels[:, :, j : j + 1] * tap_mask[:, j, None, None] * grad_conv,
                    ((j, 2 * radius - j), (0, 0), (0, 0)),
                )
                for j in range(KERNEL)
            )
        )
        grad_mixed_low = lax.optimization_barrier(
            jnp.dot(grad_logits, kernel_table.T, precision=HIGHEST).astype(jnp.bfloat16)
        )
        grad_mixed = grad_mixed_low.astype(jnp.float32)
        kernel_weight_grad = jnp.dot(
            mixed_low.astype(jnp.float32).T, grad_logits, precision=HIGHEST
        )
        grad_conv_key = (grad_mixed * query_f).astype(jnp.bfloat16)
        grad_q_total = grad_q_attn.reshape(piece_rows, attn_width) + grad_mixed * conv_key
        point_weight_grad = rows_product(pre_key_low, grad_conv_key)
        grad_pre_key = times_transposed(grad_conv_key, full_point)
        grad_tokens_ext = sum(
            (
                jnp.pad(
                    depth_table[:, j] * tap_mask[:, j : j + 1] * grad_pre_key,
                    ((j, 2 * radius - j), (0, 0)),
                )
                for j in range(KERNEL)
            )
        )
        depth_weight_grad = jnp.stack(
            [
                jnp.sum(
                    ext_tokens[j : j + piece_rows] * tap_mask[:, j : j + 1] * grad_pre_key, axis=0
                )
                for j in range(KERNEL)
            ],
            axis=1,
        )
        ext_grads = jnp.concatenate(
            [grad_tokens_ext, grad_conv_ext.reshape(piece_rows + 2 * radius, attn_width)], axis=1
        )
        rim_rows = jnp.concatenate([ext_grads[:radius], ext_grads[piece_rows + radius :]], axis=0)
        arrived = padded(rim_rows.astype(jnp.bfloat16), (("ctx", 0),), radius).astype(
            rim_rows.dtype
        )
        own_grads = ext_grads[radius : piece_rows + radius]
        own_grads = (
            own_grads.at[:radius]
            .add(arrived[:radius])
            .at[piece_rows - radius :]
            .add(arrived[3 * radius :])
        )
        grad_projected = jnp.concatenate(
            [grad_q_total, own_kv_grads, own_grads[:, D:]], axis=1
        ).astype(jnp.bfloat16)
        in_weight_grad = rows_product(tokens, grad_projected)
        input_grad = grad_pre + own_grads[:, :D] + times_transposed(grad_projected, full_in)
        input_grads.append(input_grad.astype(jnp.bfloat16))
        updates = (
            in_weight_grad,
            depth_weight_grad,
            point_weight_grad,
            kernel_weight_grad,
            out_weight_grad,
            gain_one_grad,
            bias_one_grad,
            gain_two_grad,
            bias_two_grad,
            up_weight_grad,
            down_weight_grad,
        )
        grad_totals = [running + change for running, change in zip(grad_totals, updates)]
    split_grads = (
        lax.psum_scatter(
            grad_totals[0].astype(jnp.bfloat16), "dp", scatter_dimension=0, tiled=True
        ).astype(jnp.float32),
        lax.psum_scatter(
            grad_totals[1].astype(jnp.bfloat16), "dp", scatter_dimension=0, tiled=True
        ).astype(jnp.float32),
        lax.psum_scatter(
            grad_totals[2].astype(jnp.bfloat16), "dp", scatter_dimension=0, tiled=True
        ).astype(jnp.float32),
        lax.psum_scatter(
            grad_totals[3].astype(jnp.bfloat16), "dp", scatter_dimension=0, tiled=True
        ).astype(jnp.float32),
        lax.psum_scatter(
            grad_totals[4].astype(jnp.bfloat16), "dp", scatter_dimension=0, tiled=True
        ).astype(jnp.float32),
        lax.psum_scatter(
            grad_totals[5].astype(jnp.bfloat16), "dp", scatter_dimension=0, tiled=True
        ).astype(jnp.float32),
        lax.psum_scatter(
            grad_totals[6].astype(jnp.bfloat16), "dp", scatter_dimension=0, tiled=True
        ).astype(jnp.float32),
        lax.psum_scatter(
            grad_totals[7].astype(jnp.bfloat16), "dp", scatter_dimension=0, tiled=True
        ).astype(jnp.float32),
        lax.psum_scatter(
            grad_totals[8].astype(jnp.bfloat16), "dp", scatter_dimension=0, tiled=True
        ).astype(jnp.float32),
        lax.psum_scatter(
            grad_totals[9].astype(jnp.bfloat16), "dp", scatter_dimension=0, tiled=True
        ).astype(jnp.float32),
        lax.psum_scatter(
            grad_totals[10].astype(jnp.bfloat16), "dp", scatter_dimension=0, tiled=True
        ).astype(jnp.float32),
    )
    column_count = w_up.shape[2]
    column_start = lax.axis_index("tensor") * column_count
    up_split = split_grads[9]
    down_split = split_grads[10]
    summed = lax.psum(
        (
            split_grads[0],
            split_grads[1],
            split_grads[2],
            split_grads[3],
            split_grads[4],
            split_grads[5],
            split_grads[6],
            split_grads[7],
            split_grads[8],
            up_split,
            down_split,
        ),
        ("ctx", "tensor"),
    )
    up_grad_out = lax.dynamic_slice_in_dim(summed[9], column_start, column_count, 2)
    down_grad_out = lax.dynamic_slice_in_dim(summed[10], column_start, column_count, 2)
    layer_output = jnp.stack(outputs_list)[:, None]
    layer_input_grad = jnp.stack(input_grads)[:, None]
    return (
        layer_output,
        layer_input_grad,
        summed[0],
        summed[1],
        summed[2],
        summed[3],
        summed[4],
        summed[5],
        summed[6],
        summed[7],
        summed[8],
        up_grad_out,
        down_grad_out,
    )


def solution(mesh):
    return jax.shard_map(
        body,
        mesh=mesh,
        in_specs=(
            P(None, ("dp", "tensor"), "ctx", None),
            P(None, ("dp", "tensor"), None),
            P("dp", None),
            P("dp", None),
            P("dp", None),
            P("dp", None),
            P("dp", None),
            P("dp"),
            P("dp"),
            P("dp"),
            P("dp"),
            P("dp", None, "tensor"),
            P("dp", None, "tensor"),
            P(None, ("dp", "tensor"), "ctx", None),
        ),
        out_specs=(
            P(None, ("dp", "tensor"), "ctx", None),
            P(None, ("dp", "tensor"), "ctx", None),
            P("dp", None),
            P("dp", None),
            P("dp", None),
            P("dp", None),
            P("dp", None),
            P("dp"),
            P("dp"),
            P("dp"),
            P("dp"),
            P("dp", None, "tensor"),
            P("dp", None, "tensor"),
        ),
        check_vma=False,
    )
```

profile of v0, /device:TPU:0, one launch (start us, length us, event | category | flops | bytes accessed | tf_op | source)
XLA Modules:
  0.0 930.3 jit_solution(5575996575439342488)
XLA Ops:
  9.8 10.7 %all_gather.60 = bf16[384,2,384]{2,0,1:T(8,128)(2,1)} all-gather(bf16[192,2,384]{2,0,1:T(8,128)(2,1)S(1)} %copy.196), channel_id=1, replica_groups=mesh['dp'=2,'ctx'=4,'tensor'=4] {'dp'}, dimensions={0}, use_global_device_ids=true | all-gather | bytes 884736 | tf_op jit(solution)/shard_map/all_gather | solution.py:271
  20.7 16.5 %all_gather.62 = bf16[384,2,384]{2,0,1:T(8,128)(2,1)} all-gather(bf16[192,2,384]{2,0,1:T(8,128)(2,1)S(1)} %copy.198), channel_id=1, replica_groups=mesh['dp'=2,'ctx'=4,'tensor'=4] {'dp'}, dimensions={0}, use_global_device_ids=true | all-gather | bytes 884736 | tf_op jit(solution)/shard_map/all_gather | solution.py:272
  37.9 5.3 all-gather
  44.4 4.8 all_gather.54
  49.4 12.2 %all_gather.55 = bf16[768,384]{1,0:T(8,128)(2,1)S(1)} all-gather(bf16[384,384]{1,0:T(8,128)(2,1)S(1)} %copy-done.81), channel_id=1, replica_groups=mesh['dp'=2,'ctx'=4,'tensor'=4] {'dp'}, dimensions={0}, use_global_device_ids=true | all-gather | bytes 884736 | tf_op jit(solution)/shard_map/all_gather | solution.py:264
  96.5 9.7 %all_gather.66 = bf16[1024,384]{1,0:T(8,128)(2,1)} all-gather(bf16[256,384]{1,0:T(8,128)(2,1)S(1)} %get-tuple-element.772), channel_id=1, replica_groups=mesh['dp'=2,'ctx'=4,'tensor'=4] {'ctx'}, dimensions={0}, use_global_device_ids=true | all-gather | bytes 983040 | tf_op jit(solution)/shard_map/all_gather | solution.py:355
  107.7 9.1 all_gather.67
  119.1 5.2 conditional.10
  125.7 5.4 conditional.11
  142.6 9.7 %all_gather.52 = bf16[1024,384]{1,0:T(8,128)(2,1)} all-gather(bf16[256,384]{1,0:T(8,128)(2,1)S(1)} %get-tuple-element.766), channel_id=1, replica_groups=mesh['dp'=2,'ctx'=4,'tensor'=4] {'ctx'}, dimensions={0}, use_global_device_ids=true | all-gather | bytes 983040 | tf_op jit(solution)/shard_map/all_gather | solution.py:355
  153.8 9.6 %all_gather.53 = bf16[1024,384]{1,0:T(8,128)(2,1)} all-gather(bf16[256,384]{1,0:T(8,128)(2,1)} %get-tuple-element.764), channel_id=1, replica_groups=mesh['dp'=2,'ctx'=4,'tensor'=4] {'ctx'}, dimensions={0}, use_global_device_ids=true | all-gather | bytes 983040 | tf_op jit(solution)/shard_map/all_gather | solution.py:356
  163.3 6.6 conditional.8
  173.5 5.6 conditional.9
  174.5 4.7 fusion.6
  309.4 6.9 copy.253
  316.2 5.4 fusion.36
  321.6 6.8 copy.258
  346.6 10.2 %conditional.15 = (f32[256,6,64]{0,2,1:T(8,128)S(1)}, bf16[1024,768]{0,1:T(8,128)(2,1)}) conditional(s32[]{:T(128)} %bitcast.43, f32[256,6,64]{0,2,1:T(8,128)S(1)} %copy-done.6, (s32[256]{0:T(256)}, s32[1024]{0:T(1024)S(1)}, bf16[256,6,64]{0,2,1:T(8,128)(2,1)S(1)}, bf16[1024,6,64]{0,2,1:T(8,128)(2,1)S(1)}, f32[6,256]{1,0:T(8,128)}, ...), branch_computations={%region_61.62_spmd, %region_62.63_spmd} | conditional | flops 1026752512 | bytes 41708644 | solution.py:225
  364.3 4.7 conditional.12
  369.0 10.2 %conditional.13 = (f32[256,6,64]{0,2,1:T(8,128)S(1)}, bf16[1024,768]{0,1:T(8,128)(2,1)}) conditional(s32[]{:T(128)} %bitcast.13, f32[256,6,64]{0,2,1:T(8,128)S(1)} %copy-done.6, (s32[256]{0:T(256)}, s32[1024]{0:T(1024)S(1)}, bf16[256,6,64]{0,2,1:T(8,128)(2,1)S(1)}, bf16[1024,6,64]{0,2,1:T(8,128)(2,1)S(1)}, f32[6,256]{1,0:T(8,128)}, ...), branch_computations={%region_41.42_spmd, %region_42.43_spmd} | conditional | flops 1026752512 | bytes 41708644 | solution.py:225
  386.4 5.1 multiply_multiply_fusion.17
  393.2 5.2 multiply_multiply_fusion.8
  442.7 5.4 all-reduce.54.cloned.1.call-done
  464.1 14.4 %reduce-scatter.14.cloned.1.call-done = bf16[256,768]{0,1:T(8,128)(2,1)} async-done(((bf16[1024,768]{0,1:T(8,128)(2,1)}), bf16[256,768]{0,1:T(8,128)(2,1)}) %reduce-scatter.14.cloned.1.call-update) | async-done | bytes 393232 | tf_op jit(solution)/shard_map/reduce_scatter | solution.py:436
  482.6 27.1 %reduce-scatter.16.cloned.1.call-done = bf16[256,768]{0,1:T(8,128)(2,1)} async-done(((bf16[1024,768]{0,1:T(8,128)(2,1)}), bf16[256,768]{0,1:T(8,128)(2,1)}) %reduce-scatter.16.cloned.1.call-update) | async-done | bytes 393232 | tf_op jit(solution)/shard_map/reduce_scatter | solution.py:436
  516.8 5.1 all-reduce.46
  524.2 11.3 %reduce-scatter.26.cloned.1.call-done = bf16[192,54]{1,0:T(8,128)(2,1)} async-done(((bf16[384,54]{1,0:T(8,128)(2,1)}), bf16[192,54]{1,0:T(8,128)(2,1)}) %reduce-scatter.26.cloned.1.call-update) | async-done | bytes 20752
  536.4 17.1 %reduce-scatter.18.cloned.1.call-done = bf16[384,384]{1,0:T(8,128)(2,1)} async-done(((bf16[768,384]{1,0:T(8,128)(2,1)}), bf16[384,384]{1,0:T(8,128)(2,1)}) %reduce-scatter.18.cloned.1.call-update) | async-done | bytes 294928 | tf_op jit(solution)/shard_map/reduce_scatter | solution.py:531
  553.6 24.1 %reduce-scatter.20.cloned.1.call-done = bf16[384,768]{1,0:T(8,128)(2,1)} async-done(((bf16[768,768]{1,0:T(8,128)(2,1)}), bf16[384,768]{1,0:T(8,128)(2,1)}) %reduce-scatter.20.cloned.1.call-update) | async-done | bytes 589840 | tf_op jit(solution)/shard_map/reduce_scatter | solution.py:537
  583.6 114.5 %all-reduce.52.cloned.1.call-done = (f32[192,2,1536]{2,1,0:T(2,128)}, f32[192,2,1536]{2,1,0:T(2,128)}) async-done(((f32[192,2,1536]{2,1,0:T(2,128)}, f32[192,2,1536]{2,1,0:T(2,128)}), (f32[192,2,1536]{2,1,0:T(2,128)}, f32[192,2,1536]{2,1,0:T(2,128)})) %all-reduce.52.cloned.1.call-update) | async-done | bytes 4718608 | tf_op jit(solution)/shard_map/psum | solution.py:563
  702.4 33.2 %reduce-scatter.22.cloned.1.call-done = bf16[384,1536]{1,0:T(8,128)(2,1)} async-done(((bf16[768,1536]{1,0:T(8,128)(2,1)}), bf16[384,1536]{1,0:T(8,128)(2,1)}) %reduce-scatter.22.cloned.1.call-update) | async-done | bytes 1179664
  737.3 182.9 %all-reduce.55 = (f32[384,1536]{0,1:T(8,128)}, f32[384,9]{0,1:T(8,128)}, f32[384,384]{1,0:T(8,128)}, f32[192,54]{0,1:T(8,128)}, f32[384,768]{1,0:T(8,128)}, /*in...) all-reduce(bf16[384,1536]{0,1:T(8,128)(2,1)S(1)} %copy.267, ...), channel_id=1, replica_groups=mesh['dp'=2,'ctx'=4,'tensor'=4] {'ctx','tensor'}, use_global_device_ids=true, to_apply=%region_65.66 | all-reduce | flops 1047552 | bytes 6288384 | tf_op jit(solution)/shard_map/psum | solution.py:563
  (910 shorter events, 351.9 us)
Async XLA Ops:
  7.2 82.3 %all-gather.10.cloned.1.call-start = ((), (), s32[]{:S(2)}) async-start(), calls=%async_computation.7 | async-start | bytes 3538944 | tf_op jit(solution)/shard_map/all_gather | solution.py:262
  7.9 259.1 %all-gather.12.cloned.1.call-start = ((), (), s32[]{:S(2)}) async-start(), calls=%async_computation.8 | async-start | bytes 1769472 | tf_op jit(solution)/shard_map/all_gather | solution.py:266
  8.7 264.6 %all-gather.14.cloned.1.call-start = ((), (), s32[]{:S(2)}) async-start(), calls=%async_computation.9 | async-start | bytes 2949120 | tf_op jit(solution)/shard_map/all_gather | solution.py:275
  20.5 258.8 %all-gather.16.cloned.1.call-start = ((), (), s32[]{:S(2)}) async-start(), calls=%async_computation.10 | async-start | bytes 2949120 | tf_op jit(solution)/shard_map/all_gather | solution.py:276
  37.2 410.9 %all-reduce.54.cloned.1.call-start = ((), (), s32[]{:S(2)}) async-start(), calls=%async_computation.19 | async-start | bytes 9437184
  37.3 136.3 %copy-start.92 = (s32[1,1,1024]{2,1,0:T(1,128)}, s32[1,1,1024]{2,1,0:T(1,128)S(1)}, u32[]{:S(2)}) copy-start(s32[1,1,1024]{2,1,0:T(1,128)S(1)} %get-tuple-element.865) | copy-start | bytes 12292
  37.9 143.1 %copy-start.27 = (bf16[256,768]{1,0:T(8,128)(2,1)}, bf16[256,768]{1,0:T(8,128)(2,1)S(1)}, u32[]{:S(2)}) copy-start(bf16[256,768]{1,0:T(8,128)(2,1)S(1)} %get-tuple-element.769) | copy-start | bytes 1179652
  44.4 137.9 %copy-start.149 = (f32[256,1]{0,1:T(1,128)}, f32[256,1]{0,1:T(1,128)S(1)}, u32[]{:S(2)}) copy-start(f32[256,1]{0,1:T(1,128)S(1)} %get-tuple-element.851) | copy-start | bytes 3076
  44.4 137.9 %copy-start.153 = (f32[256,1]{0,1:T(1,128)}, f32[256,1]{0,1:T(1,128)S(1)}, u32[]{:S(2)}) copy-start(f32[256,1]{0,1:T(1,128)S(1)} %get-tuple-element.852) | copy-start | bytes 3076
  44.4 137.9 %copy-start.157 = (f32[256,1]{0,1:T(1,128)}, f32[256,1]{0,1:T(1,128)S(1)}, u32[]{:S(2)}) copy-start(f32[256,1]{0,1:T(1,128)S(1)} %get-tuple-element.853) | copy-start | bytes 3076
  49.3 133.0 %copy-start.100 = (f32[768]{0:T(1024)}, f32[768]{0:T(1024)S(1)}, u32[]{:S(2)}) copy-start(f32[768]{0:T(1024)S(1)} %get-tuple-element.706) | copy-start | bytes 9220
  49.3 133.0 %copy-start.103 = (f32[768]{0:T(1024)}, f32[768]{0:T(1024)S(1)}, u32[]{:S(2)}) copy-start(f32[768]{0:T(1024)S(1)} %get-tuple-element.707) | copy-start | bytes 9220
  49.3 133.0 %copy-start.106 = (f32[768]{0:T(1024)}, f32[768]{0:T(1024)S(1)}, u32[]{:S(2)}) copy-start(f32[768]{0:T(1024)S(1)} %get-tuple-element.708) | copy-start | bytes 9220
  49.3 133.0 %copy-start.109 = (f32[768]{0:T(1024)}, f32[768]{0:T(1024)S(1)}, u32[]{:S(2)}) copy-start(f32[768]{0:T(1024)S(1)} %get-tuple-element.709) | copy-start | bytes 9220
  49.3 133.0 %copy-start.112 = (f32[768]{0:T(1024)}, f32[768]{0:T(1024)S(1)}, u32[]{:S(2)}) copy-start(f32[768]{0:T(1024)S(1)} %get-tuple-element.710) | copy-start | bytes 9220
  61.6 145.2 %copy-start.7 = (bf16[768,384]{1,0:T(8,128)(2,1)}, bf16[768,384]{1,0:T(8,128)(2,1)S(1)}, u32[]{:S(2)}) copy-start(bf16[768,384]{1,0:T(8,128)(2,1)S(1)} %all_gather.55) | copy-start | bytes 1769476
  92.0 89.0 %collective-permute-start.3 = (bf16[4,1152]{1,0:T(4,128)(2,1)S(1)}, bf16[4,1152]{1,0:T(4,128)(2,1)S(1)}, u32[]{:S(2)}, u32[]{:S(2)}) collective-permute-start(bf16[4,1152]{1,0:T(4,128)(2,1)S(1)} %get-tuple-element.781), channel_id=1, source_target_pairs={{4,0},{8,4},{12,8},{5,1},{9,5},{13,9},{6,2},{10,6},{14,10},{7,3},{... | collective-permute-start | bytes 27656 | tf_op jit(solution)/shard_map/ppermute | solution.py:29
  93.3 87.7 %collective-permute-start.2 = (bf16[4,1152]{1,0:T(4,128)(2,1)S(1)}, bf16[4,1152]{1,0:T(4,128)(2,1)S(1)}, u32[]{:S(2)}, u32[]{:S(2)}) collective-permute-start(bf16[4,1152]{1,0:T(4,128)(2,1)S(1)} %get-tuple-element.780), channel_id=1, source_target_pairs={{0,4},{4,8},{8,12},{1,5},{5,9},{9,13},{2,6},{6,10},{10,14},{3,7},{... | collective-permute-start | bytes 27656 | tf_op jit(solution)/shard_map/ppermute | solution.py:26
  136.9 67.4 %collective-permute-start.1 = (bf16[4,1152]{1,0:T(4,128)(2,1)}, bf16[4,1152]{1,0:T(4,128)(2,1)}, u32[]{:S(2)}, u32[]{:S(2)}) collective-permute-start(bf16[4,1152]{1,0:T(4,128)(2,1)} %get-tuple-element.779), channel_id=1, source_target_pairs={{4,0},{8,4},{12,8},{5,1},{9,5},{13,9},{6,2},{10,6},{14,10},{7,3},{... | collective-permute-start | bytes 27656 | tf_op jit(solution)/shard_map/ppermute | solution.py:29
  138.1 66.1 %collective-permute-start = (bf16[4,1152]{1,0:T(4,128)(2,1)}, bf16[4,1152]{1,0:T(4,128)(2,1)}, u32[]{:S(2)}, u32[]{:S(2)}) collective-permute-start(bf16[4,1152]{1,0:T(4,128)(2,1)} %get-tuple-element.778), channel_id=1, source_target_pairs={{0,4},{4,8},{8,12},{1,5},{5,9},{9,13},{2,6},{6,10},{10,14},{3,7},{... | collective-permute-start | bytes 27656 | tf_op jit(solution)/shard_map/ppermute | solution.py:26
  328.5 150.0 %reduce-scatter.14.cloned.1.call-start = ((), (), s32[]{:S(2)}) async-start(), calls=%async_computation.11 | async-start | bytes 1966080 | tf_op jit(solution)/shard_map/reduce_scatter | solution.py:436
  379.2 130.4 %reduce-scatter.16.cloned.1.call-start = ((), (), s32[]{:S(2)}) async-start(), calls=%async_computation.12 | async-start | bytes 1966080 | tf_op jit(solution)/shard_map/reduce_scatter | solution.py:436
  385.5 137.8 %reduce-scatter.24.cloned.1.call-start = ((), (), s32[]{:S(2)}) async-start(), calls=%async_computation.16 | async-start | bytes 294912
  405.7 129.8 %reduce-scatter.26.cloned.1.call-start = ((), (), s32[]{:S(2)}) async-start(), calls=%async_computation.17 | async-start | bytes 147456
  407.7 145.9 %reduce-scatter.18.cloned.1.call-start = ((), (), s32[]{:S(2)}) async-start(), calls=%async_computation.13 | async-start | bytes 884736 | tf_op jit(solution)/shard_map/reduce_scatter | solution.py:531
  411.2 166.5 %reduce-scatter.20.cloned.1.call-start = ((), (), s32[]{:S(2)}) async-start(), calls=%async_computation.14 | async-start | bytes 1769472 | tf_op jit(solution)/shard_map/reduce_scatter | solution.py:537
  414.8 42.1 %collective-permute-start.7 = (bf16[4,1152]{1,0:T(4,128)(2,1)S(1)}, bf16[4,1152]{1,0:T(4,128)(2,1)S(1)}, u32[]{:S(2)}, u32[]{:S(2)}) collective-permute-start(bf16[4,1152]{1,0:T(4,128)(2,1)S(1)} %get-tuple-element.777), channel_id=1, source_target_pairs={{4,0},{8,4},{12,8},{5,1},{9,5},{13,9},{6,2},{10,6},{14,10},{7,3},{... | collective-permute-start | bytes 27656 | tf_op jit(solution)/shard_map/ppermute | solution.py:29
  416.2 40.7 %collective-permute-start.6 = (bf16[4,1152]{1,0:T(4,128)(2,1)S(1)}, bf16[4,1152]{1,0:T(4,128)(2,1)S(1)}, u32[]{:S(2)}, u32[]{:S(2)}) collective-permute-start(bf16[4,1152]{1,0:T(4,128)(2,1)S(1)} %get-tuple-element.776), channel_id=1, source_target_pairs={{0,4},{4,8},{8,12},{1,5},{5,9},{9,13},{2,6},{6,10},{10,14},{3,7},{... | collective-permute-start | bytes 27656 | tf_op jit(solution)/shard_map/ppermute | solution.py:26
  424.5 273.7 %all-reduce.52.cloned.1.call-start = ((), (), s32[]{:S(2)}) async-start(), calls=%async_computation.18 | async-start | bytes 9437184 | tf_op jit(solution)/shard_map/psum | solution.py:563
  433.9 26.9 %collective-permute-start.5 = (bf16[4,1152]{1,0:T(4,128)(2,1)S(1)}, bf16[4,1152]{1,0:T(4,128)(2,1)S(1)}, u32[]{:S(2)}, u32[]{:S(2)}) collective-permute-start(bf16[4,1152]{1,0:T(4,128)(2,1)S(1)} %get-tuple-element.775), channel_id=1, source_target_pairs={{4,0},{8,4},{12,8},{5,1},{9,5},{13,9},{6,2},{10,6},{14,10},{7,3},{... | collective-permute-start | bytes 27656 | tf_op jit(solution)/shard_map/ppermute | solution.py:29
  435.2 25.6 %collective-permute-start.4 = (bf16[4,1152]{1,0:T(4,128)(2,1)S(1)}, bf16[4,1152]{1,0:T(4,128)(2,1)S(1)}, u32[]{:S(2)}, u32[]{:S(2)}) collective-permute-start(bf16[4,1152]{1,0:T(4,128)(2,1)S(1)} %get-tuple-element.774), channel_id=1, source_target_pairs={{0,4},{4,8},{8,12},{1,5},{5,9},{9,13},{2,6},{6,10},{10,14},{3,7},{... | collective-permute-start | bytes 27656 | tf_op jit(solution)/shard_map/ppermute | solution.py:26
  453.9 281.6 %reduce-scatter.22.cloned.1.call-start = ((), (), s32[]{:S(2)}) async-start(), calls=%async_computation.15 | async-start | bytes 3538944
  (227 other events, 2452.5 us)
Sparse Core Ops, SparseCore 0:
  9.5 50.7 all-gather.9
  61.9 22.5 all-gather.11
  86.1 50.2 all-gather.13
  137.8 48.8 all-gather.15
  328.6 119.4 all-reduce.53
  450.5 28.0 reduce-scatter.13
  481.6 27.9 reduce-scatter.15
  511.9 11.2 reduce-scatter.23
  525.4 10.0 reduce-scatter.25
  538.2 15.3 reduce-scatter.17
  555.8 21.8 reduce-scatter.19
  581.2 116.8 all-reduce.51
  701.0 34.5 reduce-scatter.21
where the time goes:
time: 942 us; the launch traced here: 930 us
  blocking collectives  293 us (31%)
  waiting for transfers between devices  249 us (26%)
  local copies, waits for them, and re-layouts  138 us (15%)
  matrix products  111 us (12%)
  other arithmetic  92.3 us (10%)
  between operations  24.9 us (3%)
  starting transfers between devices  20.5 us (2%)
    psum x1, blocking collectives, body(): lax.psum((split_grads[0], split_grads[1], split_grads[2], split_grads[3],...  183 us
    psum x1, waiting for transfers between devices, body(): lax.psum((split_grads[0], split_grads[1], split_grads[2], split_grads[3],...  115 us
    unnamed x17, waiting for transfers between devices  51.5 us
    reduce_scatter x2, waiting for transfers between devices, body(): lax.psum_scatter(all_kv_grads.astype(jnp.bfloat16), 'ctx', scatter_dimens...  41.5 us
    slice x20, local copies, waits for them, and re-layouts, body(): ext_conv[j:j + piece_rows]  36 us
    unnamed x485, local copies, waits for them, and re-layouts  28.1 us
    reduce_scatter x1, waiting for transfers between devices, body(): lax.psum_scatter(grad_totals[4].astype(jnp.bfloat16), 'dp', scatter_dimen...  24.1 us
    mul x36, local copies, waits for them, and re-layouts, body(): kernels[:, :, j:j + 1] * tap_mask[:, j, None, None]  20.6 us
  transfers between devices with their start and end apart: 21, of which 8 were waited for; matrix products, arithmetic and copies ran while one was open for 30% of the time, Pallas kernels for 0%

commit v1 on v0

--- a/solution.py
+++ b/solution.py
@@ -29,6 +29,101 @@
         high = lax.ppermute(lax.slice_in_dim(block, 0, width, axis=dim), axis, backward)
         block = jnp.concatenate([low, block, high], axis=dim)
     return block
+
+
+def swap(block, axis, bit):
+    count = lax.axis_size(axis)
+    return lax.ppermute(block, axis, [(i, i ^ bit) for i in range(count)])
+
+
+def bit_set(axis, bit):
+    return (lax.axis_index(axis) // bit) % 2 == 1
+
+
+def pick(pair, take_high):
+    return jnp.where(take_high, pair[1], pair[0])
+
+
+def halves(block, dim):
+    size = block.shape[dim] // 2
+    return (
+        lax.slice_in_dim(block, 0, size, axis=dim),
+        lax.slice_in_dim(block, size, 2 * size, axis=dim),
+    )
+
+
+def fold(block, axis, bit, dim):
+    high = bit_set(axis, bit)
+    low_half, high_half = halves(block, dim)
+    sent = jnp.where(high, low_half, high_half)
+    kept = jnp.where(high, high_half, low_half)
+    arrived = swap(sent, axis, bit)
+    return (kept.astype(jnp.float32) + arrived.astype(jnp.float32)).astype(block.dtype)
+
+
+def unfold(block, axis, bit, dim):
+    other = swap(block, axis, bit)
+    high = bit_set(axis, bit)
+    return jnp.concatenate(
+        [jnp.where(high, other, block), jnp.where(high, block, other)], axis=dim
+    )
+
+
+def bits_of(axis):
+    bits, bit = [], 1
+    while bit < lax.axis_size(axis):
+        bits.append(bit)
+        bit *= 2
+    return bits
+
+
+def gather_rows(block, axis):
+    depth = 0
+    shape = block.shape
+    for bit in reversed(bits_of(axis)):
+        other = swap(block, axis, bit)
+        high = bit_set(axis, bit)
+        block = jnp.stack([jnp.where(high, other, block), jnp.where(high, block, other)], axis=depth)
+        depth += 1
+    return block.reshape((-1,) + shape[1:])
+
+
+def scatter_rows(block, axis):
+    bits = bits_of(axis)
+    block = block.reshape((2,) * len(bits) + (-1,) + block.shape[1:])
+    for bit in bits:
+        dim = len([b for b in bits if b > bit])
+        block = fold(block, axis, bit, dim)
+        block = lax.squeeze(block, (dim,))
+    return block
+
+
+def line_gather(block, axis):
+    count = lax.axis_size(axis)
+    up = [(i, i + 1) for i in range(count - 1)]
+    down = [(i + 1, i) for i in range(count - 1)]
+    lower, upper = [], []
+    from_low, from_high = block, block
+    for _ in range(count - 1):
+        from_low = lax.ppermute(from_low, axis, up)
+        from_high = lax.ppermute(from_high, axis, down)
+        lower.insert(0, from_low)
+        upper.append(from_high)
+    line = jnp.stack(lower + [block] + upper)
+    return lax.dynamic_slice_in_dim(line, count - 1 - lax.axis_index(axis), count, axis=0)
+
+
+def pair_share(block, dim):
+    high = bit_set("ctx", 1)
+    part = pick(halves(block, dim), high)
+    arrived = swap(part, "dp", 1)
+    other = unfold(arrived, "ctx", 1, dim)
+    on_high = bit_set("dp", 1)
+    return jnp.concatenate([jnp.where(on_high, other, block), jnp.where(on_high, block, other)], axis=0)
+
+
+def fit(block, rows, columns):
+    return jnp.pad(block, ((0, rows - block.shape[0]), (0, columns - block.shape[1])))
 
 
 def gelu_exact(values):
@@ -246,35 +341,32 @@
     w_down,
     out_grad,
 ):
-    (
-        full_in,
-        full_depth,
-        full_point,
-        full_kernel,
-        full_out,
-        gain_one,
-        bias_one,
-        gain_two,
-        bias_two,
-        full_up,
-        full_down,
-    ) = (
-        lax.all_gather(w_in, "dp", axis=0, tiled=True),
-        lax.all_gather(w_depth, "dp", axis=0, tiled=True),
-        lax.all_gather(w_point, "dp", axis=0, tiled=True),
-        lax.all_gather(w_kernel, "dp", axis=0, tiled=True),
-        lax.all_gather(w_out, "dp", axis=0, tiled=True),
-        lax.all_gather(norm1_gain, "dp", axis=0, tiled=True),
-        lax.all_gather(norm1_bias, "dp", axis=0, tiled=True),
-        lax.all_gather(norm2_gain, "dp", axis=0, tiled=True),
-        lax.all_gather(norm2_bias, "dp", axis=0, tiled=True),
-        lax.all_gather(w_up, "dp", axis=0, tiled=True),
-        lax.all_gather(w_down, "dp", axis=0, tiled=True),
-    )
-    full_up, full_down = (
-        lax.all_gather(full_up, "tensor", axis=2, tiled=True),
-        lax.all_gather(full_down, "tensor", axis=2, tiled=True),
-    )
+    on_high_core = bit_set("ctx", 1)
+    full_in = pair_share(w_in, 0)
+    half_rows = w_in.shape[0]
+    kernel_rows = w_kernel.shape[0]
+    vectors = jnp.stack([norm1_gain, norm1_bias, norm2_gain, norm2_bias], axis=1)
+    small = fit(
+        jnp.concatenate([w_depth, vectors, fit(w_kernel, half_rows, HEADS * KERNEL)], axis=1),
+        half_rows,
+        128,
+    )
+    packed = pair_share(jnp.concatenate([w_out, w_point, small], axis=1), 0)
+    full_out = packed[:, :D]
+    full_point = packed[:, D : D + HEADS * HEAD_DIM]
+    small = packed[:, D + HEADS * HEAD_DIM :]
+    full_depth = small[:, :KERNEL]
+    gain_one, bias_one, gain_two, bias_two = (small[:, KERNEL + i] for i in range(4))
+    full_kernel = small[:, KERNEL + 4 : KERNEL + 4 + HEADS * KERNEL]
+    full_kernel = jnp.concatenate(
+        [full_kernel[:kernel_rows], full_kernel[half_rows : half_rows + kernel_rows]], axis=0
+    )
+    line = line_gather(jnp.where(on_high_core, w_down, w_up), "tensor")
+    both = unfold(line, "dp", 1, 1)
+    both = jnp.transpose(both, (1, 2, 0, 3)).reshape(2 * w_up.shape[0], GROUPS, -1)
+    other_both = swap(both, "ctx", 1)
+    full_up = jnp.where(on_high_core, other_both, both)
+    full_down = jnp.where(on_high_core, both, other_both)
     piece_rows = hidden.shape[2]
     seq_len = segment_ids.shape[2]
     attn_width = HEADS * HEAD_DIM
@@ -351,10 +443,8 @@
                 for j in range(KERNEL)
             )
         )
-        whole_keys, whole_values = (
-            lax.all_gather(key_rows, "ctx", axis=0, tiled=True),
-            lax.all_gather(value_rows, "ctx", axis=0, tiled=True),
-        )
+        whole_kv = gather_rows(projected[:, attn_width : 3 * attn_width], "ctx")
+        whole_keys, whole_values = whole_kv[:, :attn_width], whole_kv[:, attn_width:]
         heads_q = queries.reshape(piece_rows, HEADS, HEAD_DIM)
         key_blocks = whole_keys.reshape(block_count, block_rows, HEADS, HEAD_DIM)
         value_blocks = whole_values.reshape(block_count, block_rows, HEADS, HEAD_DIM)
@@ -433,9 +523,7 @@
             delta,
             score_scale,
         )
-        own_kv_grads = lax.psum_scatter(
-            all_kv_grads.astype(jnp.bfloat16), "ctx", scatter_dimension=0, tiled=True
-        ).astype(jnp.float32)
+        own_kv_grads = scatter_rows(all_kv_grads.astype(jnp.bfloat16), "ctx").astype(jnp.float32)
         grad_conv = (
             grad_context[:, attn_width:].astype(jnp.float32).reshape(piece_rows, HEADS, HEAD_DIM)
         )
@@ -521,63 +609,53 @@
             down_weight_grad,
         )
         grad_totals = [running + change for running, change in zip(grad_totals, updates)]
-    split_grads = (
-        lax.psum_scatter(
-            grad_totals[0].astype(jnp.bfloat16), "dp", scatter_dimension=0, tiled=True
-        ).astype(jnp.float32),
-        lax.psum_scatter(
-            grad_totals[1].astype(jnp.bfloat16), "dp", scatter_dimension=0, tiled=True
-        ).astype(jnp.float32),
-        lax.psum_scatter(
-            grad_totals[2].astype(jnp.bfloat16), "dp", scatter_dimension=0, tiled=True
-        ).astype(jnp.float32),
-        lax.psum_scatter(
-            grad_totals[3].astype(jnp.bfloat16), "dp", scatter_dimension=0, tiled=True
-        ).astype(jnp.float32),
-        lax.psum_scatter(
-            grad_totals[4].astype(jnp.bfloat16), "dp", scatter_dimension=0, tiled=True
-        ).astype(jnp.float32),
-        lax.psum_scatter(
-            grad_totals[5].astype(jnp.bfloat16), "dp", scatter_dimension=0, tiled=True
-        ).astype(jnp.float32),
-        lax.psum_scatter(
-            grad_totals[6].astype(jnp.bfloat16), "dp", scatter_dimension=0, tiled=True
-        ).astype(jnp.float32),
-        lax.psum_scatter(
-            grad_totals[7].astype(jnp.bfloat16), "dp", scatter_dimension=0, tiled=True
-        ).astype(jnp.float32),
-        lax.psum_scatter(
-            grad_totals[8].astype(jnp.bfloat16), "dp", scatter_dimension=0, tiled=True
-        ).astype(jnp.float32),
-        lax.psum_scatter(
-            grad_totals[9].astype(jnp.bfloat16), "dp", scatter_dimension=0, tiled=True
-        ).astype(jnp.float32),
-        lax.psum_scatter(
-            grad_totals[10].astype(jnp.bfloat16), "dp", scatter_dimension=0, tiled=True
-        ).astype(jnp.float32),
-    )
-    column_count = w_up.shape[2]
-    column_start = lax.axis_index("tensor") * column_count
-    up_split = split_grads[9]
-    down_split = split_grads[10]
-    summed = lax.psum(
-        (
-            split_grads[0],
-            split_grads[1],
-            split_grads[2],
-            split_grads[3],
-            split_grads[4],
-            split_grads[5],
-            split_grads[6],
-            split_grads[7],
-            split_grads[8],
-            up_split,
-            down_split,
-        ),
-        ("ctx", "tensor"),
-    )
-    up_grad_out = lax.dynamic_slice_in_dim(summed[9], column_start, column_count, 2)
-    down_grad_out = lax.dynamic_slice_in_dim(summed[10], column_start, column_count, 2)
+    low_grads = [total.astype(jnp.bfloat16) for total in grad_totals]
+    up_low, down_low = low_grads[9], low_grads[10]
+    far_bits = [bit for bit in bits_of("ctx") if bit > 1]
+    arrived = swap(jnp.where(on_high_core, up_low, down_low), "ctx", 1)
+    block = jnp.where(on_high_core, down_low, up_low)
+    block = (block.astype(jnp.float32) + arrived.astype(jnp.float32)).astype(jnp.bfloat16)
+    block = fold(block, "dp", 1, 0)
+    for bit in far_bits:
+        block = fold(block, "ctx", bit, 0)
+    columns = w_up.shape[2]
+    lanes = len(bits_of("tensor"))
+    block = block.reshape(block.shape[:2] + (2,) * lanes + (columns,))
+    for step, bit in enumerate(bits_of("tensor")):
+        block = fold(block, "tensor", bit, 2 + lanes - 1 - step)
+        block = lax.squeeze(block, (2 + lanes - 1 - step,))
+    for bit in reversed(far_bits):
+        block = unfold(block, "ctx", bit, 0)
+    other = swap(block, "ctx", 1)
+    up_grad_out = jnp.where(on_high_core, other, block).astype(jnp.float32)
+    down_grad_out = jnp.where(on_high_core, block, other).astype(jnp.float32)
+
+    kernel_grad = low_grads[3]
+    spread = jnp.zeros((D, HEADS * KERNEL), jnp.bfloat16)
+    spread = spread.at[:kernel_rows].set(kernel_grad[:kernel_rows])
+    spread = spread.at[half_rows : half_rows + kernel_rows].set(kernel_grad[kernel_rows:])
+    small = fit(
+        jnp.concatenate([low_grads[1], jnp.stack(low_grads[5:9], axis=1), spread], axis=1), D, 128
+    )
+    block = jnp.concatenate([low_grads[0], low_grads[4], low_grads[2], small], axis=1)
+    steps = [("ctx", bit, 0) for bit in bits_of("ctx")]
+    tensor_bits = bits_of("tensor")
+    steps += [("tensor", bit, 1 if i == 0 else 0) for i, bit in enumerate(tensor_bits)]
+    block = block.reshape(2, half_rows, -1)
+    block = fold(block, "dp", 1, 0)[0]
+    for axis, bit, dim in steps:
+        block = fold(block, axis, bit, dim)
+    for axis, bit, dim in reversed(steps):
+        block = unfold(block, axis, bit, dim)
+    block = block.astype(jnp.float32)
+    in_width = w_in.shape[1]
+    summed = [block[:, :in_width]]
+    small = block[:, in_width + D + HEADS * HEAD_DIM :]
+    summed.append(small[:, :KERNEL])
+    summed.append(block[:, in_width + D : in_width + D + HEADS * HEAD_DIM])
+    summed.append(small[:kernel_rows, KERNEL + 4 : KERNEL + 4 + HEADS * KERNEL])
+    summed.append(block[:, in_width : in_width + D])
+    summed += [small[:, KERNEL + i] for i in range(4)]
     layer_output = jnp.stack(outputs_list)[:, None]
     layer_input_grad = jnp.stack(input_grads)[:, None]
     return (

time: 942 us -> 695 us (0.74)
  blocking collectives: 293 us -> 0 us
  waiting for transfers between devices: 249 us -> 150 us
  local copies, waits for them, and re-layouts: 138 us -> 206 us
  other arithmetic: 92.3 us -> 149 us
  starting transfers between devices: 20.5 us -> 64.2 us
  between operations: 24.9 us -> 12 us
    psum x1 -> x0, blocking collectives: 183 us -> none  [body(): lax.psum((split_grads[0], split_grads[1], split_grads[2], split_grads[3],...]
    ppermute x0 -> x36, waiting for transfers between devices: none -> 150 us  [the longest x30 134 us: swap(): return lax.ppermute(block, axis, [(i, i ^ bit) for i in range(count)])]
    psum x1 -> x0, waiting for transfers between devices: 115 us -> none  [body(): lax.psum((split_grads[0], split_grads[1], split_grads[2], split_grads[3],...]
    all_gather x13 -> x0, blocking collectives: 105 us -> none  [the longest x2 19.5 us: body(): lax.all_gather(key_rows, 'ctx', axis=0, tiled=True)]
    reduce_scatter x4 -> x0, waiting for transfers between devices: 82.8 us -> none  [the longest x2 41.5 us: body(): lax.psum_scatter(all_kv_grads.astype(jnp.bfloat16), 'ctx', scatter_dimens...]
    unnamed x17 -> x0, waiting for transfers between devices: 51.5 us -> none
    ppermute x0 -> x36, starting transfers between devices: none -> 44.7 us  [the longest x30 26.1 us: swap(): return lax.ppermute(block, axis, [(i, i ^ bit) for i in range(count)])]
    select_n x0 -> x28, other arithmetic: none -> 24.8 us  [the longest x13 8.52 us: fold(): sent = jnp.where(high, low_half, high_half)]
  transfers between devices with their start and end apart: 21 -> 44, of which waited for: 8 -> 12; matrix products, arithmetic and copies ran while one was open for 30% -> 46% of each run, Pallas kernels for 0% -> 0%
where the time goes in v1:
time: 695 us; the launch traced here: 684 us
  local copies, waits for them, and re-layouts  206 us (30%)
  waiting for transfers between devices  150 us (22%)
  other arithmetic  149 us (21%)
  matrix products  102 us (15%)
  starting transfers between devices  64.2 us (9%)
  between operations  12 us (2%)
    ppermute x30, waiting for transfers between devices, swap(): return lax.ppermute(block, axis, [(i, i ^ bit) for i in range(count)])  134 us
    unnamed x781, local copies, waits for them, and re-layouts  31.3 us
    slice x20, local copies, waits for them, and re-layouts, body(): ext_conv[j:j + piece_rows]  30.7 us
    ppermute x30, starting transfers between devices, swap(): return lax.ppermute(block, axis, [(i, i ^ bit) for i in range(count)])  26.1 us
    ppermute x5, local copies, waits for them, and re-layouts, swap(): return lax.ppermute(block, axis, [(i, i ^ bit) for i in range(count)])  23 us
    mul x36, local copies, waits for them, and re-layouts, body(): kernels[:, :, j:j + 1] * tap_mask[:, j, None, None]  20.8 us
    dot_general x6, matrix products, times_transposed(): lax.dot_general(left, right, (((1,), (1,)), ((), ())), preferred_element_...  17 us
    ppermute x3, starting transfers between devices, line_gather(): from_low = lax.ppermute(from_low, axis, up)  14.7 us
  transfers between devices with their start and end apart: 44, of which 12 were waited for; matrix products, arithmetic and copies ran while one was open for 46% of the time, Pallas kernels for 0%

profile of v1, /device:TPU:0, one launch (start us, length us, event | category | flops | bytes accessed | tf_op | source)
XLA Modules:
  0.0 683.9 jit_solution(7320322607513413611)
XLA Ops:
  3.2 5.7 collective-permute-start.8
  17.3 4.7 collective-permute-start.9
  23.5 6.1 collective-permute-done.9
  29.6 4.3 collective-permute-start.10
  46.2 9.5 %collective-permute-done.13 = bf16[192,2,384]{0,2,1:T(8,128)(2,1)S(1)} collective-permute-done((bf16[192,2,384]{0,2,1:T(8,128)(2,1)S(1)}, bf16[192,2,384]{0,2,1:T(8,128)(2,1)S(1)}, u32[]{:S(2)}, u32[]{:S(2)}) %collective-permute-start.13) | collective-permute-done | bytes 294944 | tf_op jit(solution)/shard_map/ppermute | solution.py:109
  84.6 4.1 collective-permute-start.4
  164.0 15.5 %copy.506 = bf16[4,192,2,384]{1,3,0,2:T(8,128)(2,1)S(1)} copy(bf16[4,192,2,384]{3,1,2,0:T(8,128)(2,1)} %collective-permute-done.14) | data formatting | bytes 2359296 | tf_op jit(solution)/shard_map/ppermute | solution.py:36
  195.5 5.2 conditional.10
  208.8 5.2 conditional.8
  215.3 6.3 conditional.9
  217.1 4.5 fusion.6
  264.0 4.8 add_convert_fusion.3
  275.0 4.8 add_convert_fusion.4
  293.3 4.1 multiply_reduce_fusion.30
  299.4 5.0 multiply_multiply_fusion.8
  315.3 4.1 multiply_reduce_fusion.39
  320.5 4.8 multiply_multiply_fusion.17
  348.6 4.5 conditional.14
  353.1 26.9 %conditional.15 = (f32[256,6,64]{0,2,1:T(8,128)}, bf16[2,1,256,768]{3,2,1,0:T(8,128)(2,1)S(1)}, bf16[2,1,256,768]{3,2,1,0:T(8,128)(2,1)}) conditional(s32[]{:T(128)} %bitcast.61, f32[256,6,64]{0,2,1:T(8,128)S(1)} %broadcast.1001, (s32[256]{0:T(256)S(1)}, s32[1024]{0:T(1024)S(1)}, bf16[256,6,64]{0,2,1:T(8,128)(2,1)S(1)}, ...), branch_computations={%region_60.61_spmd, %region_61.62_spmd} | conditional | flops 1024000000 | bytes 77356160 | solution.py:320
  361.4 5.4 fusion.41
  392.5 4.5 conditional.12
  397.0 21.7 %conditional.13 = (f32[256,6,64]{0,2,1:T(8,128)S(1)}, bf16[2,1,256,768]{3,2,1,0:T(8,128)(2,1)S(1)}, bf16[2,1,256,768]{3,2,1,0:T(8,128)(2,1)S(1)}) conditional(s32[]{:T(128)} %bitcast.9, f32[256,6,64]{0,2,1:T(8,128)S(1)} %broadcast.1001, (s32[256]{0:T(256)S(1)}, s32[1024]{0:T(1024)S(1)}, bf16[256,6,64]{0,2,1:T(8,128)(2,1)S(1)}, ...), branch_computations={%region_41.42_spmd, %region_42.43_spmd} | conditional | flops 1024000000 | bytes 77356160 | solution.py:320
  404.5 4.5 fusion.26
  454.6 8.1 %collective-permute-done.23 = bf16[1,256,768]{2,1,0:T(8,128)(2,1)S(1)} collective-permute-done((bf16[1,256,768]{2,1,0:T(8,128)(2,1)S(1)}, bf16[1,256,768]{2,1,0:T(8,128)(2,1)S(1)}, u32[]{:S(2)}, u32[]{:S(2)}) %collective-permute-start.23) | collective-permute-done | bytes 393248 | tf_op jit(solution)/shard_map/ppermute | solution.py:36
  463.8 6.5 collective-permute-done.27
  481.4 43.0 %collective-permute-done.28 = bf16[1,384,2816]{1,2,0:T(8,128)(2,1)} collective-permute-done((bf16[1,384,2816]{1,2,0:T(8,128)(2,1)}, bf16[1,384,2816]{1,2,0:T(8,128)(2,1)}, u32[]{:S(2)}, u32[]{:S(2)}) %collective-permute-start.28) | collective-permute-done | bytes 2162720 | tf_op jit(solution)/shard_map/ppermute | solution.py:36
  546.3 20.3 %collective-permute-done.38 = bf16[192,2,1536]{2,0,1:T(8,128)(2,1)} collective-permute-done((bf16[192,2,1536]{2,0,1:T(8,128)(2,1)}, bf16[192,2,1536]{2,0,1:T(8,128)(2,1)}, u32[]{:S(2)}, u32[]{:S(2)}) %collective-permute-start.38) | collective-permute-done | bytes 1179680 | tf_op jit(solution)/shard_map/ppermute | solution.py:36
  575.0 9.3 %collective-permute-done.39 = bf16[96,2,1536]{2,0,1:T(8,128)(2,1)} collective-permute-done((bf16[96,2,1536]{2,0,1:T(8,128)(2,1)}, bf16[96,2,1536]{2,0,1:T(8,128)(2,1)}, u32[]{:S(2)}, u32[]{:S(2)}) %collective-permute-start.39) | collective-permute-done | bytes 589856 | tf_op jit(solution)/shard_map/ppermute | solution.py:36
  593.3 13.2 %collective-permute-done.32 = bf16[48,1408]{0,1:T(8,128)(2,1)S(1)} collective-permute-done((bf16[48,1408]{0,1:T(8,128)(2,1)S(1)}, bf16[48,1408]{0,1:T(8,128)(2,1)S(1)}, u32[]{:S(2)}, u32[]{:S(2)}) %collective-permute-start.32) | collective-permute-done | bytes 135200 | tf_op jit(solution)/shard_map/ppermute | solution.py:36
  609.0 13.8 %collective-permute-done.33 = bf16[48,1408]{0,1:T(8,128)(2,1)S(1)} collective-permute-done((bf16[48,1408]{0,1:T(8,128)(2,1)S(1)}, bf16[48,1408]{0,1:T(8,128)(2,1)S(1)}, u32[]{:S(2)}, u32[]{:S(2)}) %collective-permute-start.33) | collective-permute-done | bytes 135200 | tf_op jit(solution)/shard_map/ppermute | solution.py:36
  627.3 10.3 %collective-permute-done.34 = bf16[96,1408]{0,1:T(8,128)(2,1)S(1)} collective-permute-done((bf16[96,1408]{0,1:T(8,128)(2,1)S(1)}, bf16[96,1408]{0,1:T(8,128)(2,1)S(1)}, u32[]{:S(2)}, u32[]{:S(2)}) %collective-permute-start.34) | collective-permute-done | bytes 270368 | tf_op jit(solution)/shard_map/ppermute | solution.py:36
  646.3 8.2 %collective-permute-done.35 = bf16[96,2816]{1,0:T(8,128)(2,1)S(1)} collective-permute-done((bf16[96,2816]{1,0:T(8,128)(2,1)}, bf16[96,2816]{1,0:T(8,128)(2,1)S(1)}, u32[]{:S(2)}, u32[]{:S(2)}) %collective-permute-start.35) | collective-permute-done | bytes 540704 | tf_op jit(solution)/shard_map/ppermute | solution.py:36
  (1318 shorter events, 450.3 us)
Async XLA Ops:
  12.3 29.8 %collective-permute-start.6 = (bf16[192,1280]{1,0:T(8,128)(2,1)}, bf16[192,1280]{1,0:T(8,128)(2,1)}, u32[]{:S(2)}, u32[]{:S(2)}) collective-permute-start(bf16[192,1280]{1,0:T(8,128)(2,1)} %slice_select_fusion.1), channel_id=1, source_target_pairs={{0,16},{16,0},{1,17},{17,1},{2,18},{18,2},{3,19},{19,3},{4,20},{20... | collective-permute-start | bytes 1474568 | tf_op jit(solution)/shard_map/ppermute | solution.py:36
  14.7 27.5 %collective-permute-start = (bf16[192,1536]{1,0:T(8,128)(2,1)}, bf16[192,1536]{1,0:T(8,128)(2,1)}, u32[]{:S(2)}, u32[]{:S(2)}) collective-permute-start(bf16[192,1536]{1,0:T(8,128)(2,1)} %slice_select_fusion), channel_id=1, source_target_pairs={{0,16},{16,0},{1,17},{17,1},{2,18},{18,2},{3,19},{19,3},{4,20},{20... | collective-permute-start | bytes 1769480 | tf_op jit(solution)/shard_map/ppermute | solution.py:36
  22.2 20.4 %collective-permute-start.12 = (bf16[192,2,384]{0,2,1:T(8,128)(2,1)}, bf16[192,2,384]{0,2,1:T(8,128)(2,1)S(1)}, u32[]{:S(2)}, u32[]{:S(2)}) collective-permute-start(bf16[192,2,384]{0,2,1:T(8,128)(2,1)} %collective-permute-done.11), channel_id=1, source_target_pairs={{1,0},{2,1},{3,2},{5,4},{6,5},{7,6},{9,8},{10,9},{11,10},{13,12},{... | collective-permute-start | bytes 884744 | tf_op jit(solution)/shard_map/ppermute | solution.py:109
  42.1 18.3 %collective-permute-start.7 = (bf16[192,1280]{1,0:T(8,128)(2,1)}, bf16[192,1280]{1,0:T(8,128)(2,1)}, u32[]{:S(2)}, u32[]{:S(2)}) collective-permute-start(bf16[192,1280]{1,0:T(8,128)(2,1)} %collective-permute-done.6), channel_id=1, source_target_pairs={{0,4},{4,0},{8,12},{12,8},{1,5},{5,1},{9,13},{13,9},{2,6},{6,2},{1... | collective-permute-start | bytes 1474568 | tf_op jit(solution)/shard_map/ppermute | solution.py:36
  42.2 26.7 %collective-permute-start.1 = (bf16[192,1536]{1,0:T(8,128)(2,1)}, bf16[192,1536]{1,0:T(8,128)(2,1)}, u32[]{:S(2)}, u32[]{:S(2)}) collective-permute-start(bf16[192,1536]{1,0:T(8,128)(2,1)} %collective-permute-done), channel_id=1, source_target_pairs={{0,4},{4,0},{8,12},{12,8},{1,5},{5,1},{9,13},{13,9},{2,6},{6,2},{1... | collective-permute-start | bytes 1769480 | tf_op jit(solution)/shard_map/ppermute | solution.py:36
  58.9 105.1 %collective-permute-start.14 = (bf16[4,192,2,384]{3,1,2,0:T(8,128)(2,1)}, bf16[4,192,2,384]{3,1,2,0:T(8,128)(2,1)}, u32[]{:S(2)}, u32[]{:S(2)}) collective-permute-start(bf16[4,192,2,384]{3,1,2,0:T(8,128)(2,1)} %copy.505), channel_id=1, source_target_pairs={{0,16},{16,0},{1,17},{17,1},{2,18},{18,2},{3,19},{19,3},{4,20},{20... | collective-permute-start | bytes 3538952 | tf_op jit(solution)/shard_map/ppermute | solution.py:36
  80.3 74.4 %collective-permute-start.16 = (bf16[256,768]{0,1:T(8,128)(2,1)}, bf16[256,768]{0,1:T(8,128)(2,1)}, u32[]{:S(2)}, u32[]{:S(2)}) collective-permute-start(bf16[256,768]{0,1:T(8,128)(2,1)} %slice.1345), channel_id=1, source_target_pairs={{0,8},{4,12},{8,0},{12,4},{1,9},{5,13},{9,1},{13,5},{2,10},{6,14},... | collective-permute-start | bytes 1179656 | tf_op jit(solution)/shard_map/ppermute | solution.py:36
  81.9 76.1 %collective-permute-start.2 = (bf16[256,768]{0,1:T(8,128)(2,1)}, bf16[256,768]{0,1:T(8,128)(2,1)}, u32[]{:S(2)}, u32[]{:S(2)}) collective-permute-start(bf16[256,768]{0,1:T(8,128)(2,1)} %slice.1280), channel_id=1, source_target_pairs={{0,8},{4,12},{8,0},{12,4},{1,9},{5,13},{9,1},{13,5},{2,10},{6,14},... | collective-permute-start | bytes 1179656 | tf_op jit(solution)/shard_map/ppermute | solution.py:36
  83.3 22.7 %collective-permute-start.5 = (bf16[4,1152]{1,0:T(4,128)(2,1)}, bf16[4,1152]{1,0:T(4,128)(2,1)}, u32[]{:S(2)}, u32[]{:S(2)}) collective-permute-start(bf16[4,1152]{1,0:T(4,128)(2,1)} %get-tuple-element.936), channel_id=1, source_target_pairs={{4,0},{8,4},{12,8},{5,1},{9,5},{13,9},{6,2},{10,6},{14,10},{7,3},{... | collective-permute-start | bytes 27656 | tf_op jit(solution)/shard_map/ppermute | solution.py:29
  84.6 21.4 %collective-permute-start.4 = (bf16[4,1152]{1,0:T(4,128)(2,1)}, bf16[4,1152]{1,0:T(4,128)(2,1)}, u32[]{:S(2)}, u32[]{:S(2)}) collective-permute-start(bf16[4,1152]{1,0:T(4,128)(2,1)} %get-tuple-element.935), channel_id=1, source_target_pairs={{0,4},{4,8},{8,12},{1,5},{5,9},{9,13},{2,6},{6,10},{10,14},{3,7},{... | collective-permute-start | bytes 27656 | tf_op jit(solution)/shard_map/ppermute | solution.py:26
  156.9 26.7 %collective-permute-start.17 = (bf16[2,256,768]{1,2,0:T(8,128)(2,1)}, bf16[2,256,768]{1,2,0:T(8,128)(2,1)}, u32[]{:S(2)}, u32[]{:S(2)}) collective-permute-start(bf16[2,256,768]{1,2,0:T(8,128)(2,1)} %pad_maximum_fusion.10), channel_id=1, source_target_pairs={{0,4},{4,0},{8,12},{12,8},{1,5},{5,1},{9,13},{13,9},{2,6},{6,2},{1... | collective-permute-start | bytes 2359304 | tf_op jit(solution)/shard_map/ppermute | solution.py:36
  160.2 23.3 %collective-permute-start.3 = (bf16[2,256,768]{1,2,0:T(8,128)(2,1)}, bf16[2,256,768]{1,2,0:T(8,128)(2,1)}, u32[]{:S(2)}, u32[]{:S(2)}) collective-permute-start(bf16[2,256,768]{1,2,0:T(8,128)(2,1)} %pad_maximum_fusion.9), channel_id=1, source_target_pairs={{0,4},{4,0},{8,12},{12,8},{1,5},{5,1},{9,13},{13,9},{2,6},{6,2},{1... | collective-permute-start | bytes 2359304 | tf_op jit(solution)/shard_map/ppermute | solution.py:36
  183.3 48.9 %collective-permute-start.15 = (bf16[384,2,1536]{0,2,1:T(8,128)(2,1)}, bf16[384,2,1536]{0,2,1:T(8,128)(2,1)}, u32[]{:S(2)}, u32[]{:S(2)}) collective-permute-start(bf16[384,2,1536]{0,2,1:T(8,128)(2,1)} %bitcast.54), channel_id=1, source_target_pairs={{0,4},{4,0},{8,12},{12,8},{1,5},{5,1},{9,13},{13,9},{2,6},{6,2},{1... | collective-permute-start | bytes 7077896 | tf_op jit(solution)/shard_map/ppermute | solution.py:36
  343.5 98.2 %collective-permute-start.25 = (bf16[4,1152]{1,0:T(4,128)(2,1)}, bf16[4,1152]{1,0:T(4,128)(2,1)}, u32[]{:S(2)}, u32[]{:S(2)}) collective-permute-start(bf16[4,1152]{1,0:T(4,128)(2,1)} %get-tuple-element.932), channel_id=1, source_target_pairs={{4,0},{8,4},{12,8},{5,1},{9,5},{13,9},{6,2},{10,6},{14,10},{7,3},{... | collective-permute-start | bytes 27656 | tf_op jit(solution)/shard_map/ppermute | solution.py:29
  344.8 97.7 %collective-permute-start.24 = (bf16[4,1152]{1,0:T(4,128)(2,1)}, bf16[4,1152]{1,0:T(4,128)(2,1)}, u32[]{:S(2)}, u32[]{:S(2)}) collective-permute-start(bf16[4,1152]{1,0:T(4,128)(2,1)} %get-tuple-element.931), channel_id=1, source_target_pairs={{0,4},{4,8},{8,12},{1,5},{5,9},{9,13},{2,6},{6,10},{10,14},{3,7},{... | collective-permute-start | bytes 27656 | tf_op jit(solution)/shard_map/ppermute | solution.py:26
  381.0 69.7 %collective-permute-start.26 = (bf16[2,1,256,768]{3,2,1,0:T(8,128)(2,1)}, bf16[2,1,256,768]{3,2,1,0:T(8,128)(2,1)}, u32[]{:S(2)}, u32[]{:S(2)}) collective-permute-start(bf16[2,1,256,768]{3,2,1,0:T(8,128)(2,1)} %broadcast_select_fusion.11), channel_id=1, source_target_pairs={{0,4},{4,0},{8,12},{12,8},{1,5},{5,1},{9,13},{13,9},{2,6},{6,2},{1... | collective-permute-start | bytes 2359304 | tf_op jit(solution)/shard_map/ppermute | solution.py:36
  386.7 59.6 %collective-permute-start.21 = (bf16[4,1152]{1,0:T(4,128)(2,1)}, bf16[4,1152]{1,0:T(4,128)(2,1)}, u32[]{:S(2)}, u32[]{:S(2)}) collective-permute-start(bf16[4,1152]{1,0:T(4,128)(2,1)} %get-tuple-element.930), channel_id=1, source_target_pairs={{4,0},{8,4},{12,8},{5,1},{9,5},{13,9},{6,2},{10,6},{14,10},{7,3},{... | collective-permute-start | bytes 27656 | tf_op jit(solution)/shard_map/ppermute | solution.py:29
  388.0 58.3 %collective-permute-start.20 = (bf16[4,1152]{1,0:T(4,128)(2,1)}, bf16[4,1152]{1,0:T(4,128)(2,1)}, u32[]{:S(2)}, u32[]{:S(2)}) collective-permute-start(bf16[4,1152]{1,0:T(4,128)(2,1)} %get-tuple-element.929), channel_id=1, source_target_pairs={{0,4},{4,8},{8,12},{1,5},{5,9},{9,13},{2,6},{6,10},{10,14},{3,7},{... | collective-permute-start | bytes 27656 | tf_op jit(solution)/shard_map/ppermute | solution.py:26
  452.6 17.7 %collective-permute-start.27 = (bf16[1,256,768]{2,1,0:T(8,128)(2,1)S(1)}, bf16[1,256,768]{2,1,0:T(8,128)(2,1)S(1)}, u32[]{:S(2)}, u32[]{:S(2)}) collective-permute-start(bf16[1,256,768]{2,1,0:T(8,128)(2,1)S(1)} %select_bitcast_fusion.7), channel_id=1, source_target_pairs={{0,8},{4,12},{8,0},{12,4},{1,9},{5,13},{9,1},{13,5},{2,10},{6,14},... | collective-permute-start | bytes 1179656 | tf_op jit(solution)/shard_map/ppermute | solution.py:36
  475.9 48.5 %collective-permute-start.28 = (bf16[1,384,2816]{1,2,0:T(8,128)(2,1)}, bf16[1,384,2816]{1,2,0:T(8,128)(2,1)}, u32[]{:S(2)}, u32[]{:S(2)}) collective-permute-start(bf16[1,384,2816]{1,2,0:T(8,128)(2,1)} %select_bitcast_fusion.1), channel_id=1, source_target_pairs={{0,16},{16,0},{1,17},{17,1},{2,18},{18,2},{3,19},{19,3},{4,20},{20... | collective-permute-start | bytes 6488072 | tf_op jit(solution)/shard_map/ppermute | solution.py:36
  480.5 51.5 %collective-permute-start.37 = (bf16[384,2,1536]{2,0,1:T(8,128)(2,1)}, bf16[384,2,1536]{2,0,1:T(8,128)(2,1)}, u32[]{:S(2)}, u32[]{:S(2)}) collective-permute-start(bf16[384,2,1536]{2,0,1:T(8,128)(2,1)} %select_bitcast_fusion), channel_id=1, source_target_pairs={{0,4},{4,0},{8,12},{12,8},{1,5},{5,1},{9,13},{13,9},{2,6},{6,2},{1... | collective-permute-start | bytes 7077896 | tf_op jit(solution)/shard_map/ppermute | solution.py:36
  537.9 28.7 %collective-permute-start.38 = (bf16[192,2,1536]{2,0,1:T(8,128)(2,1)}, bf16[192,2,1536]{2,0,1:T(8,128)(2,1)}, u32[]{:S(2)}, u32[]{:S(2)}) collective-permute-start(bf16[192,2,1536]{2,0,1:T(8,128)(2,1)} %broadcast_select_fusion.6), channel_id=1, source_target_pairs={{0,16},{16,0},{1,17},{17,1},{2,18},{18,2},{3,19},{19,3},{4,20},{20... | collective-permute-start | bytes 3538952 | tf_op jit(solution)/shard_map/ppermute | solution.py:36
  545.7 24.0 %collective-permute-start.30 = (bf16[96,2816]{1,0:T(8,128)(2,1)}, bf16[96,2816]{1,0:T(8,128)(2,1)}, u32[]{:S(2)}, u32[]{:S(2)}) collective-permute-start(bf16[96,2816]{1,0:T(8,128)(2,1)} %copy.579), channel_id=1, source_target_pairs={{0,8},{4,12},{8,0},{12,4},{1,9},{5,13},{9,1},{13,5},{2,10},{6,14},... | collective-permute-start | bytes 1622024 | tf_op jit(solution)/shard_map/ppermute | solution.py:36
  569.1 15.2 %collective-permute-start.39 = (bf16[96,2,1536]{2,0,1:T(8,128)(2,1)}, bf16[96,2,1536]{2,0,1:T(8,128)(2,1)}, u32[]{:S(2)}, u32[]{:S(2)}) collective-permute-start(bf16[96,2,1536]{2,0,1:T(8,128)(2,1)} %broadcast_select_fusion.16), channel_id=1, source_target_pairs={{0,8},{4,12},{8,0},{12,4},{1,9},{5,13},{9,1},{13,5},{2,10},{6,14},... | collective-permute-start | bytes 1769480 | tf_op jit(solution)/shard_map/ppermute | solution.py:36
  573.5 14.9 %collective-permute-start.31 = (bf16[96,1408]{0,1:T(8,128)(2,1)S(1)}, bf16[96,1408]{0,1:T(8,128)(2,1)S(1)}, u32[]{:S(2)}, u32[]{:S(2)}) collective-permute-start(bf16[96,1408]{0,1:T(8,128)(2,1)S(1)} %broadcast_select_fusion.28), channel_id=1, source_target_pairs={{0,1},{1,0},{2,3},{3,2},{4,5},{5,4},{6,7},{7,6},{8,9},{9,8},{10,11... | collective-permute-start | bytes 811016 | tf_op jit(solution)/shard_map/ppermute | solution.py:36
  588.7 17.8 %collective-permute-start.32 = (bf16[48,1408]{0,1:T(8,128)(2,1)S(1)}, bf16[48,1408]{0,1:T(8,128)(2,1)S(1)}, u32[]{:S(2)}, u32[]{:S(2)}) collective-permute-start(bf16[48,1408]{0,1:T(8,128)(2,1)S(1)} %broadcast_select_fusion.25), channel_id=1, source_target_pairs={{0,2},{1,3},{2,0},{3,1},{4,6},{5,7},{6,4},{7,5},{8,10},{9,11},{10,... | collective-permute-start | bytes 405512 | tf_op jit(solution)/shard_map/ppermute | solution.py:36
  606.7 16.1 %collective-permute-start.33 = (bf16[48,1408]{0,1:T(8,128)(2,1)S(1)}, bf16[48,1408]{0,1:T(8,128)(2,1)S(1)}, u32[]{:S(2)}, u32[]{:S(2)}) collective-permute-start(bf16[48,1408]{0,1:T(8,128)(2,1)S(1)} %add_convert_fusion.16), channel_id=1, source_target_pairs={{0,2},{1,3},{2,0},{3,1},{4,6},{5,7},{6,4},{7,5},{8,10},{9,11},{10,... | collective-permute-start | bytes 405512 | tf_op jit(solution)/shard_map/ppermute | solution.py:36
  606.8 18.0 %collective-permute-start.40 = (bf16[96,2,2,1,384]{0,4,1,2,3:T(8,128)(2,1)S(1)}, bf16[96,2,2,1,384]{0,4,1,2,3:T(8,128)(2,1)S(1)}, u32[]{:S(2)}, u32[]{:S(2)}) collective-permute-start(bf16[96,2,2,1,384]{0,4,1,2,3:T(8,128)(2,1)S(1)} %broadcast_select_fusion.21), channel_id=1, source_target_pairs={{0,1},{1,0},{2,3},{3,2},{4,5},{5,4},{6,7},{7,6},{8,9},{9,8},{10,11... | collective-permute-start | bytes 884744 | tf_op jit(solution)/shard_map/ppermute | solution.py:36
  623.0 14.6 %collective-permute-start.34 = (bf16[96,1408]{0,1:T(8,128)(2,1)S(1)}, bf16[96,1408]{0,1:T(8,128)(2,1)S(1)}, u32[]{:S(2)}, u32[]{:S(2)}) collective-permute-start(bf16[96,1408]{0,1:T(8,128)(2,1)S(1)} %pad_maximum_fusion.19), channel_id=1, source_target_pairs={{0,1},{1,0},{2,3},{3,2},{4,5},{5,4},{6,7},{7,6},{8,9},{9,8},{10,11... | collective-permute-start | bytes 811016 | tf_op jit(solution)/shard_map/ppermute | solution.py:36
  625.6 17.5 %collective-permute-start.41 = (bf16[96,2,1,384]{0,3,1,2:T(8,128)(2,1)}, bf16[96,2,1,384]{0,3,1,2:T(8,128)(2,1)}, u32[]{:S(2)}, u32[]{:S(2)}) collective-permute-start(bf16[96,2,1,384]{0,3,1,2:T(8,128)(2,1)} %broadcast_select_fusion.29), channel_id=1, source_target_pairs={{0,2},{1,3},{2,0},{3,1},{4,6},{5,7},{6,4},{7,5},{8,10},{9,11},{10,... | collective-permute-start | bytes 442376 | tf_op jit(solution)/shard_map/ppermute | solution.py:36
  639.1 15.4 %collective-permute-start.35 = (bf16[96,2816]{1,0:T(8,128)(2,1)}, bf16[96,2816]{1,0:T(8,128)(2,1)S(1)}, u32[]{:S(2)}, u32[]{:S(2)}) collective-permute-start(bf16[96,2816]{1,0:T(8,128)(2,1)} %copy.581), channel_id=1, source_target_pairs={{0,8},{4,12},{8,0},{12,4},{1,9},{5,13},{9,1},{13,5},{2,10},{6,14},... | collective-permute-start | bytes 1622024 | tf_op jit(solution)/shard_map/ppermute | solution.py:36
  644.8 14.9 %collective-permute-start.42 = (bf16[96,2,384]{0,2,1:T(8,128)(2,1)}, bf16[96,2,384]{0,2,1:T(8,128)(2,1)}, u32[]{:S(2)}, u32[]{:S(2)}) collective-permute-start(bf16[96,2,384]{0,2,1:T(8,128)(2,1)} %fusion.121), channel_id=1, source_target_pairs={{0,8},{4,12},{8,0},{12,4},{1,9},{5,13},{9,1},{13,5},{2,10},{6,14},... | collective-permute-start | bytes 442376 | tf_op jit(solution)/shard_map/ppermute | solution.py:36
  (396 other events, 2649.5 us)

commit v2 on v0

v2 whole, which is shorter than its diff:
```python
import functools

import jax
import jax.numpy as jnp
from jax import lax
from jax.experimental import pallas as pl
from jax.experimental.pallas import tpu as pltpu
from jax.sharding import PartitionSpec as P

D = 768
HEADS = 6
HEAD_DIM = 64
KERNEL = 9
GROUPS = 2
MICRO = 2
WIDTH = HEADS * HEAD_DIM
PAIRS = HEADS // 2
RADIUS = KERNEL // 2
HALO = 16
SLOT = 8
LANES = 128
GROUP_WIDTH = D // GROUPS
NORM_EPS = 1e-05
NEG_FILL = -1e30
SCORE_SCALE = HEAD_DIM ** (-0.5)
F32 = jnp.float32
BF16 = jnp.bfloat16
VMEM_BYTES = 60 * 1024 * 1024


def nn(left, right):
    return lax.dot_general(left, right, (((1,), (0,)), ((), ())), preferred_element_type=F32)


def nt(left, right):
    return lax.dot_general(left, right, (((1,), (1,)), ((), ())), preferred_element_type=F32)


def tn(left, right):
    return lax.dot_general(left, right, (((0,), (0,)), ((), ())), preferred_element_type=F32)


def split(values):
    high = values.astype(BF16)
    return high, (values - high.astype(F32)).astype(BF16)


def rows_at(start, size, unit=16):
    return pl.ds(pl.multiple_of(start, unit), size)


def whole(shape):
    return pl.BlockSpec(shape, lambda *_: (0,) * len(shape))


def per_micro(shape):
    return pl.BlockSpec((None,) + shape, lambda m: (m,) + (0,) * len(shape))


SCALARS = pl.BlockSpec(memory_space=pltpu.SMEM)


def run(kernel, outs, args, specs=None, out_specs=None, grid=None, scratch=(), flops=0, name=None):
    moved = sum(a.size * a.dtype.itemsize for a in args) + sum(
        o.size * o.dtype.itemsize for o in outs
    )
    extra = {} if grid is None else {"grid": grid}
    if specs is None:
        specs = [SCALARS] + [pl.BlockSpec(memory_space=pltpu.VMEM)] * (len(args) - 1)
    if out_specs is None:
        out_specs = [pl.BlockSpec(memory_space=pltpu.VMEM)] * len(outs)
    return pl.pallas_call(
        kernel,
        out_shape=tuple(outs),
        in_specs=specs,
        out_specs=tuple(out_specs),
        scratch_shapes=list(scratch),
        compiler_params=pltpu.CompilerParams(vmem_limit_bytes=VMEM_BYTES),
        cost_estimate=pl.CostEstimate(flops=int(flops), bytes_accessed=moved, transcendentals=0),
        name=name,
        **extra,
    )(*args)


def shaped(shape, kind):
    return jax.ShapeDtypeStruct(shape, kind)


DP, CORE, YBIT, TENSOR, CTX = range(5)


def assemble(target, pos, own, mine, theirs):
    dp, core = pos[DP], pos[CORE]
    half, part = own.shape[0], mine.shape[0]
    target[rows_at(dp * half, half), :] = own
    target[rows_at((1 - dp) * half + core * part, part), :] = mine
    target[rows_at((1 - dp) * half + (1 - core) * part, part), :] = theirs


def kv_kernel(pos, tokens, own, mine, theirs, kv_out, w_out, table):
    assemble(w_out, pos, own[:, WIDTH : 3 * WIDTH], mine[...], theirs[...])

    def step(i, carry):
        rows = rows_at(i * 128, 128)
        kv_out[rows, :] = nn(tokens[rows, :], w_out[...]).astype(BF16)
        return carry

    lax.fori_loop(0, tokens.shape[0] // 128, step, 0)


def slot_max(values):
    for shift in (8, 16, 32, 64):
        values = jnp.maximum(values, pltpu.roll(values, shift, 1))
    return values


def slot_sum(values):
    for shift in (8, 16, 32, 64):
        values = values + pltpu.roll(values, shift, 1)
    return values


def tap_column(mask, j):
    return mask[:, SLOT * j : SLOT * j + 1]


def conv_kernel(
    pos, ext, mask, own_in, own_point, mine, theirs, taps, w_tap, spread,
    q_out, c_out, pre_out, key_out, mixed_out, kern_out, conv_out, w_qcp,
    ext_f, c_f, acc,
):
    rows = q_out.shape[0]
    span = ext.shape[0]

    @pl.when(pl.program_id(0) == 0)
    def _():
        assemble(w_qcp.at[:, :WIDTH], pos, own_in[:, :WIDTH], mine[:, :WIDTH], theirs[:, :WIDTH])
        assemble(
            w_qcp.at[:, WIDTH : 2 * WIDTH], pos, own_in[:, 3 * WIDTH :],
            mine[:, WIDTH : 2 * WIDTH], theirs[:, WIDTH : 2 * WIDTH],
        )
        assemble(
            w_qcp.at[:, 2 * WIDTH :], pos, own_point[...], mine[:, 2 * WIDTH :], theirs[:, 2 * WIDTH :]
        )

    ext_f[...] = ext[...].astype(F32)
    q = nn(ext[HALO : HALO + rows, :], w_qcp[:, :WIDTH]).astype(BF16)
    q_out[...] = q
    c_low = nn(ext[...], w_qcp[:, WIDTH : 2 * WIDTH]).astype(BF16)
    c_out[...] = c_low
    c_f[...] = c_low.astype(F32)

    def pre_step(i, carry):
        start = i * 64
        mask_rows = mask[rows_at(start, 64), :]
        for lane in range(0, D, 256):
            block = ext_f[rows_at(start + 8, 80, 8), lane : lane + 256]
            total = jnp.zeros((64, 256), F32)
            for j in range(KERNEL):
                total += block[RADIUS + j : RADIUS + j + 64, :] * taps[j : j + 1, lane : lane + 256] * tap_column(mask_rows, j)
            pre_out[rows_at(start, 64), lane : lane + 256] = total.astype(BF16)
        return carry

    lax.fori_loop(0, rows // 64, pre_step, 0)
    conv_key = nn(pre_out[...], w_qcp[:, 2 * WIDTH :])
    key_out[...] = conv_key
    mixed = (conv_key * q.astype(F32)).astype(BF16)
    mixed_out[...] = mixed
    logits = nn(mixed, w_tap[...])
    lane_id = lax.broadcasted_iota(jnp.int32, logits.shape, 1)
    logits = jnp.where(lane_id < SLOT * KERNEL, logits, NEG_FILL)
    expo = jnp.exp(logits - slot_max(logits))
    kern = expo / slot_sum(expo)
    kern_out[...] = kern
    high, low = split(kern * mask[...])
    both = jnp.concatenate([high, low], axis=1)
    for j in range(KERNEL):
        part = nn(both, spread[j]) * c_f[HALO - RADIUS + j : HALO - RADIUS + j + rows, :]
        if j == 0:
            acc[...] = part
        else:
            acc[...] += part
    conv_out[...] = acc[...].astype(BF16)


def attend_kernel(bounds, q, kv, key_ids, query_ids, context_out, out_t, lse_out, q_t, top, total, acc):
    micro = pl.program_id(0)
    block = q.shape[0]
    rows = q.shape[0]
    half = lax.broadcasted_iota(jnp.int32, (LANES, rows), 0) < HEAD_DIM
    scaled = q[...].astype(F32) * SCORE_SCALE
    for p in range(PAIRS):
        pair = jnp.transpose(scaled[:, p * LANES : (p + 1) * LANES])
        q_t[2 * p] = jnp.where(half, pair, 0.0).astype(BF16)
        q_t[2 * p + 1] = jnp.where(half, 0.0, pair).astype(BF16)
    top[...] = jnp.full_like(top, NEG_FILL)
    total[...] = jnp.zeros_like(total)
    acc[...] = jnp.zeros_like(acc)

    def step(b, carry):
        keys = rows_at(b * block, block)
        bias = jnp.where(key_ids[keys, :] == query_ids[...], 0.0, NEG_FILL)
        for h in range(HEADS):
            p = h // 2
            k_block = kv[keys, p * LANES : (p + 1) * LANES]
            v_block = kv[keys, WIDTH + p * LANES : WIDTH + (p + 1) * LANES]
            scores = nn(k_block, q_t[h]) + bias
            old = top[h : h + 1, :]
            new = jnp.maximum(old, jnp.max(scores, axis=0, keepdims=True))
            scale = jnp.exp(old - new)
            weights = jnp.exp(scores - new)
            total[h : h + 1, :] = total[h : h + 1, :] * scale + jnp.sum(weights, axis=0, keepdims=True)
            top[h : h + 1, :] = new
            part = tn(v_block, weights.astype(BF16))
            first = (h % 2) * HEAD_DIM
            own = slice(h * HEAD_DIM, (h + 1) * HEAD_DIM)
            acc[own, :] = acc[own, :] * scale + part[first : first + HEAD_DIM, :]
        return carry

    lax.fori_loop(bounds[0, micro], bounds[1, micro], step, 0)
    lse_out[...] = top[...] + jnp.log(jnp.maximum(total[...], 1e-37))
    for h in range(HEADS):
        own = slice(h * HEAD_DIM, (h + 1) * HEAD_DIM)
        out_t[own, :] = acc[own, :] / total[h : h + 1, :]
    for p in range(PAIRS):
        pair = slice(p * LANES, (p + 1) * LANES)
        context_out[:, pair] = jnp.transpose(out_t[pair, :]).astype(BF16)


def attend_back_kernel(
    bounds, pos, q, grad, kv, key_ids, query_ids, lse, out_t, dq_out, kv_grad,
    q_t, g_t, q_z, g_z, delta, acc,
):
    micro = pl.program_id(0)
    rows = q.shape[0]
    block = rows
    half = lax.broadcasted_iota(jnp.int32, (LANES, rows), 0) < HEAD_DIM
    half_lane = lax.broadcasted_iota(jnp.int32, (rows, LANES), 1) < HEAD_DIM
    for p in range(PAIRS):
        lanes = slice(p * LANES, (p + 1) * LANES)
        q_pair = q[:, lanes].astype(F32) * SCORE_SCALE
        g_pair = grad[:, lanes].astype(F32)
        for source, across, along in ((q_pair, q_t, q_z), (g_pair, g_t, g_z)):
            turned = jnp.transpose(source)
            across[2 * p] = jnp.where(half, turned, 0.0).astype(BF16)
            across[2 * p + 1] = jnp.where(half, 0.0, turned).astype(BF16)
            along[2 * p] = jnp.where(half_lane, source, 0.0).astype(BF16)
            along[2 * p + 1] = jnp.where(half_lane, 0.0, source).astype(BF16)
            if source is g_pair:
                product = turned * out_t[lanes, :]
                delta[2 * p : 2 * p + 1, :] = jnp.sum(product[:HEAD_DIM], axis=0, keepdims=True)
                delta[2 * p + 1 : 2 * p + 2, :] = jnp.sum(product[HEAD_DIM:], axis=0, keepdims=True)
    acc[...] = jnp.zeros_like(acc)
    kv_grad[...] = jnp.zeros_like(kv_grad)

    def step(b, carry):
        keys = rows_at(b * block, block)
        place = jnp.bitwise_xor(b, pos[CTX])
        near, far = place % 2, place // 2
        bias = jnp.where(key_ids[keys, :] == query_ids[...], 0.0, NEG_FILL)
        for p in range(PAIRS):
            lanes = slice(p * LANES, (p + 1) * LANES)
            k_block = kv[keys, lanes]
            v_block = kv[keys, WIDTH + p * LANES : WIDTH + (p + 1) * LANES]
            k_grad = v_grad = 0.0
            for h in (2 * p, 2 * p + 1):
                weights = jnp.exp(nn(k_block, q_t[h]) + bias - lse[h : h + 1, :])
                slopes = (weights * (nn(v_block, g_t[h]) - delta[h : h + 1, :])).astype(BF16)
                first = (h % 2) * HEAD_DIM
                own = slice(h * HEAD_DIM, (h + 1) * HEAD_DIM)
                acc[own, :] += tn(k_block, slopes)[first : first + HEAD_DIM, :]
                k_grad = k_grad + nn(slopes, q_z[h])
                v_grad = v_grad + nn(weights.astype(BF16), g_z[h])
            kv_grad[near, far, :, lanes] = k_grad.astype(BF16)
            kv_grad[near, far, :, WIDTH + p * LANES : WIDTH + (p + 1) * LANES] = v_grad.astype(BF16)
        return carry

    lax.fori_loop(bounds[0, micro], bounds[1, micro], step, 0)
    for p in range(PAIRS):
        pair = slice(p * LANES, (p + 1) * LANES)
        dq_out[:, pair] = jnp.transpose(acc[pair, :]) * SCORE_SCALE


def gelu_parts(values):
    spread = 0.5 * (1.0 + lax.erf(values * 0.7071067811865476))
    slope = spread + values * (jnp.exp(values * values * -0.5) * 0.3989422804014327)
    return values * spread, slope


def norm_stats(values):
    average = jnp.mean(values, axis=-1, keepdims=True)
    centred = values - average
    inverse = lax.rsqrt(jnp.mean(centred * centred, axis=-1, keepdims=True) + NORM_EPS)
    return centred * inverse, inverse


def norm_back(scaled, normal, inverse):
    inner = (
        scaled
        - jnp.mean(scaled, axis=-1, keepdims=True)
        - normal * jnp.mean(scaled * normal, axis=-1, keepdims=True)
    )
    return inner * inverse


def emit_rows(source, pos, keep, send):
    depth = keep.shape[3]
    for cc, target in ((0, keep), (1, send)):
        for dd in range(2):
            for yy in range(2):
                for k in range(keep.shape[2]):
                    start = (
                        jnp.bitwise_xor(pos[DP], dd) * (D // 2)
                        + jnp.bitwise_xor(pos[CORE], cc) * (D // 4)
                        + jnp.bitwise_xor(pos[YBIT], yy) * (D // 8)
                        + jnp.bitwise_xor(pos[TENSOR], k) * depth
                    )
                    target[dd, yy, k] = source[rows_at(start, depth, 8), :].astype(BF16)


ROWS_A = 256


def middle_kernel(
    pos, attn, conv, tokens, cotangent, own_out, mine_out, theirs_out, vectors,
    ffn_own, ffn_other, ffn_core_own, ffn_core_other,
    rows_out, pre_out, grad_attn, grad_conv, ffn_keep, ffn_send, out_keep, out_send, vector_grads,
    w_out, w_up, w_down, context, ffn_in, low_down, act, slope, grad_up, low_mix,
    normal, inverse, normed, total, out_grad,
):
    dp, core = pos[DP], pos[CORE]
    hidden = w_up.shape[2]
    shard = hidden // ffn_own.shape[0]
    half = GROUP_WIDTH // 2
    assemble(w_out, pos, own_out[...], mine_out[...], theirs_out[...])
    for gg, pair in ((0, (ffn_own, ffn_other)), (1, (ffn_core_own, ffn_core_other))):
        for dd in range(2):
            place = rows_at(jnp.bitwise_xor(dp, dd) * half, half)
            for k in range(ffn_own.shape[0]):
                columns = slice(k * shard, (k + 1) * shard)
                w_up[gg, place, columns] = pair[dd][k, 0]
                w_down[gg, place, columns] = pair[dd][k, 1]
    context[:, :WIDTH] = attn[...]
    context[:, WIDTH:] = conv[...]
    vector_grads[...] = jnp.zeros_like(vector_grads)
    gain_one, bias_one = vectors[0:1, :], vectors[1:2, :]
    gain_two, bias_two = vectors[2:3, :], vectors[3:4, :]
    group_of = [jnp.bitwise_xor(core, gg) * GROUP_WIDTH for gg in range(GROUPS)]

    def lanes_of(gg):
        return pl.ds(pl.multiple_of(group_of[gg], LANES), GROUP_WIDTH)

    def tile(i, carry):
        rows = rows_at(i * ROWS_A, ROWS_A)
        summed = tokens[rows, :].astype(F32) + nn(context[rows, :], w_out[...])
        normal_rows, inverse_rows = norm_stats(summed)
        normal[...] = normal_rows
        inverse[...] = inverse_rows
        normed_rows = normal_rows * gain_one + bias_one
        normed[...] = normed_rows
        ffn_in[rows, :] = normed_rows.astype(BF16)
        for gg in range(GROUPS):
            group_in = ffn_in[rows, lanes_of(gg)]

            def forward(k, carry):
                columns = pl.ds(pl.multiple_of(k * shard, LANES), shard)
                value, rate = gelu_parts(nn(group_in, w_up[gg, :, columns]))
                act[gg, rows, columns] = value.astype(BF16)
                slope[gg, :, columns] = rate
                return carry

            lax.fori_loop(0, hidden // shard, forward, 0)
            total[:, lanes_of(gg)] = normed[:, lanes_of(gg)] + nt(act[gg, rows, :], w_down[gg])
        normal_two, inverse_two = norm_stats(total[...])
        rows_out[rows, :] = (normal_two * gain_two + bias_two).astype(BF16)
        upstream = cotangent[rows, :].astype(F32)
        vector_grads[2:3, :] += jnp.sum(upstream * normal_two, axis=0, keepdims=True)
        vector_grads[3:4, :] += jnp.sum(upstream, axis=0, keepdims=True)
        grad_z = norm_back(upstream * gain_two, normal_two, inverse_two)
        total[...] = grad_z
        low_down[rows, :] = grad_z.astype(BF16)
        for gg in range(GROUPS):
            group_grad = low_down[rows, lanes_of(gg)]

            def backward(k, carry):
                columns = pl.ds(pl.multiple_of(k * shard, LANES), shard)
                grad = nn(group_grad, w_down[gg, :, columns]) * slope[gg, :, columns]
                grad_up[gg, rows, columns] = grad.astype(BF16)
                return carry

            lax.fori_loop(0, hidden // shard, backward, 0)
            total[:, lanes_of(gg)] += nt(grad_up[gg, rows, :], w_up[gg])
        grad_normed = total[...]
        vector_grads[0:1, :] += jnp.sum(grad_normed * normal[...], axis=0, keepdims=True)
        vector_grads[1:2, :] += jnp.sum(grad_normed, axis=0, keepdims=True)
        grad_pre = norm_back(grad_normed * gain_one, normal[...], inverse[...])
        pre_out[rows, :] = grad_pre
        low_mix[rows, :] = grad_pre.astype(BF16)
        grad_attn[rows, :] = nt(low_mix[rows, :], w_out[:WIDTH, :]).astype(BF16)
        grad_conv[rows, :] = nt(low_mix[rows, :], w_out[WIDTH:, :]).astype(BF16)
        return carry

    lax.fori_loop(0, tokens.shape[0] // ROWS_A, tile, 0)

    for gg, target in ((0, ffn_keep), (1, ffn_send)):

        def weights(k, carry):
            columns = pl.ds(pl.multiple_of(k * shard, LANES), shard)
            up_grad = tn(ffn_in[:, lanes_of(gg)], grad_up[gg, :, columns]).astype(BF16)
            down_grad = tn(low_down[:, lanes_of(gg)], act[gg, :, columns]).astype(BF16)
            for d in range(2):
                dd = jnp.bitwise_xor(dp, d)
                part = slice(d * half, (d + 1) * half)
                target[dd, pos[YBIT], k] = up_grad[part]
                target[dd, 1 - pos[YBIT], k] = down_grad[part]
            return carry

        lax.fori_loop(0, hidden // shard, weights, 0)
    out_grad[...] = tn(context[...], low_mix[...])
    emit_rows(out_grad, pos, out_keep, out_send)


def conv_back_kernel(
    grad_ext, kern_ext, c_ext, mask, mixed, q, conv_key, pre_key, ext, w_tap, w_qcp, spread,
    grad_c_out, dq_out, gpk_out, tap_grad, point_grad, depth_grad,
    grad_f, c_f, ext_f, prod, acc,
):
    rows = q.shape[0]
    own = slice(HALO, HALO + rows)

    @pl.when(pl.program_id(0) == 0)
    def _():
        tap_grad[...] = jnp.zeros_like(tap_grad)
        point_grad[...] = jnp.zeros_like(point_grad)
        depth_grad[...] = jnp.zeros_like(depth_grad)

    grad_f[...] = grad_ext[...].astype(F32)
    c_f[...] = c_ext[...].astype(F32)
    ext_f[...] = ext[...].astype(F32)
    taps = jnp.zeros((rows, LANES), F32)
    for j in range(KERNEL):
        shifted = slice(HALO - RADIUS + j, HALO - RADIUS + j + rows)
        taps += nt((grad_f[own, :] * c_f[shifted, :]).astype(BF16), spread[j, :LANES, :])
    taps = taps * mask[...]
    kern = kern_ext[own, :]
    grad_logits = kern * (taps - slot_sum(kern * taps))
    high, low = split(grad_logits)
    grad_mixed = (nt(high, w_tap[...]) + nt(low, w_tap[...])).astype(BF16).astype(F32)
    tap_grad[...] += tn(mixed[...], high) + tn(mixed[...], low)
    grad_key = (grad_mixed * q[...].astype(F32)).astype(BF16)
    dq_out[...] = grad_mixed * conv_key[...]
    point_grad[...] += tn(pre_key[...], grad_key)
    gpk_out[...] = nt(grad_key, w_qcp[:, 2 * WIDTH :])

    def depth_step(i, carry):
        start = i * 64
        mask_rows = mask[rows_at(start, 64), :]
        for lane in range(0, D, 256):
            lanes = slice(lane, lane + 256)
            block = ext_f[rows_at(start + 8, 80, 8), lanes]
            gpk = gpk_out[rows_at(start, 64), lanes]
            for j in range(KERNEL):
                value = block[RADIUS + j : RADIUS + j + 64, :] * (gpk * tap_column(mask_rows, j))
                depth_grad[j : j + 1, lanes] += jnp.sum(value, axis=0, keepdims=True)
        return carry

    lax.fori_loop(0, rows // 64, depth_step, 0)
    kern_high, kern_low = split(kern_ext[...])
    both = jnp.concatenate([kern_high, kern_low], axis=1)
    for j in range(KERNEL):
        prod[...] = nn(both, spread[KERNEL - 1 - j]) * grad_f[...]
        shifted = slice(HALO - RADIUS + j, HALO - RADIUS + j + rows)
        part = prod[shifted, :] * tap_column(mask[...], j)
        if j == 0:
            acc[...] = part
        else:
            acc[...] += part
    grad_c_out[...] = acc[...].astype(BF16)


def first_grads_kernel(
    pos, tokens, dq_attn, dq_conv, grad_c, point_grad, grad_q_out, keep, send, low_q, total
):
    low_q[...] = (dq_attn[...] + dq_conv[...]).astype(BF16)
    grad_q_out[...] = low_q[...]
    total[:, :WIDTH] = tn(tokens[...], low_q[...])
    total[:, WIDTH : 2 * WIDTH] = tn(tokens[...], grad_c[...])
    total[:, 2 * WIDTH :] = point_grad[...]
    emit_rows(total, pos, keep, send)


def second_grads_kernel(pos, tokens, kept, arrived, grad_kv_out, keep, send, low_kv, total):
    low_kv[...] = (kept[...].astype(F32) + arrived[...].astype(F32)).astype(BF16)
    grad_kv_out[...] = low_kv[...]
    total[...] = tn(tokens[...], low_kv[...])
    emit_rows(total, pos, keep, send)


def input_grad_kernel(
    pre, gpk, low_edge, high_edge, mask, taps, grad_q, grad_kv, grad_c, w_kv, w_qcp, out,
    gpk_ext, base,
):
    rows = gpk.shape[0]
    gpk_ext[:HALO, :] = low_edge[...].astype(F32)
    gpk_ext[HALO : HALO + rows, :] = gpk[...]
    gpk_ext[HALO + rows :, :] = high_edge[...].astype(F32)
    base[...] = (
        nt(grad_kv[...], w_kv[...])
        + nt(grad_q[...], w_qcp[:, :WIDTH])
        + nt(grad_c[...], w_qcp[:, WIDTH : 2 * WIDTH])
    )

    def step(i, carry):
        start = i * 64
        mask_rows = mask[rows_at(start, 64), :]
        for lane in range(0, D, 256):
            lanes = slice(lane, lane + 256)
            block = gpk_ext[rows_at(start + 8, 80, 8), lanes]
            place = rows_at(start, 64)
            value = base[place, lanes] + pre[place, lanes]
            for j in range(KERNEL):
                tap = taps[KERNEL - 1 - j : KERNEL - j, lanes]
                value += block[RADIUS + j : RADIUS + j + 64, :] * tap * tap_column(mask_rows, j)
            out[place, lanes] = value.astype(BF16)
        return carry

    lax.fori_loop(0, rows // 64, step, 0)


def unpack_kernel(pos, first_own, first_other, second_own, second_other, third_own, third_other,
                  in_out, out_out, point_out):
    depth = first_own.shape[2]
    for cc in range(2):
        for yy in range(2):
            for k in range(first_own.shape[1]):
                start = (
                    jnp.bitwise_xor(pos[CORE], cc) * (D // 4)
                    + jnp.bitwise_xor(pos[YBIT], yy) * (D // 8)
                    + jnp.bitwise_xor(pos[TENSOR], k) * depth
                )
                place = rows_at(start, depth, 8)
                first = (first_own, first_other)[cc][yy, k].astype(F32)
                second = (second_own, second_other)[cc][yy, k].astype(F32)
                third = (third_own, third_other)[cc][yy, k].astype(F32)
                out_out[place, :] = first
                in_out[place, :WIDTH] = second[:, :WIDTH]
                in_out[place, 3 * WIDTH :] = second[:, WIDTH : 2 * WIDTH]
                point_out[place, :] = second[:, 2 * WIDTH :]
                in_out[place, WIDTH : 3 * WIDTH] = third


def flips(axis, bit):
    return [(i, i ^ bit) for i in range(lax.axis_size(axis))]


def swap(block, axis, bit):
    return lax.ppermute(block, axis, flips(axis, bit))


def swap_both(block, bit):
    count = lax.axis_size("ctx")
    pairs = [
        (d * count + c, (1 - d) * count + (c ^ bit)) for d in range(2) for c in range(count)
    ]
    return lax.ppermute(block, ("dp", "ctx"), pairs)


def add_low(*blocks):
    return sum(b.astype(F32) for b in blocks).astype(BF16)


def far_bits():
    bits, bit = [], 4
    while bit < lax.axis_size("ctx"):
        bits.append(bit)
        bit *= 2
    return bits


def reduce_shares(keep, send):
    arrived = swap(send, "ctx", 1)
    part = {(d, y): add_low(keep[d, y], arrived[d, y]) for d in range(2) for y in range(2)}
    from_y = swap(part[0, 1], "ctx", 2)
    from_x = swap(part[1, 0], "dp", 1)
    from_xy = swap_both(part[1, 1], 2)
    count = keep.shape[2]
    slices = [
        add_low(part[0, 0][k], from_y[k], from_x[k], from_xy[k]) for k in range(count)
    ]
    share = add_low(slices[0], *[swap(slices[k], "tensor", k) for k in range(1, count)])
    for bit in far_bits():
        share = add_low(share, swap(share, "ctx", bit))
    return share


def gather_shares(share):
    count = lax.axis_size("tensor")
    stacked = jnp.stack([share] + [swap(share, "tensor", k) for k in range(1, count)])
    own = jnp.stack([stacked, swap(stacked, "ctx", 2)])
    return own, swap(own, "ctx", 1)


def neighbours(block):
    count = lax.axis_size("ctx")
    up = [(i, i + 1) for i in range(count - 1)]
    down = [(i + 1, i) for i in range(count - 1)]
    rows = block.shape[1]
    low = lax.ppermute(block[:, rows - HALO :], "ctx", up)
    high = lax.ppermute(block[:, :HALO], "ctx", down)
    return low, high


def with_edges(block, edges):
    return jnp.concatenate([edges[0], block, edges[1]], axis=1)


def ordered(own, other, high):
    return jnp.where(high, other, own), jnp.where(high, own, other)


def gather_kv(block):
    count, bit, depth = lax.axis_size("ctx"), lax.axis_size("ctx") // 2, 1
    index = lax.axis_index("ctx")
    micro, rows, width = block.shape
    while bit:
        other = swap(block, "ctx", bit)
        block = jnp.stack(ordered(block, other, (index // bit) % 2 == 1), axis=depth)
        depth += 1
        bit //= 2
    return block.reshape(micro, count * rows, width)


def body(
    hidden, segment_ids, w_in, w_depth, w_point, w_kernel, w_out,
    norm1_gain, norm1_bias, norm2_gain, norm2_bias, w_up, w_down, out_grad,
):
    micro, rows = MICRO, hidden.shape[2]
    seq = segment_ids.shape[2]
    flat = micro * rows
    ctx_count = lax.axis_size("ctx")
    tensor_count = lax.axis_size("tensor")
    dp, ctx, tensor = lax.axis_index("dp"), lax.axis_index("ctx"), lax.axis_index("tensor")
    core = ctx % 2
    pos = jnp.stack([dp, core, (ctx // 2) % 2, tensor, ctx]).astype(jnp.int32)
    tokens = hidden[:, 0]
    tokens_flat = tokens.reshape(flat, D)
    cotangent = out_grad[:, 0].reshape(flat, D)
    ids = segment_ids[:, 0]
    half = w_in.shape[0]
    part = half // 2
    depth_rows = D // 8 // tensor_count

    def part_of(weight):
        return lax.dynamic_slice_in_dim(weight, core * part, part, axis=0)

    kv_mine = swap(part_of(w_in[:, WIDTH : 3 * WIDTH]), "dp", 1)
    edges = neighbours(tokens)
    qcp_mine = swap(
        part_of(jnp.concatenate([w_in[:, :WIDTH], w_in[:, 3 * WIDTH :], w_point], axis=1)), "dp", 1
    )
    kv_theirs = swap(kv_mine, "ctx", 1)
    vectors = jnp.stack([norm1_gain, norm1_bias, norm2_gain, norm2_bias], axis=0)
    small = jnp.concatenate([w_depth.T, vectors], axis=0)
    small = jnp.pad(small, ((0, 16 - small.shape[0]), (0, 0)))
    tap_half = w_kernel.reshape(-1, HEADS, KERNEL).transpose(0, 2, 1)
    tap_half = jnp.pad(tap_half, ((0, 0), (0, 0), (0, SLOT - HEADS))).reshape(-1, SLOT * KERNEL)
    tap_half = jnp.pad(tap_half, ((0, 0), (0, LANES - SLOT * KERNEL)))
    small = jnp.concatenate(ordered(small, swap(small, "dp", 1), dp == 1), axis=1).astype(F32)
    w_tap = jnp.concatenate(ordered(tap_half, swap(tap_half, "dp", 1), dp == 1), axis=0)
    taps = jnp.pad(small[:KERNEL], ((0, 16 - KERNEL), (0, 0)))
    vectors = jnp.pad(small[KERNEL : KERNEL + 4], ((0, 4), (0, 0)))
    qcp_theirs = swap(qcp_mine, "ctx", 1)

    group = jnp.where(core == 1, jnp.stack([w_up[:, 1], w_down[:, 1]]), jnp.stack([w_up[:, 0], w_down[:, 0]]))
    ffn_own = jnp.stack([group] + [swap(group, "tensor", k) for k in range(1, tensor_count)])
    out_mine = swap(part_of(w_out), "dp", 1)
    out_theirs = swap(out_mine, "ctx", 1)
    ffn_other = swap(ffn_own, "dp", 1)
    ffn_core_own = swap(ffn_own, "ctx", 1)
    ffn_core_other = swap(ffn_other, "ctx", 1)

    offset = ctx * rows
    own_ids = lax.dynamic_slice_in_dim(ids, offset, rows, axis=1)
    window = lax.dynamic_slice_in_dim(
        jnp.pad(ids, ((0, 0), (RADIUS, RADIUS)), constant_values=-1), offset, rows + 2 * RADIUS, axis=1
    )
    mask = jnp.stack([window[:, j : j + rows] == own_ids for j in range(KERNEL)], axis=2)
    mask = jnp.broadcast_to(mask[..., None], mask.shape + (SLOT,)).reshape(micro, rows, SLOT * KERNEL)
    mask = jnp.pad(mask.astype(F32), ((0, 0), (0, 0), (0, LANES - SLOT * KERNEL)))
    blocks = ids.reshape(micro, ctx_count, rows)
    first = jnp.sum((blocks[:, :, -1] < own_ids[:, :1]).astype(jnp.int32), axis=1)
    last = jnp.sum((blocks[:, :, 0] <= own_ids[:, -1:]).astype(jnp.int32), axis=1)
    bounds = jnp.stack([first, last])
    key_ids = ids[:, :, None]
    query_ids = own_ids[:, None, :]
    lane_id = lax.broadcasted_iota(jnp.int32, (KERNEL, 2 * LANES, WIDTH), 1) % LANES
    head_id = lax.broadcasted_iota(jnp.int32, (KERNEL, 2 * LANES, WIDTH), 2) // HEAD_DIM
    tap_id = lax.broadcasted_iota(jnp.int32, (KERNEL, 2 * LANES, WIDTH), 0)
    spread = (lane_id == SLOT * tap_id + head_id).astype(BF16)

    kv_rows, w_kv = run(
        kv_kernel,
        [shaped((flat, 2 * WIDTH), BF16), shaped((D, 2 * WIDTH), BF16)],
        [pos, tokens_flat, w_in, kv_mine, kv_theirs],
        scratch=[pltpu.SMEM((1,), jnp.int32)],
        flops=2 * flat * D * 2 * WIDTH,
        name="kv",
    )
    kv = gather_kv(kv_rows.reshape(micro, rows, 2 * WIDTH))

    depth = {"pipeline_mode": pl.Buffered(1)} if seq > 2048 else {}

    def long_block(shape, index):
        return pl.BlockSpec(shape, index, **depth)

    seq_kv = long_block((None, seq, 2 * WIDTH), lambda m: (m, 0, 0))
    seq_ids = long_block((None, seq, 1), lambda m: (m, 0, 0))
    span = rows + 2 * HALO
    ext = with_edges(tokens, edges)
    once = whole
    q, c_ext, pre_key, conv_key, mixed, kern, conv_out, w_qcp = run(
        conv_kernel,
        [
            shaped((micro, rows, WIDTH), BF16), shaped((micro, span, WIDTH), BF16),
            shaped((micro, rows, D), BF16), shaped((micro, rows, WIDTH), F32),
            shaped((micro, rows, WIDTH), BF16), shaped((micro, rows, LANES), F32),
            shaped((micro, rows, WIDTH), BF16), shaped((D, 3 * WIDTH), BF16),
        ],
        [pos, ext, mask, w_in, w_point, qcp_mine, qcp_theirs, taps, w_tap, spread],
        specs=[SCALARS, per_micro((span, D)), per_micro((rows, LANES)), once(w_in.shape), once(w_point.shape),
               once(qcp_mine.shape), once(qcp_theirs.shape), once(taps.shape), once(w_tap.shape), once(spread.shape)],
        out_specs=[per_micro((rows, WIDTH)), per_micro((span, WIDTH)), per_micro((rows, D)), per_micro((rows, WIDTH)),
                   per_micro((rows, WIDTH)), per_micro((rows, LANES)), per_micro((rows, WIDTH)), once((D, 3 * WIDTH))],
        grid=(micro,),
        scratch=[pltpu.VMEM((span, D), F32), pltpu.VMEM((span, WIDTH), F32), pltpu.VMEM((rows, WIDTH), F32)],
        flops=2 * flat * WIDTH * (3 * D + 256 * KERNEL),
        name="conv",
    )
    kern_edges = neighbours(kern)

    head_scratch = pltpu.VMEM((HEADS, LANES, rows), BF16)
    lane_scratch = pltpu.VMEM((HEADS, rows, LANES), BF16)
    row_scratch = pltpu.VMEM((8, rows), F32)
    context, attn_t, lse = run(
        attend_kernel,
        [shaped((micro, rows, WIDTH), BF16), shaped((micro, WIDTH, rows), F32), shaped((micro, 8, rows), F32)],
        [bounds, q, kv, key_ids, query_ids],
        specs=[SCALARS, per_micro((rows, WIDTH)), seq_kv, seq_ids, per_micro((1, rows))],
        out_specs=[per_micro((rows, WIDTH)), per_micro((WIDTH, rows)), per_micro((8, rows))],
        grid=(micro,),
        scratch=[head_scratch, row_scratch, row_scratch, pltpu.VMEM((WIDTH, rows), F32)],
        flops=16 * flat * 4 * rows * WIDTH,
        name="attend",
    )

    hidden_units = tensor_count * w_up.shape[2]
    shard = w_up.shape[2]
    ffn_share = (2, 2, tensor_count, GROUP_WIDTH // 2, shard)

    def share(columns):
        return (2, 2, tensor_count, depth_rows, columns)

    rows_out, grad_pre, grad_attn, grad_conv, ffn_keep, ffn_send, out_keep, out_send, vector_grads = run(
        middle_kernel,
        [
            shaped((flat, D), BF16), shaped((flat, D), F32), shaped((flat, WIDTH), BF16), shaped((flat, WIDTH), BF16),
            shaped(ffn_share, BF16), shaped(ffn_share, BF16), shaped(share(D), BF16), shaped(share(D), BF16),
            shaped((8, D), F32),
        ],
        [pos, context.reshape(flat, WIDTH), conv_out.reshape(flat, WIDTH), tokens_flat, cotangent,
         w_out, out_mine, out_theirs, vectors, ffn_own, ffn_other, ffn_core_own, ffn_core_other],
        scratch=[
            pltpu.VMEM((D, D), BF16),
            pltpu.VMEM((GROUPS, GROUP_WIDTH, hidden_units), BF16),
            pltpu.VMEM((GROUPS, GROUP_WIDTH, hidden_units), BF16),
            pltpu.VMEM((flat, D), BF16), pltpu.VMEM((flat, D), BF16), pltpu.VMEM((flat, D), BF16),
            pltpu.VMEM((GROUPS, flat, hidden_units), BF16),
            pltpu.VMEM((GROUPS, ROWS_A, hidden_units), F32),
            pltpu.VMEM((GROUPS, flat, hidden_units), BF16),
            pltpu.VMEM((flat, D), BF16),
            pltpu.VMEM((ROWS_A, D), F32), pltpu.VMEM((ROWS_A, 1), F32),
            pltpu.VMEM((ROWS_A, D), F32), pltpu.VMEM((ROWS_A, D), F32), pltpu.VMEM((D, D), F32),
        ],
        flops=2 * flat * D * (3 * D + 3 * hidden_units),
        name="middle",
    )

    grad_attn = grad_attn.reshape(micro, rows, WIDTH)
    grad_conv = grad_conv.reshape(micro, rows, WIDTH)
    grad_ext = with_edges(grad_conv, neighbours(grad_conv))
    kern_ext = with_edges(kern, kern_edges)

    dq_attn, kv_grad = run(
        attend_back_kernel,
        [shaped((micro, rows, WIDTH), F32), shaped((2, ctx_count // 2, micro, rows, 2 * WIDTH), BF16)],
        [bounds, pos, q, grad_attn, kv, key_ids, query_ids, lse, attn_t],
        specs=[SCALARS, SCALARS, per_micro((rows, WIDTH)), per_micro((rows, WIDTH)), seq_kv,
               seq_ids, per_micro((1, rows)), per_micro((8, rows)), per_micro((WIDTH, rows))],
        out_specs=[per_micro((rows, WIDTH)),
                   long_block((2, ctx_count // 2, None, rows, 2 * WIDTH), lambda m: (0, 0, m, 0, 0))],
        grid=(micro,),
        scratch=[head_scratch, head_scratch, lane_scratch, lane_scratch, row_scratch, pltpu.VMEM((WIDTH, rows), F32)],
        flops=40 * flat * 4 * rows * WIDTH,
        name="attend_back",
    )
    arrived = swap(kv_grad[1], "ctx", 1)
    kv_parts = [add_low(kv_grad[0, k], arrived[k]) for k in range(ctx_count // 2)]
    bit = 2
    while len(kv_parts) > 2:
        received = swap(jnp.stack(kv_parts[1::2]), "ctx", bit)
        kv_parts = [add_low(a, received[k]) for k, a in enumerate(kv_parts[0::2])]
        bit *= 2
    kv_arrived = swap(kv_parts[1], "ctx", bit)

    grad_c, dq_conv, gpk, tap_grad, point_grad, depth_grad = run(
        conv_back_kernel,
        [
            shaped((micro, rows, WIDTH), BF16), shaped((micro, rows, WIDTH), F32), shaped((micro, rows, D), F32),
            shaped((WIDTH, LANES), F32), shaped((D, WIDTH), F32), shaped((16, D), F32),
        ],
        [grad_ext, kern_ext, c_ext, mask, mixed, q, conv_key, pre_key, ext, w_tap, w_qcp, spread],
        specs=[per_micro((span, WIDTH)), per_micro((span, LANES)), per_micro((span, WIDTH)), per_micro((rows, LANES)),
               per_micro((rows, WIDTH)), per_micro((rows, WIDTH)), per_micro((rows, WIDTH)), per_micro((rows, D)),
               per_micro((span, D)), once(w_tap.shape), once(w_qcp.shape), once(spread.shape)],
        out_specs=[per_micro((rows, WIDTH)), per_micro((rows, WIDTH)), per_micro((rows, D)),
                   once((WIDTH, LANES)), once((D, WIDTH)), once((16, D))],
        grid=(micro,),
        scratch=[pltpu.VMEM((span, WIDTH), F32), pltpu.VMEM((span, WIDTH), F32), pltpu.VMEM((span, D), F32),
                 pltpu.VMEM((span, WIDTH), F32), pltpu.VMEM((rows, WIDTH), F32)],
        flops=2 * flat * WIDTH * (3 * D + 512 * KERNEL),
        name="conv_back",
    )
    gpk_edges = neighbours(gpk.astype(BF16))

    wide = 3 * WIDTH
    grad_q, first_keep, first_send = run(
        first_grads_kernel,
        [shaped((flat, WIDTH), BF16), shaped(share(wide), BF16), shaped(share(wide), BF16)],
        [pos, tokens_flat, dq_attn.reshape(flat, WIDTH), dq_conv.reshape(flat, WIDTH),
         grad_c.reshape(flat, WIDTH), point_grad],
        scratch=[pltpu.VMEM((flat, WIDTH), BF16), pltpu.VMEM((D, wide), F32)],
        flops=2 * flat * D * 2 * WIDTH,
        name="first_grads",
    )
    grad_kv, second_keep, second_send = run(
        second_grads_kernel,
        [shaped((flat, 2 * WIDTH), BF16), shaped(share(2 * WIDTH), BF16), shaped(share(2 * WIDTH), BF16)],
        [pos, tokens_flat, kv_parts[0].reshape(flat, 2 * WIDTH), kv_arrived.reshape(flat, 2 * WIDTH)],
        scratch=[pltpu.VMEM((flat, 2 * WIDTH), BF16), pltpu.VMEM((D, 2 * WIDTH), F32)],
        flops=2 * flat * D * 2 * WIDTH,
        name="second_grads",
    )
    (input_grad,) = run(
        input_grad_kernel,
        [shaped((micro, rows, D), BF16)],
        [grad_pre.reshape(micro, rows, D), gpk, gpk_edges[0], gpk_edges[1], mask, taps,
         grad_q.reshape(micro, rows, WIDTH), grad_kv.reshape(micro, rows, 2 * WIDTH), grad_c, w_kv, w_qcp],
        specs=[per_micro((rows, D)), per_micro((rows, D)), per_micro((HALO, D)), per_micro((HALO, D)),
               per_micro((rows, LANES)), once(taps.shape), per_micro((rows, WIDTH)), per_micro((rows, 2 * WIDTH)),
               per_micro((rows, WIDTH)), once(w_kv.shape), once(w_qcp.shape)],
        out_specs=[per_micro((rows, D))],
        grid=(micro,),
        scratch=[pltpu.VMEM((span, D), F32), pltpu.VMEM((rows, D), F32)],
        flops=2 * flat * D * 4 * WIDTH,
        name="input_grad",
    )

    ffn_piece = reduce_shares(ffn_keep, ffn_send)
    ffn_pair = jnp.stack([ffn_piece, swap(ffn_piece, "ctx", 2)])
    ffn_far = swap(ffn_pair, "ctx", 1)
    on_y, on_core = (ctx // 2) % 2 == 1, core == 1
    groups = ordered(ffn_pair, ffn_far, on_core)
    up_parts, down_parts = zip(*[ordered(g[0], g[1], on_y) for g in groups])
    up_grad = jnp.stack(up_parts, axis=1).astype(F32)
    down_grad = jnp.stack(down_parts, axis=1).astype(F32)

    out_shares = gather_shares(reduce_shares(out_keep, out_send))
    first_shares = gather_shares(reduce_shares(first_keep, first_send))
    second_shares = gather_shares(reduce_shares(second_keep, second_send))
    in_grad, w_out_grad, w_point_grad = run(
        unpack_kernel,
        [shaped((half, 4 * WIDTH), F32), shaped((half, D), F32), shaped((half, WIDTH), F32)],
        [pos, *out_shares, *first_shares, *second_shares],
        name="unpack",
    )

    vector_half = D // 2
    packed = jnp.concatenate([depth_grad[:KERNEL], vector_grads[:4]], axis=0)
    packed = jnp.pad(packed, ((0, 16 - packed.shape[0]), (0, 0)))
    packed = jnp.concatenate(
        [packed.reshape(16, 2, vector_half).transpose(1, 0, 2).reshape(2, -1, LANES), tap_grad.reshape(2, -1, LANES)],
        axis=1,
    )
    sent = lax.dynamic_index_in_dim(packed, 1 - dp, 0, keepdims=False)
    packed = lax.dynamic_index_in_dim(packed, dp, 0, keepdims=False) + swap(sent, "dp", 1)
    bit = 1
    while bit < ctx_count:
        packed = packed + swap(packed, "ctx", bit)
        bit *= 2
    bit = 1
    while bit < tensor_count:
        packed = packed + swap(packed, "tensor", bit)
        bit *= 2
    rows_small = 16 * vector_half // LANES
    rest = packed[:rows_small].reshape(16, vector_half)
    tap_sum = packed[rows_small:][:, : SLOT * KERNEL].reshape(-1, KERNEL, SLOT)[:, :, :HEADS]
    tap_sum = tap_sum.transpose(0, 2, 1).reshape(-1, HEADS * KERNEL)

    return (
        rows_out.reshape(micro, 1, rows, D),
        input_grad[:, None],
        in_grad,
        rest[:KERNEL].T,
        w_point_grad,
        tap_sum,
        w_out_grad,
        rest[KERNEL],
        rest[KERNEL + 1],
        rest[KERNEL + 2],
        rest[KERNEL + 3],
        up_grad,
        down_grad,
    )


def solution(mesh):
    return jax.shard_map(
        body,
        mesh=mesh,
        in_specs=(
            P(None, ("dp", "tensor"), "ctx", None),
            P(None, ("dp", "tensor"), None),
            P("dp", None),
            P("dp", None),
            P("dp", None),
            P("dp", None),
            P("dp", None),
            P("dp"),
            P("dp"),
            P("dp"),
            P("dp"),
            P("dp", None, "tensor"),
            P("dp", None, "tensor"),
            P(None, ("dp", "tensor"), "ctx", None),
        ),
        out_specs=(
            P(None, ("dp", "tensor"), "ctx", None),
            P(None, ("dp", "tensor"), "ctx", None),
            P("dp", None),
            P("dp", None),
            P("dp", None),
            P("dp", None),
            P("dp", None),
            P("dp"),
            P("dp"),
            P("dp"),
            P("dp"),
            P("dp", None, "tensor"),
            P("dp", None, "tensor"),
        ),
        check_vma=False,
    )
```

time: 942 us -> 368 us (0.39)
  blocking collectives: 293 us -> 0 us
  waiting for transfers between devices: 249 us -> 74.9 us
  matrix products: 111 us -> 0 us
  Pallas kernels: 0 us -> 109 us
  local copies, waits for them, and re-layouts: 138 us -> 38.3 us
  starting transfers between devices: 20.5 us -> 107 us
  other arithmetic: 92.3 us -> 30.1 us
  between operations: 24.9 us -> 2.16 us
    psum x1 -> x0, blocking collectives: 183 us -> none  [body(): lax.psum((split_grads[0], split_grads[1], split_grads[2], split_grads[3],...]
    psum x1 -> x0, waiting for transfers between devices: 115 us -> none  [body(): lax.psum((split_grads[0], split_grads[1], split_grads[2], split_grads[3],...]
    dot_general x54 -> x0, matrix products: 111 us -> none  [the longest x6 17.8 us: times_transposed(): lax.dot_general(left, right, (((1,), (1,)), ((), ())), preferred_element_...]
    pallas_call x0 -> x10, Pallas kernels: none -> 109 us  [run(): pl.pallas_call(kernel, out_shape=tuple(outs), in_specs=specs, out_specs=t...]
    all_gather x13 -> x0, blocking collectives: 105 us -> none  [the longest x2 19.5 us: body(): lax.all_gather(key_rows, 'ctx', axis=0, tiled=True)]
    ppermute x8 -> x76, starting transfers between devices: 19.3 us -> 107 us  [the longest x64 87.3 us: swap(): return lax.ppermute(block, axis, flips(axis, bit))]
    reduce_scatter x4 -> x0, waiting for transfers between devices: 82.8 us -> none  [the longest x2 41.5 us: body(): lax.psum_scatter(all_kv_grads.astype(jnp.bfloat16), 'ctx', scatter_dimens...]
    ppermute x8 -> x76, waiting for transfers between devices: 0.02 us -> 74.9 us  [the longest x64 58.5 us: swap(): return lax.ppermute(block, axis, flips(axis, bit))]
  transfers between devices with their start and end apart: 21 -> 76, of which waited for: 8 -> 21; matrix products, arithmetic and copies ran while one was open for 30% -> 15% of each run, Pallas kernels for 0% -> 25%
where the time goes in v2:
time: 368 us; the launch traced here: 361 us
  Pallas kernels  109 us (30%)
  starting transfers between devices  107 us (29%)
  waiting for transfers between devices  74.9 us (20%)
  local copies, waits for them, and re-layouts  38.3 us (10%)
  other arithmetic  30.1 us (8%)
    pallas_call x10, Pallas kernels, run(): pl.pallas_call(kernel, out_shape=tuple(outs), in_specs=specs, out_specs=t...  109 us
    ppermute x64, starting transfers between devices, swap(): return lax.ppermute(block, axis, flips(axis, bit))  87.3 us
    ppermute x64, waiting for transfers between devices, swap(): return lax.ppermute(block, axis, flips(axis, bit))  58.5 us
    ppermute x4, waiting for transfers between devices, swap_both(): return lax.ppermute(block, ('dp', 'ctx'), pairs)  12.3 us
    unnamed x87, local copies, waits for them, and re-layouts  9.87 us
    ppermute x4, starting transfers between devices, neighbours(): low = lax.ppermute(block[:, rows - HALO:], 'ctx', up)  9.48 us
    convert_element_type x10, other arithmetic, add_low(): return sum((b.astype(F32) for b in blocks)).astype(BF16)  7.92 us
  transfers between devices with their start and end apart: 76, of which 21 were waited for; matrix products, arithmetic and copies ran while one was open for 15% of the time, Pallas kernels for 25%

profile of v2, /device:TPU:0, one launch (start us, length us, event | category | flops | bytes accessed | tf_op | source)
XLA Modules:
  0.0 361.1 jit_solution(3050966243612248027)
XLA Ops:
  3.0 3.1 collective-permute-start.12
  16.6 2.9 collective-permute-done.6.mine
  21.8 4.0 %kv.1 = (bf16[512,768]{1,0:T(8,128)(2,1)}, bf16[768,768]{1,0:T(8,128)(2,1)}) custom-call(s32[5]{0:T(128)} %stack.214.pos, bf16[512,768]{1,0:T(8,128)(2,1)} %bitcast.333, bf16[384,1536]{1,0:T(8,128)(2,1)} %own.1, bf16[192,768]{1,0:T(8,128)(2,1)} %copy-done.21, bf16[192,768]{1,0:T(8,128)(2,1)} %copy-done.22), custom_call_target="tpu_custom_call" | custom-call | flops 603979776 | bytes 4522004 | tf_op jit(solution)/shard_map/kv/pallas_call | solution.py:72
  37.7 8.3 %collective-permute-done.8 = bf16[2,256,768]{2,1,0:T(8,128)(2,1)} collective-permute-done((bf16[2,256,768]{2,1,0:T(8,128)(2,1)}, bf16[2,256,768]{2,1,0:T(8,128)(2,1)}, u32[]{:S(2)}, u32[]{:S(2)}) %collective-permute-start.8) | collective-permute-done | bytes 786464 | tf_op jit(solution)/shard_map/ppermute | solution.py:557
  71.7 12.0 %conv.1 = (bf16[2,256,384]{2,1,0:T(8,128)(2,1)}, bf16[2,288,384]{2,1,0:T(8,128)(2,1)}, bf16[2,256,768]{2,1,0:T(8,128)(2,1)}, f32[2,256,384]{2,1,0:T(8,128)}, bf1...) custom-call(s32[5]{0:T(128)} %stack.214.pos, ...), custom_call_target="tpu_custom_call" | custom-call | flops 1811939328 | bytes 10649620 | tf_op jit(solution)/shard_map/conv/pallas_call | solution.py:72
  91.5 11.9 %attend.1 = (bf16[2,256,384]{2,1,0:T(8,128)(2,1)}, f32[2,384,256]{2,1,0:T(8,128)}, f32[2,8,256]{2,1,0:T(8,128)}) custom-call(s32[2,2]{1,0:T(2,128)} %pad_add_fusion.bounds, bf16[2,256,384]{2,1,0:T(8,128)(2,1)} %get-tuple-element.52.q, bf16[2,1024,768]{2,1,0:T(8,128)(2,1)} %bitcast.338, s32[2,1024,1]{2,1,0:T(8,128)} %broadcast_in_dim_squeeze.4.key_ids, ...), custom_call_target="tpu_custom_call" | custom-call | flops 3221225472 | bytes 4745232 | tf_op jit(solution)/shard_map/attend/pallas_call | solution.py:72
  104.1 31.6 %middle.1 = (bf16[512,768]{1,0:T(8,128)(2,1)}, f32[512,768]{1,0:T(8,128)}, bf16[512,384]{1,0:T(8,128)(2,1)}, bf16[512,384]{1,0:T(8,128)(2,1)}, bf16[2,2,4,192,38...) custom-call(s32[5]{0:T(128)} %stack.214.pos, ...), custom_call_target="tpu_custom_call" | custom-call | flops 5435817984 | bytes 17350676 | tf_op jit(solution)/shard_map/middle/pallas_call | solution.py:72
  136.5 3.0 collective-permute-start.18
  146.9 14.4 %conv_back.1 = (bf16[2,256,384]{2,1,0:T(8,128)(2,1)}, f32[2,256,384]{2,1,0:T(8,128)}, f32[2,256,768]{2,1,0:T(8,128)}, f32[384,128]{1,0:T(8,128)}, f32[768,384]{1,0:T(8,128)}, /*index=5*/f32[16,768]{1,0:T(8,128)}) custom-call(bf16[2,288,384]{2,1,0:T(8,128)(2,1)} %pad_maximum_fusion.4.grad_ext, f32[2,288,128]{2,1,0:T(8,128)} %pad_maximum_fusion.6.kern_ext, ...), custom_call_target="tpu_custom_call" | custom-call | flops 2717908992 | bytes 12500992 | tf_op jit(solution)/shard_map/conv_back/pallas_call | solution.py:72
  164.1 4.3 %collective-permute-done.62 = f32[240,128]{0,1:T(8,128)S(1)} collective-permute-done((f32[240,128]{0,1:T(8,128)S(1)}, f32[240,128]{0,1:T(8,128)S(1)}, u32[]{:S(2)}, u32[]{:S(2)}) %collective-permute-start.62) | collective-permute-done | bytes 122912 | tf_op jit(solution)/shard_map/ppermute | solution.py:557
  172.6 13.8 %attend_back.1 = (f32[2,256,384]{2,1,0:T(8,128)}, bf16[2,2,2,256,768]{4,3,2,1,0:T(8,128)(2,1)}) custom-call(s32[2,2]{1,0:T(2,128)} %pad_add_fusion.bounds, s32[5]{0:T(128)} %stack.214.pos, bf16[2,256,384]{2,1,0:T(8,128)(2,1)} %get-tuple-element.52.q, bf16[2,256,384]{2,1,0:T(8,128)(2,1)} %bitcast.399, bf16[2,1024,768]{2,1,0:T(8,128)(2,1)} %bitcast.339, ...), custom_call_target="tpu_custom_call" | custom-call | flops 8053063680 | bytes 8677412 | tf_op jit(solution)/shard_map/attend_back/pallas_call | solution.py:72
  186.5 3.1 collective-permute-start.65
  189.6 2.7 slice_bitcast_fusion
  193.6 3.5 collective-permute-start.24
  197.2 3.1 collective-permute-start.66
  206.2 4.6 %first_grads.1 = (bf16[512,384]{1,0:T(8,128)(2,1)}, bf16[2,2,4,24,1152]{4,3,2,1,0:T(8,128)(2,1)}, bf16[2,2,4,24,1152]{4,3,2,1,0:T(8,128)(2,1)}) custom-call(s32[5]{0:T(128)} %stack.214.pos, bf16[512,768]{1,0:T(8,128)(2,1)} %bitcast.335, f32[512,384]{1,0:T(8,128)} %bitcast.356, f32[512,384]{1,0:T(8,128)} %bitcast.355, bf16[512,384]{1,0:T(8,128)(2,1)} %bitcast.340, ...), custom_call_target="tpu_custom_call" | custom-call | flops 603979776 | bytes 6094868 | tf_op jit(solution)/shard_map/first_grads/pallas_call | solution.py:72
  213.8 3.2 collective-permute-start.32
  220.4 3.1 collective-permute-start.34
  223.6 3.2 collective-permute-start.35
  240.6 5.0 %collective-permute-done.39 = bf16[4,24,1152]{2,1,0:T(8,128)(2,1)S(1)} collective-permute-done((bf16[4,24,1152]{2,1,0:T(8,128)(2,1)S(1)}, bf16[4,24,1152]{2,1,0:T(8,128)(2,1)S(1)}, u32[]{:S(2)}, u32[]{:S(2)}) %collective-permute-start.39) | collective-permute-done | bytes 221216 | tf_op jit(solution)/shard_map/ppermute | solution.py:557
  253.5 6.6 %collective-permute-done.25 = bf16[2,256,768]{2,1,0:T(8,128)(2,1)} collective-permute-done((bf16[2,256,768]{2,1,0:T(8,128)(2,1)S(1)}, bf16[2,256,768]{2,1,0:T(8,128)(2,1)}, u32[]{:S(2)}, u32[]{:S(2)}) %collective-permute-start.25) | collective-permute-done | bytes 786464 | tf_op jit(solution)/shard_map/ppermute | solution.py:557
  261.9 3.5 second_grads.1
  272.6 11.3 %collective-permute-done.68 = bf16[4,192,384]{2,1,0:T(8,128)(2,1)S(1)} collective-permute-done((bf16[4,192,384]{2,1,0:T(8,128)(2,1)S(1)}, bf16[4,192,384]{2,1,0:T(8,128)(2,1)S(1)}, u32[]{:S(2)}, u32[]{:S(2)}) %collective-permute-start.68) | collective-permute-done | bytes 589856 | tf_op jit(solution)/shard_map/ppermute | solution.py:557
  287.5 10.7 %collective-permute-done.70 = bf16[4,192,384]{2,1,0:T(8,128)(2,1)S(1)} collective-permute-done((bf16[4,192,384]{2,1,0:T(8,128)(2,1)S(1)}, bf16[4,192,384]{2,1,0:T(8,128)(2,1)S(1)}, u32[]{:S(2)}, u32[]{:S(2)}) %collective-permute-start.70) | collective-permute-done | bytes 589856 | tf_op jit(solution)/shard_map/ppermute | solution.py:565
  298.3 2.8 collective-permute-start.53
  301.5 3.1 collective-permute-start.72
  309.0 6.8 %collective-permute-done.72 = bf16[192,384]{1,0:T(8,128)(2,1)S(1)} collective-permute-done((bf16[192,384]{1,0:T(8,128)(2,1)S(1)}, bf16[192,384]{1,0:T(8,128)(2,1)S(1)}, u32[]{:S(2)}, u32[]{:S(2)}) %collective-permute-start.72) | collective-permute-done | bytes 147488 | tf_op jit(solution)/shard_map/ppermute | solution.py:557
  321.1 3.3 collective-permute-start.47
  327.4 3.1 collective-permute-start.59
  335.4 6.1 %collective-permute-done.48 = bf16[4,24,1152]{2,1,0:T(8,128)(2,1)S(1)} collective-permute-done((bf16[4,24,1152]{2,1,0:T(8,128)(2,1)S(1)}, bf16[4,24,1152]{2,1,0:T(8,128)(2,1)S(1)}, u32[]{:S(2)}, u32[]{:S(2)}) %collective-permute-start.48) | collective-permute-done | bytes 221216 | tf_op jit(solution)/shard_map/ppermute | solution.py:557
  342.8 9.2 %input_grad.1 = bf16[2,256,768]{2,1,0:T(8,128)(2,1)} custom-call(f32[2,256,768]{2,1,0:T(8,128)} %bitcast.341, f32[2,256,768]{2,1,0:T(8,128)} %get-tuple-element.65.gpk, bf16[2,16,768]{2,1,0:T(8,128)(2,1)} %collective-permute-done.22.low_edge, bf16[2,16,768]{2,1,0:T(8,128)(2,1)} %copy-done.25, f32[2,256,128]{2,1,0:T(8,128)} %pad.33.mask, ...), custom_call_target="tpu_custom_call" | custom-call | flops 1207959552 | bytes 8863744 | tf_op jit(solution)/shard_map/input_grad/pallas_call | solution.py:72
  356.9 3.8 %unpack.1 = (f32[384,1536]{1,0:T(8,128)}, f32[384,768]{1,0:T(8,128)}, f32[384,384]{1,0:T(8,128)}) custom-call(s32[5]{0:T(128)} %stack.214.pos, bf16[2,4,24,768]{3,2,1,0:T(8,128)(2,1)} %copy-done.5, bf16[2,4,24,768]{3,2,1,0:T(8,128)(2,1)} %copy-done.18, bf16[2,4,24,1152]{3,2,1,0:T(8,128)(2,1)} %copy-done.4, bf16[2,4,24,1152]{3,2,1,0:T(8,128)(2,1)} %copy-done.14, ...), custom_call_target="tpu_custom_call" | custom-call | bytes 6193172 | tf_op jit(solution)/shard_map/unpack/pallas_call | solution.py:72
  (341 shorter events, 147.7 us)
Async XLA Ops:
  3.0 29.2 %collective-permute-start.12 = (bf16[2,192,384]{2,1,0:T(8,128)(2,1)S(1)}, bf16[2,192,384]{2,1,0:T(8,128)(2,1)S(1)}, u32[]{:S(2)}, u32[]{:S(2)}) collective-permute-start(bf16[2,192,384]{2,1,0:T(8,128)(2,1)S(1)} %maximum_select_fusion.1), channel_id=1, source_target_pairs={{0,1},{1,0},{2,3},{3,2},{4,5},{5,4},{6,7},{7,6},{8,9},{9,8},{10,11... | collective-permute-start | bytes 884744 | tf_op jit(solution)/shard_map/ppermute | solution.py:557
  6.1 27.6 %collective-permute-start.13 = (bf16[2,192,384]{2,1,0:T(8,128)(2,1)S(1)}, bf16[2,192,384]{2,1,0:T(8,128)(2,1)S(1)}, u32[]{:S(2)}, u32[]{:S(2)}) collective-permute-start(bf16[2,192,384]{2,1,0:T(8,128)(2,1)S(1)} %maximum_select_fusion.1), channel_id=1, source_target_pairs={{0,2},{1,3},{2,0},{3,1},{4,6},{5,7},{6,4},{7,5},{8,10},{9,11},{10,... | collective-permute-start | bytes 884744 | tf_op jit(solution)/shard_map/ppermute | solution.py:557
  8.7 25.6 %collective-permute-start.14 = (bf16[2,192,384]{2,1,0:T(8,128)(2,1)S(1)}, bf16[2,192,384]{2,1,0:T(8,128)(2,1)S(1)}, u32[]{:S(2)}, u32[]{:S(2)}) collective-permute-start(bf16[2,192,384]{2,1,0:T(8,128)(2,1)S(1)} %maximum_select_fusion.1), channel_id=1, source_target_pairs={{0,3},{1,2},{2,1},{3,0},{4,7},{5,6},{6,5},{7,4},{8,11},{9,10},{10,... | collective-permute-start | bytes 884744 | tf_op jit(solution)/shard_map/ppermute | solution.py:557
  12.0 49.6 %collective-permute-start.2 = (bf16[192,1152]{1,0:T(8,128)(2,1)}, bf16[192,1152]{1,0:T(8,128)(2,1)}, u32[]{:S(2)}, u32[]{:S(2)}) collective-permute-start(bf16[192,1152]{1,0:T(8,128)(2,1)} %fusion.7), channel_id=1, source_target_pairs={{0,16},{16,0},{1,17},{17,1},{2,18},{18,2},{3,19},{19,3},{4,20},{20... | collective-permute-start | bytes 1327112 | tf_op jit(solution)/shard_map/ppermute | solution.py:557
  25.8 20.2 %collective-permute-start.8 = (bf16[2,256,768]{2,1,0:T(8,128)(2,1)}, bf16[2,256,768]{2,1,0:T(8,128)(2,1)}, u32[]{:S(2)}, u32[]{:S(2)}) collective-permute-start(bf16[2,256,768]{2,1,0:T(8,128)(2,1)} %bitcast.357), channel_id=1, source_target_pairs={{0,8},{4,12},{8,0},{12,4},{1,9},{5,13},{9,1},{13,5},{2,10},{6,14},... | collective-permute-start | bytes 2359304 | tf_op jit(solution)/shard_map/ppermute | solution.py:557
  32.2 22.7 %collective-permute-start.4 = (bf16[16,384]{1,0:T(8,128)(2,1)}, bf16[16,384]{1,0:T(8,128)(2,1)}, u32[]{:S(2)}, u32[]{:S(2)}) collective-permute-start(bf16[16,384]{1,0:T(8,128)(2,1)} %pad.34), channel_id=1, source_target_pairs={{0,16},{16,0},{1,17},{17,1},{2,18},{18,2},{3,19},{19,3},{4,20},{20... | collective-permute-start | bytes 36872 | tf_op jit(solution)/shard_map/ppermute | solution.py:557
  33.7 26.3 %collective-permute-start.5 = (bf16[192,128]{1,0:T(8,128)(2,1)}, bf16[192,128]{1,0:T(8,128)(2,1)}, u32[]{:S(2)}, u32[]{:S(2)}) collective-permute-start(bf16[192,128]{1,0:T(8,128)(2,1)} %pad.37), channel_id=1, source_target_pairs={{0,16},{16,0},{1,17},{17,1},{2,18},{18,2},{3,19},{19,3},{4,20},{20... | collective-permute-start | bytes 147464 | tf_op jit(solution)/shard_map/ppermute | solution.py:557
  36.1 34.4 %collective-permute-start.15 = (bf16[4,2,192,384]{3,2,1,0:T(8,128)(2,1)S(1)}, bf16[4,2,192,384]{3,2,1,0:T(8,128)(2,1)}, u32[]{:S(2)}, u32[]{:S(2)}) collective-permute-start(bf16[4,2,192,384]{3,2,1,0:T(8,128)(2,1)S(1)} %pad_maximum_fusion.2.ffn_own), channel_id=1, source_target_pairs={{0,16},{16,0},{1,17},{17,1},{2,18},{18,2},{3,19},{19,3},{4,20},{20... | collective-permute-start | bytes 3538952 | tf_op jit(solution)/shard_map/ppermute | solution.py:557
  48.5 37.9 %collective-permute-start.9 = (bf16[2,2,256,768]{3,2,1,0:T(8,128)(2,1)}, bf16[2,2,256,768]{3,2,1,0:T(8,128)(2,1)}, u32[]{:S(2)}, u32[]{:S(2)}) collective-permute-start(bf16[2,2,256,768]{3,2,1,0:T(8,128)(2,1)} %pad_maximum_fusion.1), channel_id=1, source_target_pairs={{0,4},{4,0},{8,12},{12,8},{1,5},{5,1},{9,13},{13,9},{2,6},{6,2},{1... | collective-permute-start | bytes 4718600 | tf_op jit(solution)/shard_map/ppermute | solution.py:557
  67.7 35.7 %collective-permute-start.16 = (bf16[4,2,192,384]{3,2,1,0:T(8,128)(2,1)S(1)}, bf16[4,2,192,384]{3,2,1,0:T(8,128)(2,1)}, u32[]{:S(2)}, u32[]{:S(2)}) collective-permute-start(bf16[4,2,192,384]{3,2,1,0:T(8,128)(2,1)S(1)} %pad_maximum_fusion.2.ffn_own), channel_id=1, source_target_pairs={{0,4},{4,0},{8,12},{12,8},{1,5},{5,1},{9,13},{13,9},{2,6},{6,2},{1... | collective-permute-start | bytes 3538952 | tf_op jit(solution)/shard_map/ppermute | solution.py:557
  70.4 33.0 %collective-permute-start.11 = (bf16[192,768]{1,0:T(8,128)(2,1)}, bf16[192,768]{1,0:T(8,128)(2,1)S(1)}, u32[]{:S(2)}, u32[]{:S(2)}) collective-permute-start(bf16[192,768]{1,0:T(8,128)(2,1)} %collective-permute-done.10.mine_out), channel_id=1, source_target_pairs={{0,4},{4,0},{8,12},{12,8},{1,5},{5,1},{9,13},{13,9},{2,6},{6,2},{1... | collective-permute-start | bytes 884744 | tf_op jit(solution)/shard_map/ppermute | solution.py:557
  70.5 32.9 %collective-permute-start.17 = (bf16[4,2,192,384]{3,2,1,0:T(8,128)(2,1)}, bf16[4,2,192,384]{3,2,1,0:T(8,128)(2,1)}, u32[]{:S(2)}, u32[]{:S(2)}) collective-permute-start(bf16[4,2,192,384]{3,2,1,0:T(8,128)(2,1)} %collective-permute-done.15.ffn_other), channel_id=1, source_target_pairs={{0,4},{4,0},{8,12},{12,8},{1,5},{5,1},{9,13},{13,9},{2,6},{6,2},{1... | collective-permute-start | bytes 3538952 | tf_op jit(solution)/shard_map/ppermute | solution.py:557
  84.5 56.5 %collective-permute-start.20 = (f32[2,16,128]{2,1,0:T(8,128)S(1)}, f32[2,16,128]{2,1,0:T(8,128)S(1)}, u32[]{:S(2)}, u32[]{:S(2)}) collective-permute-start(f32[2,16,128]{2,1,0:T(8,128)S(1)} %get-tuple-element.190), channel_id=1, source_target_pairs={{0,4},{4,8},{8,12},{1,5},{5,9},{9,13},{2,6},{6,10},{10,14},{3,7},{... | collective-permute-start | bytes 49160 | tf_op jit(solution)/shard_map/ppermute | solution.py:608
  86.4 54.6 %collective-permute-start.21 = (f32[2,16,128]{2,1,0:T(8,128)S(1)}, f32[2,16,128]{2,1,0:T(8,128)S(1)}, u32[]{:S(2)}, u32[]{:S(2)}) collective-permute-start(f32[2,16,128]{2,1,0:T(8,128)S(1)} %get-tuple-element.191), channel_id=1, source_target_pairs={{4,0},{8,4},{12,8},{5,1},{9,5},{13,9},{6,2},{10,6},{14,10},{7,3},{... | collective-permute-start | bytes 49160 | tf_op jit(solution)/shard_map/ppermute | solution.py:609
  169.9 30.4 %collective-permute-start.26 = (bf16[2,2,4,24,768]{4,3,2,1,0:T(8,128)(2,1)S(1)}, bf16[2,2,4,24,768]{4,3,2,1,0:T(8,128)(2,1)S(1)}, u32[]{:S(2)}, u32[]{:S(2)}) collective-permute-start(bf16[2,2,4,24,768]{4,3,2,1,0:T(8,128)(2,1)S(1)} %copy-done.37), channel_id=1, source_target_pairs={{0,4},{4,0},{8,12},{12,8},{1,5},{5,1},{9,13},{13,9},{2,6},{6,2},{1... | collective-permute-start | bytes 1769480 | tf_op jit(solution)/shard_map/ppermute | solution.py:557
  170.9 15.5 %collective-permute-start.64 = (f32[240,128]{0,1:T(8,128)S(1)}, f32[240,128]{0,1:T(8,128)S(1)}, u32[]{:S(2)}, u32[]{:S(2)}) collective-permute-start(f32[240,128]{0,1:T(8,128)S(1)} %add.488), channel_id=1, source_target_pairs={{0,8},{4,12},{8,0},{12,4},{1,9},{5,13},{9,1},{13,5},{2,10},{6,14},... | collective-permute-start | bytes 368648 | tf_op jit(solution)/shard_map/ppermute | solution.py:557
  193.6 43.6 %collective-permute-start.24 = (bf16[2,2,256,768]{3,2,1,0:T(8,128)(2,1)}, bf16[2,2,256,768]{3,2,1,0:T(8,128)(2,1)}, u32[]{:S(2)}, u32[]{:S(2)}) collective-permute-start(bf16[2,2,256,768]{3,2,1,0:T(8,128)(2,1)} %slice_bitcast_fusion), channel_id=1, source_target_pairs={{0,4},{4,0},{8,12},{12,8},{1,5},{5,1},{9,13},{13,9},{2,6},{6,2},{1... | collective-permute-start | bytes 4718600 | tf_op jit(solution)/shard_map/ppermute | solution.py:557
  210.9 20.7 %collective-permute-start.38 = (bf16[2,2,4,24,1152]{4,3,2,1,0:T(8,128)(2,1)}, bf16[2,2,4,24,1152]{4,3,2,1,0:T(8,128)(2,1)S(1)}, u32[]{:S(2)}, u32[]{:S(2)}) collective-permute-start(bf16[2,2,4,24,1152]{4,3,2,1,0:T(8,128)(2,1)} %get-tuple-element.80), channel_id=1, source_target_pairs={{0,4},{4,0},{8,12},{12,8},{1,5},{5,1},{9,13},{13,9},{2,6},{6,2},{1... | collective-permute-start | bytes 2654216 | tf_op jit(solution)/shard_map/ppermute | solution.py:557
  217.1 48.3 %collective-permute-start.67 = (bf16[2,2,4,192,384]{4,3,2,1,0:T(8,128)(2,1)}, bf16[2,2,4,192,384]{4,3,2,1,0:T(8,128)(2,1)}, u32[]{:S(2)}, u32[]{:S(2)}) collective-permute-start(bf16[2,2,4,192,384]{4,3,2,1,0:T(8,128)(2,1)} %get-tuple-element.90), channel_id=1, source_target_pairs={{0,4},{4,0},{8,12},{12,8},{1,5},{5,1},{9,13},{13,9},{2,6},{6,2},{1... | collective-permute-start | bytes 7077896 | tf_op jit(solution)/shard_map/ppermute | solution.py:557
  239.0 21.1 %collective-permute-start.25 = (bf16[2,256,768]{2,1,0:T(8,128)(2,1)S(1)}, bf16[2,256,768]{2,1,0:T(8,128)(2,1)}, u32[]{:S(2)}, u32[]{:S(2)}) collective-permute-start(bf16[2,256,768]{2,1,0:T(8,128)(2,1)S(1)} %fusion.1), channel_id=1, source_target_pairs={{0,8},{4,12},{8,0},{12,4},{1,9},{5,13},{9,1},{13,5},{2,10},{6,14},... | collective-permute-start | bytes 2359304 | tf_op jit(solution)/shard_map/ppermute | solution.py:557
  245.6 95.9 %collective-permute-start.22 = (bf16[2,16,768]{2,1,0:T(8,128)(2,1)}, bf16[2,16,768]{2,1,0:T(8,128)(2,1)}, u32[]{:S(2)}, u32[]{:S(2)}) collective-permute-start(bf16[2,16,768]{2,1,0:T(8,128)(2,1)} %get-tuple-element.161), channel_id=1, source_target_pairs={{0,4},{4,8},{8,12},{1,5},{5,9},{9,13},{2,6},{6,10},{10,14},{3,7},{... | collective-permute-start | bytes 147464 | tf_op jit(solution)/shard_map/ppermute | solution.py:608
  248.5 19.3 %collective-permute-start.42 = (bf16[24,1152]{1,0:T(8,128)(2,1)}, bf16[24,1152]{1,0:T(8,128)(2,1)}, u32[]{:S(2)}, u32[]{:S(2)}) collective-permute-start(bf16[24,1152]{1,0:T(8,128)(2,1)} %get-tuple-element.157), channel_id=1, source_target_pairs={{0,1},{1,0},{2,3},{3,2},{4,5},{5,4},{6,7},{7,6},{8,9},{9,8},{10,11... | collective-permute-start | bytes 165896 | tf_op jit(solution)/shard_map/ppermute | solution.py:557
  248.5 21.4 %collective-permute-start.43 = (bf16[24,1152]{1,0:T(8,128)(2,1)}, bf16[24,1152]{1,0:T(8,128)(2,1)}, u32[]{:S(2)}, u32[]{:S(2)}) collective-permute-start(bf16[24,1152]{1,0:T(8,128)(2,1)} %get-tuple-element.159), channel_id=1, source_target_pairs={{0,2},{1,3},{2,0},{3,1},{4,6},{5,7},{6,4},{7,5},{8,10},{9,11},{10,... | collective-permute-start | bytes 165896 | tf_op jit(solution)/shard_map/ppermute | solution.py:557
  267.8 16.1 %collective-permute-start.68 = (bf16[4,192,384]{2,1,0:T(8,128)(2,1)S(1)}, bf16[4,192,384]{2,1,0:T(8,128)(2,1)S(1)}, u32[]{:S(2)}, u32[]{:S(2)}) collective-permute-start(bf16[4,192,384]{2,1,0:T(8,128)(2,1)S(1)} %get-tuple-element.135), channel_id=1, source_target_pairs={{0,8},{4,12},{8,0},{12,4},{1,9},{5,13},{9,1},{13,5},{2,10},{6,14},... | collective-permute-start | bytes 1769480 | tf_op jit(solution)/shard_map/ppermute | solution.py:557
  269.9 16.2 %collective-permute-start.69 = (bf16[4,192,384]{2,1,0:T(8,128)(2,1)S(1)}, bf16[4,192,384]{2,1,0:T(8,128)(2,1)S(1)}, u32[]{:S(2)}, u32[]{:S(2)}) collective-permute-start(bf16[4,192,384]{2,1,0:T(8,128)(2,1)S(1)} %get-tuple-element.134), channel_id=1, source_target_pairs={{0,16},{16,0},{1,17},{17,1},{2,18},{18,2},{3,19},{19,3},{4,20},{20... | collective-permute-start | bytes 1769480 | tf_op jit(solution)/shard_map/ppermute | solution.py:557
  271.3 26.9 %collective-permute-start.70 = (bf16[4,192,384]{2,1,0:T(8,128)(2,1)S(1)}, bf16[4,192,384]{2,1,0:T(8,128)(2,1)S(1)}, u32[]{:S(2)}, u32[]{:S(2)}) collective-permute-start(bf16[4,192,384]{2,1,0:T(8,128)(2,1)S(1)} %get-tuple-element.133), channel_id=1, source_target_pairs={{0,24},{4,28},{8,16},{12,20},{16,8},{20,12},{24,0},{28,4},{1,25},{... | collective-permute-start | bytes 1769480 | tf_op jit(solution)/shard_map/ppermute | solution.py:565
  272.3 52.4 %collective-permute-start.45 = (bf16[24,1152]{1,0:T(8,128)(2,1)S(1)}, bf16[24,1152]{1,0:T(8,128)(2,1)S(1)}, u32[]{:S(2)}, u32[]{:S(2)}) collective-permute-start(bf16[24,1152]{1,0:T(8,128)(2,1)S(1)} %fusion.49), channel_id=1, source_target_pairs={{0,1},{1,0},{2,3},{3,2},{4,5},{5,4},{6,7},{7,6},{8,9},{9,8},{10,11... | collective-permute-start | bytes 165896 | tf_op jit(solution)/shard_map/ppermute | solution.py:557
  283.8 17.5 %collective-permute-start.51 = (bf16[4,24,768]{2,1,0:T(8,128)(2,1)S(1)}, bf16[4,24,768]{2,1,0:T(8,128)(2,1)S(1)}, u32[]{:S(2)}, u32[]{:S(2)}) collective-permute-start(bf16[4,24,768]{2,1,0:T(8,128)(2,1)S(1)} %get-tuple-element.150), channel_id=1, source_target_pairs={{0,8},{4,12},{8,0},{12,4},{1,9},{5,13},{9,1},{13,5},{2,10},{6,14},... | collective-permute-start | bytes 442376 | tf_op jit(solution)/shard_map/ppermute | solution.py:557
  286.1 15.4 %collective-permute-start.52 = (bf16[4,24,768]{2,1,0:T(8,128)(2,1)S(1)}, bf16[4,24,768]{2,1,0:T(8,128)(2,1)S(1)}, u32[]{:S(2)}, u32[]{:S(2)}) collective-permute-start(bf16[4,24,768]{2,1,0:T(8,128)(2,1)S(1)} %get-tuple-element.149), channel_id=1, source_target_pairs={{0,16},{16,0},{1,17},{17,1},{2,18},{18,2},{3,19},{19,3},{4,20},{20... | collective-permute-start | bytes 442376 | tf_op jit(solution)/shard_map/ppermute | solution.py:557
  301.5 14.3 %collective-permute-start.72 = (bf16[192,384]{1,0:T(8,128)(2,1)S(1)}, bf16[192,384]{1,0:T(8,128)(2,1)S(1)}, u32[]{:S(2)}, u32[]{:S(2)}) collective-permute-start(bf16[192,384]{1,0:T(8,128)(2,1)S(1)} %get-tuple-element.140), channel_id=1, source_target_pairs={{0,2},{1,3},{2,0},{3,1},{4,6},{5,7},{6,4},{7,5},{8,10},{9,11},{10,... | collective-permute-start | bytes 442376 | tf_op jit(solution)/shard_map/ppermute | solution.py:557
  331.9 23.4 %collective-permute-start.37 = (bf16[2,4,24,768]{3,2,1,0:T(8,128)(2,1)S(1)}, bf16[2,4,24,768]{3,2,1,0:T(8,128)(2,1)S(1)}, u32[]{:S(2)}, u32[]{:S(2)}) collective-permute-start(bf16[2,4,24,768]{3,2,1,0:T(8,128)(2,1)S(1)} %pad_maximum_fusion.7.first_own), channel_id=1, source_target_pairs={{0,4},{4,0},{8,12},{12,8},{1,5},{5,1},{9,13},{13,9},{2,6},{6,2},{1... | collective-permute-start | bytes 884744 | tf_op jit(solution)/shard_map/ppermute | solution.py:557
  334.2 17.7 %collective-permute-start.60 = (bf16[4,24,768]{2,1,0:T(8,128)(2,1)S(1)}, bf16[4,24,768]{2,1,0:T(8,128)(2,1)S(1)}, u32[]{:S(2)}, u32[]{:S(2)}) collective-permute-start(bf16[4,24,768]{2,1,0:T(8,128)(2,1)S(1)} %get-tuple-element.197), channel_id=1, source_target_pairs={{0,8},{4,12},{8,0},{12,4},{1,9},{5,13},{9,1},{13,5},{2,10},{6,14},... | collective-permute-start | bytes 442376 | tf_op jit(solution)/shard_map/ppermute | solution.py:557
  (85 other events, 767.2 us)

commit v3 on v2

v3 whole, which is shorter than its diff:
```python
import jax
import jax.numpy as jnp
from jax import lax
from jax.experimental import pallas as pl
from jax.experimental.pallas import tpu as pltpu
from jax.sharding import PartitionSpec as P


D = 768
HEADS = 6
HEAD_DIM = 64
KERNEL = 9
GROUPS = 2
MICRO = 2
WIDTH = HEADS * HEAD_DIM
PAIRS = HEADS // 2
RADIUS = KERNEL // 2
HALO = 16
PAD = 8
ID_PAD = HALO + PAD
TILE = 32
SLOT = 8
LANES = 128
GROUP_WIDTH = D // GROUPS
NORM_EPS = 1e-05
NEG_FILL = -1e30
SCORE_SCALE = HEAD_DIM ** (-0.5)
F32 = jnp.float32
BF16 = jnp.bfloat16
VMEM_BYTES = 60 * 1024 * 1024


def nn(left, right):
    return lax.dot_general(left, right, (((1,), (0,)), ((), ())), preferred_element_type=F32)


def nt(left, right):
    return lax.dot_general(left, right, (((1,), (1,)), ((), ())), preferred_element_type=F32)


def tn(left, right):
    return lax.dot_general(left, right, (((0,), (0,)), ((), ())), preferred_element_type=F32)


def split(values):
    high = values.astype(BF16)
    return high, (values - high.astype(F32)).astype(BF16)


def rows_at(start, size, unit=16):
    return pl.ds(pl.multiple_of(start, unit), size)


def whole(shape):
    return pl.BlockSpec(shape, lambda *_: (0,) * len(shape))


def per_micro(shape):
    return pl.BlockSpec((None,) + shape, lambda m: (m,) + (0,) * len(shape))


SCALARS = pl.BlockSpec(memory_space=pltpu.SMEM)


def run(kernel, outs, args, specs=None, out_specs=None, grid=None, scratch=(), flops=0):
    moved = sum(a.size * a.dtype.itemsize for a in args) + sum(
        o.size * o.dtype.itemsize for o in outs
    )
    extra = {} if grid is None else {"grid": grid}
    if specs is None:
        specs = [SCALARS] + [pl.BlockSpec(memory_space=pltpu.VMEM)] * (len(args) - 1)
    if out_specs is None:
        out_specs = [pl.BlockSpec(memory_space=pltpu.VMEM)] * len(outs)
    return pl.pallas_call(
        kernel,
        out_shape=tuple(outs),
        in_specs=specs,
        out_specs=tuple(out_specs),
        scratch_shapes=list(scratch),
        compiler_params=pltpu.CompilerParams(vmem_limit_bytes=VMEM_BYTES),
        cost_estimate=pl.CostEstimate(flops=int(flops), bytes_accessed=moved, transcendentals=0),
        **extra,
    )(*args)


def shaped(shape, kind):
    return jax.ShapeDtypeStruct(shape, kind)


DP, CORE, YBIT, _, CTX = range(5)


def assemble(target, pos, own, mine, theirs):
    dp, core = pos[DP], pos[CORE]
    half, part = own.shape[0], mine.shape[0]
    target[rows_at(dp * half, half), :] = own
    target[rows_at((1 - dp) * half + core * part, part), :] = mine
    target[rows_at((1 - dp) * half + (1 - core) * part, part), :] = theirs


def kv_kernel(pos, tokens, own, mine, theirs, kv_out, w_out):
    assemble(w_out, pos, own[:, WIDTH : 3 * WIDTH], mine[...], theirs[...])

    def step(i, carry):
        rows = rows_at(i * 128, 128)
        kv_out[rows, :] = nn(tokens[rows, :], w_out[...]).astype(BF16)
        return carry

    lax.fori_loop(0, tokens.shape[0] // 128, step, 0)


def slot_max(values):
    for shift in (8, 16, 32, 64):
        values = jnp.maximum(values, pltpu.roll(values, shift, 1))
    return values


def slot_sum(values):
    for shift in (8, 16, 32, 64):
        values = values + pltpu.roll(values, shift, 1)
    return values


def tap_column(mask, j):
    return mask[:, SLOT * j : SLOT * j + 1]


def conv_kernel(
    pos, ext, ids, own_in, own_point, mine, theirs, taps, w_tap, spread,
    q_out, c_out, pre_out, key_out, mixed_out, kern_out, mask_out, conv_out, w_qcp,
    ext_f, c_f, acc, pre_all,
):
    span = ext.shape[0]
    rows = conv_out.shape[0]
    own = slice(HALO, HALO + rows)

    @pl.when(pl.program_id(0) == 0)
    def _():
        assemble(w_qcp.at[:, :WIDTH], pos, own_in[:, :WIDTH], mine[:, :WIDTH], theirs[:, :WIDTH])
        assemble(
            w_qcp.at[:, WIDTH : 2 * WIDTH], pos, own_in[:, 3 * WIDTH :],
            mine[:, WIDTH : 2 * WIDTH], theirs[:, WIDTH : 2 * WIDTH],
        )
        assemble(
            w_qcp.at[:, 2 * WIDTH :], pos, own_point[...],
            mine[:, 2 * WIDTH : 3 * WIDTH], theirs[:, 2 * WIDTH : 3 * WIDTH],
        )
        for padded in (ext_f, c_f):
            padded[:PAD, :] = jnp.zeros((PAD, padded.shape[1]), F32)
            padded[PAD + span :, :] = jnp.zeros((PAD, padded.shape[1]), F32)

    window = ids[rows_at(pos[CTX] * rows, span + 2 * PAD, 8), :]
    centre = window[PAD : PAD + span, :]
    slot_id = lax.broadcasted_iota(jnp.int32, (span, LANES), 1) // SLOT
    mask = jnp.zeros((span, LANES), F32)
    for j in range(KERNEL):
        same = jnp.where(window[PAD - RADIUS + j : PAD - RADIUS + j + span, :] == centre, 1.0, 0.0)
        mask = jnp.where(slot_id == j, same, mask)
    mask_out[...] = mask

    ext_f[PAD : PAD + span, :] = ext[...].astype(F32)
    q = nn(ext[...], w_qcp[:, :WIDTH]).astype(BF16)
    q_out[...] = q
    c_low = nn(ext[...], w_qcp[:, WIDTH : 2 * WIDTH]).astype(BF16)
    c_out[...] = c_low
    c_f[PAD : PAD + span, :] = c_low.astype(F32)

    def pre_step(i, carry):
        start = i * TILE
        mask_rows = mask_out[rows_at(start, TILE), :]
        for lane in range(0, D, WIDTH):
            lanes = slice(lane, lane + WIDTH)
            block = ext_f[rows_at(start, TILE + 2 * PAD, 8), lanes]
            total = jnp.zeros((TILE, WIDTH), F32)
            for j in range(KERNEL):
                first = PAD - RADIUS + j
                total += block[first : first + TILE, :] * taps[j : j + 1, lanes] * tap_column(mask_rows, j)
            pre_all[rows_at(start, TILE), lanes] = total.astype(BF16)
        return carry

    lax.fori_loop(0, span // TILE, pre_step, 0)
    pre_out[...] = pre_all[own, :]
    conv_key = nn(pre_all[...], w_qcp[:, 2 * WIDTH :])
    key_out[...] = conv_key[own, :]
    mixed = (conv_key * q.astype(F32)).astype(BF16)
    mixed_out[...] = mixed[own, :]
    logits = nn(mixed, w_tap[...])
    logits = jnp.where(slot_id < KERNEL, logits, NEG_FILL)
    expo = jnp.exp(logits - slot_max(logits))
    kern = expo / slot_sum(expo)
    kern_out[...] = kern
    high, low = split((kern * mask)[own, :])
    both = jnp.concatenate([high, low], axis=1)
    for j in range(KERNEL):
        first = PAD + HALO - RADIUS + j
        part = nn(both, spread[j]) * c_f[first : first + rows, :]
        if j == 0:
            acc[...] = part
        else:
            acc[...] += part
    conv_out[...] = acc[...].astype(BF16)


def kv_block(kv_near, kv_far, place):
    return jnp.where(place % 2 == 1, kv_far[place // 2], kv_near[place // 2])


def attend_kernel(
    bounds, pos, q_ext, kv_near, kv_far, key_ids, query_ids, context_out, out_t, lse_out,
    q_t, top, total, acc, kv,
):
    micro = pl.program_id(0)
    rows = context_out.shape[0]
    q = q_ext.at[HALO : HALO + rows, :]
    half = lax.broadcasted_iota(jnp.int32, (LANES, rows), 0) < HEAD_DIM
    scaled = q[...].astype(F32) * SCORE_SCALE
    for p in range(PAIRS):
        pair = jnp.transpose(scaled[:, p * LANES : (p + 1) * LANES])
        q_t[2 * p] = jnp.where(half, pair, 0.0).astype(BF16)
        q_t[2 * p + 1] = jnp.where(half, 0.0, pair).astype(BF16)
    top[...] = jnp.full_like(top, NEG_FILL)
    total[...] = jnp.zeros_like(total)
    acc[...] = jnp.zeros_like(acc)

    def step(b, carry):
        kv[...] = kv_block(kv_near, kv_far, jnp.bitwise_xor(b, pos[CTX]))
        bias = jnp.where(key_ids[rows_at(ID_PAD + b * rows, rows, 8), :] == query_ids[...], 0.0, NEG_FILL)
        for h in range(HEADS):
            p = h // 2
            k_block = kv[:, p * LANES : (p + 1) * LANES]
            v_block = kv[:, WIDTH + p * LANES : WIDTH + (p + 1) * LANES]
            scores = nn(k_block, q_t[h]) + bias
            old = top[h : h + 1, :]
            new = jnp.maximum(old, jnp.max(scores, axis=0, keepdims=True))
            scale = jnp.exp(old - new)
            weights = jnp.exp(scores - new)
            total[h : h + 1, :] = total[h : h + 1, :] * scale + jnp.sum(weights, axis=0, keepdims=True)
            top[h : h + 1, :] = new
            part = tn(v_block, weights.astype(BF16))
            first = (h % 2) * HEAD_DIM
            own = slice(h * HEAD_DIM, (h + 1) * HEAD_DIM)
            acc[own, :] = acc[own, :] * scale + part[first : first + HEAD_DIM, :]
        return carry

    lax.fori_loop(bounds[0, micro], bounds[1, micro], step, 0)
    lse_out[...] = top[...] + jnp.log(jnp.maximum(total[...], 1e-37))
    for h in range(HEADS):
        own = slice(h * HEAD_DIM, (h + 1) * HEAD_DIM)
        out_t[own, :] = acc[own, :] / total[h : h + 1, :]
    for p in range(PAIRS):
        pair = slice(p * LANES, (p + 1) * LANES)
        context_out[:, pair] = jnp.transpose(out_t[pair, :]).astype(BF16)


def attend_back_kernel(
    bounds, pos, q_ext, grad, kv_near, kv_far, key_ids, query_ids, lse, out_t, dq_out, grad_near, grad_far,
    q_t, g_t, q_z, g_z, delta, acc, kv,
):
    micro = pl.program_id(0)
    rows = grad.shape[0]
    q = q_ext.at[HALO : HALO + rows, :]
    half = lax.broadcasted_iota(jnp.int32, (LANES, rows), 0) < HEAD_DIM
    half_lane = lax.broadcasted_iota(jnp.int32, (rows, LANES), 1) < HEAD_DIM
    for p in range(PAIRS):
        lanes = slice(p * LANES, (p + 1) * LANES)
        q_pair = q[:, lanes].astype(F32) * SCORE_SCALE
        g_pair = grad[:, lanes].astype(F32)
        for source, across, along in ((q_pair, q_t, q_z), (g_pair, g_t, g_z)):
            turned = jnp.transpose(source)
            across[2 * p] = jnp.where(half, turned, 0.0).astype(BF16)
            across[2 * p + 1] = jnp.where(half, 0.0, turned).astype(BF16)
            along[2 * p] = jnp.where(half_lane, source, 0.0).astype(BF16)
            along[2 * p + 1] = jnp.where(half_lane, 0.0, source).astype(BF16)
            if source is g_pair:
                product = turned * out_t[lanes, :]
                delta[2 * p : 2 * p + 1, :] = jnp.sum(product[:HEAD_DIM], axis=0, keepdims=True)
                delta[2 * p + 1 : 2 * p + 2, :] = jnp.sum(product[HEAD_DIM:], axis=0, keepdims=True)
    acc[...] = jnp.zeros_like(acc)
    grad_near[...] = jnp.zeros_like(grad_near)
    grad_far[...] = jnp.zeros_like(grad_far)

    def step(b, carry):
        place = jnp.bitwise_xor(b, pos[CTX])
        kv[...] = kv_block(kv_near, kv_far, place)
        bias = jnp.where(key_ids[rows_at(ID_PAD + b * rows, rows, 8), :] == query_ids[...], 0.0, NEG_FILL)
        for p in range(PAIRS):
            lanes = slice(p * LANES, (p + 1) * LANES)
            value_lanes = slice(WIDTH + p * LANES, WIDTH + (p + 1) * LANES)
            k_block, v_block = kv[:, lanes], kv[:, value_lanes]
            k_grad = v_grad = 0.0
            for h in (2 * p, 2 * p + 1):
                weights = jnp.exp(nn(k_block, q_t[h]) + bias - lse[h : h + 1, :])
                slopes = (weights * (nn(v_block, g_t[h]) - delta[h : h + 1, :])).astype(BF16)
                first = (h % 2) * HEAD_DIM
                own = slice(h * HEAD_DIM, (h + 1) * HEAD_DIM)
                acc[own, :] += tn(k_block, slopes)[first : first + HEAD_DIM, :]
                k_grad = k_grad + nn(slopes, q_z[h])
                v_grad = v_grad + nn(weights.astype(BF16), g_z[h])
            kv[:, lanes] = k_grad.astype(BF16)
            kv[:, value_lanes] = v_grad.astype(BF16)

        @pl.when(place % 2 == 0)
        def _():
            grad_near[place // 2] = kv[...]

        @pl.when(place % 2 == 1)
        def _():
            grad_far[place // 2] = kv[...]

        return carry

    lax.fori_loop(bounds[0, micro], bounds[1, micro], step, 0)
    for p in range(PAIRS):
        pair = slice(p * LANES, (p + 1) * LANES)
        dq_out[:, pair] = jnp.transpose(acc[pair, :]) * SCORE_SCALE


def gelu_parts(values):
    spread = 0.5 * (1.0 + lax.erf(values * 0.7071067811865476))
    slope = spread + values * (jnp.exp(values * values * -0.5) * 0.3989422804014327)
    return values * spread, slope


def norm_stats(values):
    average = jnp.mean(values, axis=-1, keepdims=True)
    centred = values - average
    inverse = lax.rsqrt(jnp.mean(centred * centred, axis=-1, keepdims=True) + NORM_EPS)
    return centred * inverse, inverse


def norm_back(scaled, normal, inverse):
    inner = (
        scaled
        - jnp.mean(scaled, axis=-1, keepdims=True)
        - normal * jnp.mean(scaled * normal, axis=-1, keepdims=True)
    )
    return inner * inverse


def emit_rows(source, pos, keep, send):
    depth = D // 8
    for cc, target in ((0, keep), (1, send)):
        for dd in range(2):
            for yy in range(2):
                start = (
                    jnp.bitwise_xor(pos[DP], dd) * (D // 2)
                    + jnp.bitwise_xor(pos[CORE], cc) * (D // 4)
                    + jnp.bitwise_xor(pos[YBIT], yy) * depth
                )
                target[dd, yy, :depth] = source[rows_at(start, depth), :].astype(BF16)


ROWS_A = 256


def middle_kernel(
    pos, attn, conv, tokens, cotangent, own_out, mine_out, theirs_out, vectors, *rest
):
    ffn_parts, rest = rest[:8], rest[8:]
    rows_out, pre_out, grad_attn, grad_conv, ffn_keep, ffn_send, vector_grads = rest[:7]
    middle_steps(
        pos, attn, conv, tokens, cotangent, own_out, mine_out, theirs_out, vectors, ffn_parts,
        rows_out, pre_out, grad_attn, grad_conv, ffn_keep, ffn_send, vector_grads, *rest[7:]
    )


def middle_steps(
    pos, attn, conv, tokens, cotangent, own_out, mine_out, theirs_out, vectors, ffn_parts,
    rows_out, pre_out, grad_attn, grad_conv, ffn_keep, ffn_send, vector_grads,
    w_out, w_ffn, context, ffn_in, low_down, act, slope, grad_up, low_mix,
    normal, inverse, normed, total, out_grad,
):
    dp, core = pos[DP], pos[CORE]
    w_up, w_down = w_ffn.at[0], w_ffn.at[1]
    hidden = w_ffn.shape[3]
    shard = ffn_parts[0].shape[3]
    half = GROUP_WIDTH // 2
    low, high = 3 * WIDTH, 3 * WIDTH + D
    assemble(w_out, pos, own_out[...], mine_out[:, low:high], theirs_out[:, low:high])
    for gg in range(GROUPS):
        for dd in range(2):
            place = rows_at(jnp.bitwise_xor(dp, dd) * half, half)
            for part in range(2):
                piece = ffn_parts[4 * gg + 2 * dd + part]
                for k in range(piece.shape[0]):
                    first = (part * piece.shape[0] + k) * shard
                    for ud in range(2):
                        w_ffn[ud, gg, place, first : first + shard] = piece[k, ud]
    context[:, :WIDTH] = attn[...]
    context[:, WIDTH:] = conv[...]
    vector_grads[...] = jnp.zeros_like(vector_grads)
    gain_one, bias_one = vectors[0:1, :], vectors[1:2, :]
    gain_two, bias_two = vectors[2:3, :], vectors[3:4, :]
    group_of = [jnp.bitwise_xor(core, gg) * GROUP_WIDTH for gg in range(GROUPS)]

    def lanes_of(gg):
        return pl.ds(pl.multiple_of(group_of[gg], LANES), GROUP_WIDTH)

    def tile(i, carry):
        rows = rows_at(i * ROWS_A, ROWS_A)
        summed = tokens[rows, :].astype(F32) + nn(context[rows, :], w_out[...])
        normal_rows, inverse_rows = norm_stats(summed)
        normal[...] = normal_rows
        inverse[...] = inverse_rows
        normed_rows = normal_rows * gain_one + bias_one
        normed[...] = normed_rows
        ffn_in[rows, :] = normed_rows.astype(BF16)
        for gg in range(GROUPS):
            group_in = ffn_in[rows, lanes_of(gg)]

            def forward(k, carry):
                columns = pl.ds(pl.multiple_of(k * shard, LANES), shard)
                value, rate = gelu_parts(nn(group_in, w_up[gg, :, columns]))
                act[gg, rows, columns] = value.astype(BF16)
                slope[gg, :, columns] = rate
                return carry

            lax.fori_loop(0, hidden // shard, forward, 0)
            total[:, lanes_of(gg)] = normed[:, lanes_of(gg)] + nt(act[gg, rows, :], w_down[gg])
        normal_two, inverse_two = norm_stats(total[...])
        rows_out[rows, :] = (normal_two * gain_two + bias_two).astype(BF16)
        upstream = cotangent[rows, :].astype(F32)
        vector_grads[2:3, :] += jnp.sum(upstream * normal_two, axis=0, keepdims=True)
        vector_grads[3:4, :] += jnp.sum(upstream, axis=0, keepdims=True)
        grad_z = norm_back(upstream * gain_two, normal_two, inverse_two)
        total[...] = grad_z
        low_down[rows, :] = grad_z.astype(BF16)
        for gg in range(GROUPS):
            group_grad = low_down[rows, lanes_of(gg)]

            def backward(k, carry):
                columns = pl.ds(pl.multiple_of(k * shard, LANES), shard)
                grad = nn(group_grad, w_down[gg, :, columns]) * slope[gg, :, columns]
                grad_up[gg, rows, columns] = grad.astype(BF16)
                return carry

            lax.fori_loop(0, hidden // shard, backward, 0)
            total[:, lanes_of(gg)] += nt(grad_up[gg, rows, :], w_up[gg])
        grad_normed = total[...]
        vector_grads[0:1, :] += jnp.sum(grad_normed * normal[...], axis=0, keepdims=True)
        vector_grads[1:2, :] += jnp.sum(grad_normed, axis=0, keepdims=True)
        grad_pre = norm_back(grad_normed * gain_one, normal[...], inverse[...])
        pre_out[rows, :] = grad_pre
        low_mix[rows, :] = grad_pre.astype(BF16)
        grad_attn[rows, :] = nt(low_mix[rows, :], w_out[:WIDTH, :]).astype(BF16)
        grad_conv[rows, :] = nt(low_mix[rows, :], w_out[WIDTH:, :]).astype(BF16)
        return carry

    lax.fori_loop(0, tokens.shape[0] // ROWS_A, tile, 0)

    for gg, target in ((0, ffn_keep), (1, ffn_send)):

        def weights(k, carry):
            columns = pl.ds(pl.multiple_of(k * shard, LANES), shard)
            up_grad = tn(ffn_in[:, lanes_of(gg)], grad_up[gg, :, columns]).astype(BF16)
            down_grad = tn(low_down[:, lanes_of(gg)], act[gg, :, columns]).astype(BF16)
            for d in range(2):
                dd = jnp.bitwise_xor(dp, d)
                part = slice(d * half, (d + 1) * half)
                target[dd, pos[YBIT], k] = up_grad[part]
                target[dd, 1 - pos[YBIT], k] = down_grad[part]
            return carry

        lax.fori_loop(0, hidden // shard, weights, 0)
    out_grad[...] = tn(context[...], low_mix[...])
    last = hidden // shard
    for cc, target in ((0, ffn_keep), (1, ffn_send)):
        for dd in range(2):
            start = jnp.bitwise_xor(dp, dd) * (D // 2) + jnp.bitwise_xor(core, cc) * (D // 4)
            for yy in range(2):
                columns = pl.ds(
                    pl.multiple_of(jnp.bitwise_xor(pos[YBIT], yy) * (D // 2), LANES), D // 2
                )
                target[dd, yy, last] = out_grad[rows_at(start, D // 4), columns].astype(BF16)


def conv_back_kernel(
    grad_ext, kern_ext, c_ext, mask, mixed, q_ext, conv_key, pre_key, ext, pre_grad,
    w_tap, w_qcp, spread, tap_table,
    grad_c_out, dq_out, direct_out, tap_grad, point_grad, depth_grad,
    grad_f, c_f, ext_f, prod, acc, gpk_f,
):
    span = ext.shape[0]
    rows = mixed.shape[0]
    own = slice(HALO, HALO + rows)
    body = slice(PAD, PAD + span)

    @pl.when(pl.program_id(0) == 0)
    def _():
        tap_grad[...] = jnp.zeros_like(tap_grad)
        point_grad[...] = jnp.zeros_like(point_grad)
        depth_grad[...] = jnp.zeros_like(depth_grad)
        for padded in (grad_f, c_f, ext_f, prod, gpk_f):
            padded[:PAD, :] = jnp.zeros((PAD, padded.shape[1]), F32)
            padded[PAD + span :, :] = jnp.zeros((PAD, padded.shape[1]), F32)

    grad_f[body, :] = grad_ext[...].astype(F32)
    c_f[body, :] = c_ext[...].astype(F32)
    ext_f[body, :] = ext[...].astype(F32)
    taps = jnp.zeros((span, LANES), F32)
    for j in range(KERNEL):
        shifted = slice(PAD - RADIUS + j, PAD - RADIUS + j + span)
        taps += nt((grad_f[body, :] * c_f[shifted, :]).astype(BF16), spread[j, :LANES, :])
    taps = taps * mask[...]
    kern = kern_ext[...]
    grad_logits = kern * (taps - slot_sum(kern * taps))
    high, low = split(grad_logits)
    grad_mixed = (nt(high, w_tap[...]) + nt(low, w_tap[...])).astype(BF16).astype(F32)
    tap_grad[...] += tn(mixed[...], high[own, :]) + tn(mixed[...], low[own, :])
    grad_key = (grad_mixed * q_ext[...].astype(F32)).astype(BF16)
    dq_out[...] = grad_mixed[own, :] * conv_key[...]
    point_grad[...] += tn(pre_key[...], grad_key[own, :])
    gpk_f[body, :] = nt(grad_key, w_qcp[:, 2 * WIDTH :])

    def depth_step(i, carry):
        start = i * TILE
        place = rows_at(start, TILE)
        mask_rows = mask[rows_at(start + HALO, TILE), :]
        for lane in range(0, D, WIDTH):
            lanes = slice(lane, lane + WIDTH)
            block = ext_f[rows_at(start + HALO, TILE + 2 * PAD, 8), lanes]
            gpk_block = gpk_f[rows_at(start + HALO, TILE + 2 * PAD, 8), lanes]
            gpk = gpk_block[PAD : PAD + TILE, :]
            direct = pre_grad[place, lanes]
            for j in range(KERNEL):
                first = PAD - RADIUS + j
                column = tap_column(mask_rows, j)
                value = block[first : first + TILE, :] * (gpk * column)
                folded = value[0:8, :]
                for r in range(8, TILE, 8):
                    folded = folded + value[r : r + 8, :]
                depth_grad[8 * j : 8 * j + 8, lanes] += folded
                tap = tap_table[KERNEL - 1 - j : KERNEL - j, lanes]
                direct += gpk_block[first : first + TILE, :] * tap * column
            direct_out[place, lanes] = direct
        return carry

    lax.fori_loop(0, rows // TILE, depth_step, 0)
    kern_high, kern_low = split(kern)
    both = jnp.concatenate([kern_high, kern_low], axis=1)
    for j in range(KERNEL):
        prod[body, :] = nn(both, spread[KERNEL - 1 - j]) * grad_f[body, :]
        shifted = slice(PAD + HALO - RADIUS + j, PAD + HALO - RADIUS + j + rows)
        part = prod[shifted, :] * tap_column(mask[own, :], j)
        if j == 0:
            acc[...] = part
        else:
            acc[...] += part
    grad_c_out[...] = acc[...].astype(BF16)


EXTRA = 16
TAP_ROWS = 24


def first_grads_kernel(
    pos, tokens, dq_attn, dq_conv, grad_c, point_grad, depth_grad, vector_grads, tap_grad,
    grad_q_out, keep, send, low_q, total, extra,
):
    low_q[...] = (dq_attn[...] + dq_conv[...]).astype(BF16)
    grad_q_out[...] = low_q[...]
    total[:, :WIDTH] = tn(tokens[...], low_q[...])
    total[:, WIDTH : 2 * WIDTH] = tn(tokens[...], grad_c[...])
    total[:, 2 * WIDTH :] = point_grad[...]
    emit_rows(total, pos, keep, send)
    extra[...] = jnp.zeros_like(extra)
    half = D // 2
    for d in range(2):
        for i in range(WIDTH // 2 // TAP_ROWS):
            first = d * (WIDTH // 2) + i * TAP_ROWS
            extra[d, :TAP_ROWS, i * LANES : (i + 1) * LANES] = tap_grad[first : first + TAP_ROWS, :]
        lanes = slice(d * half, (d + 1) * half)
        for j in range(KERNEL):
            extra[d, TAP_ROWS + j : TAP_ROWS + j + 1, :half] = jnp.sum(
                depth_grad[8 * j : 8 * j + 8, lanes], axis=0, keepdims=True
            )
        extra[d, TAP_ROWS + KERNEL : TAP_ROWS + KERNEL + 4, :half] = vector_grads[:4, lanes]
    depth = D // 8
    for cc, target in ((0, keep), (1, send)):
        for dd in range(2):
            for yy in range(2):
                quarter = 2 * jnp.bitwise_xor(pos[CORE], cc) + jnp.bitwise_xor(pos[YBIT], yy)
                sheet = extra[jnp.bitwise_xor(pos[DP], dd), rows_at(quarter * EXTRA, EXTRA), :]
                target[dd, yy, depth:] = sheet.astype(BF16)


def second_grads_kernel(pos, tokens, kept, arrived, grad_kv_out, keep, send, low_kv, total):
    low_kv[...] = (kept[...].astype(F32) + arrived[...].astype(F32)).astype(BF16)
    grad_kv_out[...] = low_kv[...]
    total[...] = tn(tokens[...], low_kv[...])
    emit_rows(total, pos, keep, send)


def input_grad_kernel(direct, grad_q, grad_kv, grad_c, w_kv, w_qcp, out):
    value = direct[...] + nt(grad_q[...], w_qcp[:, :WIDTH])
    value += nt(grad_c[...], w_qcp[:, WIDTH : 2 * WIDTH])
    value += nt(grad_kv[...], w_kv[...])
    out[...] = value.astype(BF16)


def unpack_kernel(pos, f_own, f_other, first_own, first_other, second_own, second_other,
                  in_out, out_out, point_out, extra):
    depth = D // 8
    for cc in range(2):
        core = jnp.bitwise_xor(pos[CORE], cc)
        for yy in range(2):
            side = jnp.bitwise_xor(pos[YBIT], yy)
            place = rows_at(core * (D // 4) + side * depth, depth, 8)
            first = (first_own, first_other)[cc][yy].astype(F32)
            second = (second_own, second_other)[cc][yy].astype(F32)
            columns = pl.ds(pl.multiple_of(side * (D // 2), LANES), D // 2)
            out_out[rows_at(core * (D // 4), D // 4, 8), columns] = (f_own, f_other)[cc][yy, 1].astype(F32)
            in_out[place, :WIDTH] = first[:depth, :WIDTH]
            in_out[place, 3 * WIDTH :] = first[:depth, WIDTH : 2 * WIDTH]
            point_out[place, :] = first[:depth, 2 * WIDTH :]
            in_out[place, WIDTH : 3 * WIDTH] = second
            extra[rows_at((2 * core + side) * EXTRA, EXTRA, 8), :] = first[depth:, :]


def flips(axis, bit):
    return [(i, i ^ bit) for i in range(lax.axis_size(axis))]


def swap(block, axis, bit):
    return lax.ppermute(block, axis, flips(axis, bit))


def add_low(*blocks):
    return sum(b.astype(F32) for b in blocks).astype(BF16)


def far_bits():
    bits, bit = [], 4
    while bit < lax.axis_size("ctx"):
        bits.append(bit)
        bit *= 2
    return bits


def reduce_shares(keep, send):
    arrived = swap(send, "ctx", 1)
    sent = add_low(keep[1], arrived[1])
    received = swap(sent, "dp", 1)
    sent = add_low(keep[0, 1], arrived[0, 1], received[1])
    share = add_low(keep[0, 0], arrived[0, 0], received[0], swap(sent, "ctx", 2))
    for bit in far_bits():
        share = add_low(share, swap(share, "ctx", bit))
    return share


def reduce_line(share):
    bit = 1
    while bit < lax.axis_size("tensor"):
        share = add_low(share, swap(share, "tensor", bit))
        bit *= 2
    return share


def reduce_ffn(share):
    count, bit = lax.axis_size("tensor"), 1
    places = list(range(count))
    blocks = {k: share[k] for k in range(count + 1)}
    while bit < count:
        sent = jnp.stack([blocks[k] for k in places if k & bit] + [blocks[count]])
        received = swap(sent, "tensor", bit)
        kept = [k for k in places if not k & bit]
        blocks = {k: add_low(blocks[k], received[i]) for i, k in enumerate(kept + [count])}
        places = kept
        bit *= 2
    return jnp.stack([blocks[0], blocks[count]])


def gather_shares(share):
    own = jnp.stack([share, swap(share, "ctx", 2)])
    return own, swap(own, "ctx", 1)


def neighbours(block):
    count = lax.axis_size("ctx")
    up = [(i, i + 1) for i in range(count - 1)]
    down = [(i + 1, i) for i in range(count - 1)]
    rows = block.shape[1]
    low = lax.ppermute(block[:, rows - HALO :], "ctx", up)
    high = lax.ppermute(block[:, :HALO], "ctx", down)
    return low, high


def with_edges(block, edges):
    return jnp.concatenate([edges[0], block, edges[1]], axis=1)


def ordered(own, other, high):
    return jnp.where(high, other, own), jnp.where(high, own, other)


def gather_kv(block):
    block, bit = block[None], 2
    while bit < lax.axis_size("ctx"):
        block = jnp.concatenate([block, swap(block, "ctx", bit)], axis=0)
        bit *= 2
    return block, swap(block, "ctx", 1)


def layer(
    hidden, segment_ids, w_in, w_depth, w_point, w_kernel, w_out,
    norm1_gain, norm1_bias, norm2_gain, norm2_bias, w_up, w_down, out_grad,
):
    micro, rows = MICRO, hidden.shape[2]
    seq = segment_ids.shape[2]
    flat = micro * rows
    ctx_count = lax.axis_size("ctx")
    tensor_count = lax.axis_size("tensor")
    dp, ctx, tensor = lax.axis_index("dp"), lax.axis_index("ctx"), lax.axis_index("tensor")
    core = ctx % 2
    pos = jnp.stack([dp, core, (ctx // 2) % 2, tensor, ctx]).astype(jnp.int32)
    tokens = hidden[:, 0]
    tokens_flat = tokens.reshape(flat, D)
    cotangent = out_grad[:, 0].reshape(flat, D)
    ids = segment_ids[:, 0]
    half = w_in.shape[0]
    part = half // 2

    def part_of(weight):
        return lax.dynamic_slice_in_dim(weight, core * part, part, axis=0)

    kv_mine = swap(part_of(w_in)[:, WIDTH : 3 * WIDTH], "dp", 1)
    edges = neighbours(tokens)
    vectors = jnp.stack([norm1_gain, norm1_bias, norm2_gain, norm2_bias], axis=0)
    small = jnp.concatenate([w_depth.T, vectors], axis=0)
    small = jnp.pad(small, ((0, 16 - small.shape[0]), (0, 0)))
    tap_half = w_kernel.reshape(-1, HEADS, KERNEL).transpose(0, 2, 1)
    tap_half = jnp.pad(tap_half, ((0, 0), (0, 0), (0, SLOT - HEADS))).reshape(-1, SLOT * KERNEL)
    tap_half = jnp.pad(tap_half, ((0, 0), (0, LANES - SLOT * KERNEL)))
    sheet = small.reshape(-1, LANES)
    sheet = jnp.pad(sheet, ((0, part - sheet.shape[0]), (0, 0)))
    own_part = part_of(w_in)
    pack = jnp.concatenate(
        [own_part[:, :WIDTH], own_part[:, 3 * WIDTH :], part_of(w_point), part_of(w_out),
         jnp.where(core == 1, sheet, tap_half)],
        axis=1,
    )
    pack_mine = swap(pack, "dp", 1)
    kv_theirs = swap(kv_mine, "ctx", 1)
    pack_theirs = swap(pack_mine, "ctx", 1)
    tap_other, small_other = ordered(pack_mine[:, 3 * WIDTH + D :], pack_theirs[:, 3 * WIDTH + D :], core == 1)
    small_other = small_other[: 16 * half // LANES].reshape(16, half)
    small = jnp.concatenate(ordered(small, small_other, dp == 1), axis=1).astype(F32)
    w_tap = jnp.concatenate(ordered(tap_half, tap_other, dp == 1), axis=0)
    taps = small
    vectors = small[KERNEL : KERNEL + 4]

    def side(weight):
        return jnp.where(core == 1, weight[:, 1], weight[:, 0])

    ffn, bit = jnp.stack([side(w_up), side(w_down)])[None], 1
    while 2 * bit < tensor_count:
        ffn = jnp.concatenate([ffn, swap(ffn, "tensor", bit)], axis=0)
        bit *= 2
    ffn_parts = [ffn, swap(ffn, "tensor", bit)]
    ffn_parts += [swap(piece, "dp", 1) for piece in ffn_parts]
    ffn_parts += [swap(piece, "ctx", 1) for piece in ffn_parts]

    offset = ctx * rows
    own_ids = lax.dynamic_slice_in_dim(ids, offset, rows, axis=1)
    blocks = ids.reshape(micro, ctx_count, rows)
    first = jnp.sum((blocks[:, :, -1] < own_ids[:, :1]).astype(jnp.int32), axis=1)
    last = jnp.sum((blocks[:, :, 0] <= own_ids[:, -1:]).astype(jnp.int32), axis=1)
    bounds = jnp.stack([first, last])
    key_ids = jnp.pad(ids, ((0, 0), (ID_PAD, ID_PAD)), constant_values=-1)[:, :, None]
    query_ids = own_ids[:, None, :]
    lane_id = lax.broadcasted_iota(jnp.int32, (KERNEL, 2 * LANES, WIDTH), 1) % LANES
    head_id = lax.broadcasted_iota(jnp.int32, (KERNEL, 2 * LANES, WIDTH), 2) // HEAD_DIM
    tap_id = lax.broadcasted_iota(jnp.int32, (KERNEL, 2 * LANES, WIDTH), 0)
    spread = (lane_id == SLOT * tap_id + head_id).astype(BF16)

    kv_rows, w_kv = run(
        kv_kernel,
        [shaped((flat, 2 * WIDTH), BF16), shaped((D, 2 * WIDTH), BF16)],
        [pos, tokens_flat, w_in, kv_mine, kv_theirs],
        flops=2 * flat * D * 2 * WIDTH,
    )
    kv_near, kv_far = gather_kv(kv_rows.reshape(micro, rows, 2 * WIDTH))

    depth = {"pipeline_mode": pl.Buffered(1)} if seq > 2048 else {}

    def long_block(shape, index):
        return pl.BlockSpec(shape, index, **depth)

    kv_half = long_block((ctx_count // 2, None, rows, 2 * WIDTH), lambda m: (0, m, 0, 0))
    seq_ids = long_block((None, seq + 2 * ID_PAD, 1), lambda m: (m, 0, 0))
    span = rows + 2 * HALO
    ext = with_edges(tokens, edges)
    once = whole
    q_ext, c_ext, pre_key, conv_key, mixed, kern_ext, mask, conv_out, w_qcp = run(
        conv_kernel,
        [
            shaped((micro, span, WIDTH), BF16), shaped((micro, span, WIDTH), BF16),
            shaped((micro, rows, D), BF16), shaped((micro, rows, WIDTH), F32),
            shaped((micro, rows, WIDTH), BF16), shaped((micro, span, LANES), F32), shaped((micro, span, LANES), F32),
            shaped((micro, rows, WIDTH), BF16), shaped((D, 3 * WIDTH), BF16),
        ],
        [pos, ext, key_ids, w_in, w_point, pack_mine, pack_theirs, taps, w_tap, spread],
        specs=[SCALARS, per_micro((span, D)), seq_ids, once(w_in.shape), once(w_point.shape),
               once(pack_mine.shape), once(pack_theirs.shape), once(taps.shape), once(w_tap.shape), once(spread.shape)],
        out_specs=[per_micro((span, WIDTH)), per_micro((span, WIDTH)), per_micro((rows, D)), per_micro((rows, WIDTH)),
                   per_micro((rows, WIDTH)), per_micro((span, LANES)), per_micro((span, LANES)),
                   per_micro((rows, WIDTH)), once((D, 3 * WIDTH))],
        grid=(micro,),
        scratch=[pltpu.VMEM((span + 2 * PAD, D), F32), pltpu.VMEM((span + 2 * PAD, WIDTH), F32),
                 pltpu.VMEM((rows, WIDTH), F32), pltpu.VMEM((span, D), BF16)],
        flops=2 * flat * WIDTH * (3 * D + 256 * KERNEL),
    )

    head_scratch = pltpu.VMEM((HEADS, LANES, rows), BF16)
    lane_scratch = pltpu.VMEM((HEADS, rows, LANES), BF16)
    row_scratch = pltpu.VMEM((8, rows), F32)
    block_scratch = pltpu.VMEM((rows, 2 * WIDTH), BF16)
    context, attn_t, lse = run(
        attend_kernel,
        [shaped((micro, rows, WIDTH), BF16), shaped((micro, WIDTH, rows), F32), shaped((micro, 8, rows), F32)],
        [bounds, pos, q_ext, kv_near, kv_far, key_ids, query_ids],
        specs=[SCALARS, SCALARS, per_micro((span, WIDTH)), kv_half, kv_half, seq_ids, per_micro((1, rows))],
        out_specs=[per_micro((rows, WIDTH)), per_micro((WIDTH, rows)), per_micro((8, rows))],
        grid=(micro,),
        scratch=[head_scratch, row_scratch, row_scratch, pltpu.VMEM((WIDTH, rows), F32), block_scratch],
        flops=16 * flat * 4 * rows * WIDTH,
    )

    hidden_units = tensor_count * w_up.shape[2]
    shard = w_up.shape[2]
    ffn_share = (2, 2, tensor_count + 1, GROUP_WIDTH // 2, shard)

    rows_out, grad_pre, grad_attn, grad_conv, ffn_keep, ffn_send, vector_grads = run(
        middle_kernel,
        [
            shaped((flat, D), BF16), shaped((flat, D), F32), shaped((flat, WIDTH), BF16), shaped((flat, WIDTH), BF16),
            shaped(ffn_share, BF16), shaped(ffn_share, BF16),
            shaped((8, D), F32),
        ],
        [pos, context.reshape(flat, WIDTH), conv_out.reshape(flat, WIDTH), tokens_flat, cotangent,
         w_out, pack_mine, pack_theirs, vectors, *ffn_parts],
        scratch=[
            pltpu.VMEM((D, D), BF16),
            pltpu.VMEM((2, GROUPS, GROUP_WIDTH, hidden_units), BF16),
            pltpu.VMEM((flat, D), BF16), pltpu.VMEM((flat, D), BF16), pltpu.VMEM((flat, D), BF16),
            pltpu.VMEM((GROUPS, flat, hidden_units), BF16),
            pltpu.VMEM((GROUPS, ROWS_A, hidden_units), F32),
            pltpu.VMEM((GROUPS, flat, hidden_units), BF16),
            pltpu.VMEM((flat, D), BF16),
            pltpu.VMEM((ROWS_A, D), F32), pltpu.VMEM((ROWS_A, 1), F32),
            pltpu.VMEM((ROWS_A, D), F32), pltpu.VMEM((ROWS_A, D), F32), pltpu.VMEM((D, D), F32),
        ],
        flops=2 * flat * D * (3 * D + 3 * hidden_units),
    )

    grad_attn = grad_attn.reshape(micro, rows, WIDTH)
    grad_conv = grad_conv.reshape(micro, rows, WIDTH)
    grad_ext = with_edges(grad_conv, neighbours(grad_conv))

    dq_attn, grad_near, grad_far = run(
        attend_back_kernel,
        [shaped((micro, rows, WIDTH), F32), shaped((ctx_count // 2, micro, rows, 2 * WIDTH), BF16),
         shaped((ctx_count // 2, micro, rows, 2 * WIDTH), BF16)],
        [bounds, pos, q_ext, grad_attn, kv_near, kv_far, key_ids, query_ids, lse, attn_t],
        specs=[SCALARS, SCALARS, per_micro((span, WIDTH)), per_micro((rows, WIDTH)), kv_half, kv_half,
               seq_ids, per_micro((1, rows)), per_micro((8, rows)), per_micro((WIDTH, rows))],
        out_specs=[per_micro((rows, WIDTH)), kv_half, kv_half],
        grid=(micro,),
        scratch=[head_scratch, head_scratch, lane_scratch, lane_scratch, row_scratch,
                 pltpu.VMEM((WIDTH, rows), F32), block_scratch],
        flops=40 * flat * 4 * rows * WIDTH,
    )
    arrived = swap(grad_far, "ctx", 1)
    kv_parts = [add_low(grad_near[k], arrived[k]) for k in range(ctx_count // 2)]
    bit = 2
    while len(kv_parts) > 2:
        received = swap(jnp.stack(kv_parts[1::2]), "ctx", bit)
        kv_parts = [add_low(a, received[k]) for k, a in enumerate(kv_parts[0::2])]
        bit *= 2
    kv_arrived = swap(kv_parts[1], "ctx", bit)

    grad_c, dq_conv, direct, tap_grad, point_grad, depth_grad = run(
        conv_back_kernel,
        [
            shaped((micro, rows, WIDTH), BF16), shaped((micro, rows, WIDTH), F32), shaped((micro, rows, D), F32),
            shaped((WIDTH, LANES), F32), shaped((D, WIDTH), F32), shaped((8 * KERNEL, D), F32),
        ],
        [grad_ext, kern_ext, c_ext, mask, mixed, q_ext, conv_key, pre_key, ext, grad_pre.reshape(micro, rows, D),
         w_tap, w_qcp, spread, taps],
        specs=[per_micro((span, WIDTH)), per_micro((span, LANES)), per_micro((span, WIDTH)), per_micro((span, LANES)),
               per_micro((rows, WIDTH)), per_micro((span, WIDTH)), per_micro((rows, WIDTH)), per_micro((rows, D)),
               per_micro((span, D)), per_micro((rows, D)), once(w_tap.shape), once(w_qcp.shape), once(spread.shape),
               once(taps.shape)],
        out_specs=[per_micro((rows, WIDTH)), per_micro((rows, WIDTH)), per_micro((rows, D)),
                   once((WIDTH, LANES)), once((D, WIDTH)), once((8 * KERNEL, D))],
        grid=(micro,),
        scratch=[pltpu.VMEM((span + 2 * PAD, WIDTH), F32), pltpu.VMEM((span + 2 * PAD, WIDTH), F32),
                 pltpu.VMEM((span + 2 * PAD, D), F32), pltpu.VMEM((span + 2 * PAD, WIDTH), F32),
                 pltpu.VMEM((rows, WIDTH), F32), pltpu.VMEM((span + 2 * PAD, D), F32)],
        flops=2 * flat * WIDTH * (3 * D + 512 * KERNEL),
    )

    wide = 3 * WIDTH
    depth = D // 8
    first_share = shaped((2, 2, depth + EXTRA, wide), BF16)
    grad_q, first_keep, first_send = run(
        first_grads_kernel,
        [shaped((flat, WIDTH), BF16), first_share, first_share],
        [pos, tokens_flat, dq_attn.reshape(flat, WIDTH), dq_conv.reshape(flat, WIDTH),
         grad_c.reshape(flat, WIDTH), point_grad, depth_grad, vector_grads, tap_grad],
        scratch=[pltpu.VMEM((flat, WIDTH), BF16), pltpu.VMEM((D, wide), F32), pltpu.VMEM((2, 4 * EXTRA, wide), F32)],
        flops=2 * flat * D * 2 * WIDTH,
    )
    second_share = shaped((2, 2, depth, 2 * WIDTH), BF16)
    grad_kv, second_keep, second_send = run(
        second_grads_kernel,
        [shaped((flat, 2 * WIDTH), BF16), second_share, second_share],
        [pos, tokens_flat, kv_parts[0].reshape(flat, 2 * WIDTH), kv_arrived.reshape(flat, 2 * WIDTH)],
        scratch=[pltpu.VMEM((flat, 2 * WIDTH), BF16), pltpu.VMEM((D, 2 * WIDTH), F32)],
        flops=2 * flat * D * 2 * WIDTH,
    )
    (input_grad,) = run(
        input_grad_kernel,
        [shaped((micro, rows, D), BF16)],
        [direct, grad_q.reshape(micro, rows, WIDTH), grad_kv.reshape(micro, rows, 2 * WIDTH), grad_c, w_kv, w_qcp],
        specs=[per_micro((rows, D)), per_micro((rows, WIDTH)), per_micro((rows, 2 * WIDTH)),
               per_micro((rows, WIDTH)), once(w_kv.shape), once(w_qcp.shape)],
        out_specs=[per_micro((rows, D))],
        grid=(micro,),
        flops=2 * flat * D * 4 * WIDTH,
    )

    f_own, f_other = gather_shares(reduce_ffn(reduce_shares(ffn_keep, ffn_send)))
    groups = ordered(f_own[:, 0], f_other[:, 0], core == 1)
    up_parts, down_parts = zip(*[ordered(g[0], g[1], (ctx // 2) % 2 == 1) for g in groups])
    up_grad = jnp.stack(up_parts, axis=1).astype(F32)
    down_grad = jnp.stack(down_parts, axis=1).astype(F32)
    first_shares = gather_shares(reduce_line(reduce_shares(first_keep, first_send)))
    second_shares = gather_shares(reduce_line(reduce_shares(second_keep, second_send)))
    in_grad, w_out_grad, w_point_grad, extra = run(
        unpack_kernel,
        [shaped((half, 4 * WIDTH), F32), shaped((half, D), F32), shaped((half, WIDTH), F32),
         shaped((4 * EXTRA, wide), F32)],
        [pos, f_own, f_other, *first_shares, *second_shares],
    )
    tap_sum = extra[:TAP_ROWS, : WIDTH // 2 // TAP_ROWS * LANES].reshape(TAP_ROWS, -1, LANES)
    tap_sum = tap_sum.transpose(1, 0, 2).reshape(WIDTH // 2, LANES)[:, : SLOT * KERNEL]
    tap_sum = tap_sum.reshape(-1, KERNEL, SLOT)[:, :, :HEADS].transpose(0, 2, 1).reshape(-1, HEADS * KERNEL)
    rest = extra[TAP_ROWS : TAP_ROWS + 16, :half]

    return (
        rows_out.reshape(micro, 1, rows, D),
        input_grad[:, None],
        in_grad,
        rest[:KERNEL].T,
        w_point_grad,
        tap_sum,
        w_out_grad,
        rest[KERNEL],
        rest[KERNEL + 1],
        rest[KERNEL + 2],
        rest[KERNEL + 3],
        up_grad,
        down_grad,
    )


def solution(mesh):
    return jax.shard_map(
        layer,
        mesh=mesh,
        in_specs=(
            P(None, ("dp", "tensor"), "ctx", None),
            P(None, ("dp", "tensor"), None),
            P("dp", None),
            P("dp", None),
            P("dp", None),
            P("dp", None),
            P("dp", None),
            P("dp"),
            P("dp"),
            P("dp"),
            P("dp"),
            P("dp", None, "tensor"),
            P("dp", None, "tensor"),
            P(None, ("dp", "tensor"), "ctx", None),
        ),
        out_specs=(
            P(None, ("dp", "tensor"), "ctx", None),
            P(None, ("dp", "tensor"), "ctx", None),
            P("dp", None),
            P("dp", None),
            P("dp", None),
            P("dp", None),
            P("dp", None),
            P("dp"),
            P("dp"),
            P("dp"),
            P("dp"),
            P("dp", None, "tensor"),
            P("dp", None, "tensor"),
        ),
        check_vma=False,
    )
```

time: 368 us -> 314 us (0.85); the launches traced: 361 us -> 313 us
  starting transfers between devices: 107 us -> 50.4 us
  waiting for transfers between devices: 74.9 us -> 109 us
  local copies, waits for them, and re-layouts: 38.3 us -> 20.9 us
  other arithmetic: 30.1 us -> 22.7 us
    ppermute x64 -> x37, waiting for transfers between devices: 58.5 us -> 106 us  [swap(): return lax.ppermute(block, axis, flips(axis, bit))]
    ppermute x64 -> x37, starting transfers between devices: 87.3 us -> 43.4 us  [swap(): return lax.ppermute(block, axis, flips(axis, bit))]
    ppermute x4 -> x0, waiting for transfers between devices: 12.3 us -> none  [swap_both(): return lax.ppermute(block, ('dp', 'ctx'), pairs)]
    another operation x14 -> x7, other arithmetic: 8.16 us -> 0.87 us  [the longest x1 0.57 us: layer(): bounds = jnp.stack([first, last])]
    ppermute x4 -> x2, starting transfers between devices: 9.48 us -> 4.33 us  [neighbours(): low = lax.ppermute(block[:, rows - HALO:], 'ctx', up)]
    convert_element_type x10 -> x16, other arithmetic: 7.92 us -> 12.9 us  [add_low(): return sum((b.astype(F32) for b in blocks)).astype(BF16)]
    slice x20 -> x10, local copies, waits for them, and re-layouts: 10.3 us -> 5.39 us  [the longest x2 1.97 us: side(): return jnp.where(core == 1, weight[:, 1], weight[:, 0])]
    ppermute x4 -> x0, starting transfers between devices: 4.62 us -> none  [swap_both(): return lax.ppermute(block, ('dp', 'ctx'), pairs)]
  transfers between devices with their start and end apart: 76 -> 41, of which waited for: 21 -> 20; matrix products, arithmetic and copies ran while one was open for 15% -> 10% of each run, Pallas kernels for 25% -> 23%
where the time goes in v3:
time: 314 us; the launch traced here: 313 us
  waiting for transfers between devices  109 us (35%)
  Pallas kernels  108 us (34%)
  starting transfers between devices  50.4 us (16%)
  other arithmetic  22.7 us (7%)
  local copies, waits for them, and re-layouts  20.9 us (7%)
    pallas_call x10, Pallas kernels, run(): pl.pallas_call(kernel, out_shape=tuple(outs), in_specs=specs, out_specs=t...  108 us
    ppermute x37, waiting for transfers between devices, swap(): return lax.ppermute(block, axis, flips(axis, bit))  106 us
    ppermute x37, starting transfers between devices, swap(): return lax.ppermute(block, axis, flips(axis, bit))  43.4 us
    convert_element_type x16, other arithmetic, add_low(): return sum((b.astype(F32) for b in blocks)).astype(BF16)  12.9 us
    unnamed x71, local copies, waits for them, and re-layouts  8.02 us
  transfers between devices with their start and end apart: 41, of which 20 were waited for; matrix products, arithmetic and copies ran while one was open for 10% of the time, Pallas kernels for 23%

profile of v3, /device:TPU:0, one launch (start us, length us, event | category | flops | bytes accessed | tf_op | source)
XLA Modules:
  0.0 313.0 jit_solution(16889539414541585232)
XLA Ops:
  17.9 4.0 %shard_map.238 = (bf16[512,768]{1,0:T(8,128)(2,1)}, bf16[768,768]{1,0:T(8,128)(2,1)}) custom-call(s32[5]{0:T(128)} %stack.100.pos, bf16[512,768]{1,0:T(8,128)(2,1)} %bitcast.135, bf16[384,1536]{1,0:T(8,128)(2,1)} %own.1, bf16[192,768]{1,0:T(8,128)(2,1)} %copy-done.16, bf16[192,768]{1,0:T(8,128)(2,1)} %copy-done.17), custom_call_target="tpu_custom_call" | custom-call | flops 603979776 | bytes 4522004 | tf_op jit(solution)/shard_map/pallas_call | solution.py:74
  23.9 2.6 collective-permute-start.9
  28.2 6.3 %collective-permute-done.2.mine.mine_out = bf16[192,2048]{1,0:T(8,128)(2,1)S(1)} collective-permute-done((bf16[192,2048]{1,0:T(8,128)(2,1)S(1)}, bf16[192,2048]{1,0:T(8,128)(2,1)S(1)}, u32[]{:S(2)}, u32[]{:S(2)}) %collective-permute-start.2) | collective-permute-done | bytes 786464 | tf_op jit(solution)/shard_map/ppermute | solution.py:625
  35.5 17.3 %collective-permute-done.9.rest_1_ = bf16[2,2,192,384]{3,2,1,0:T(8,128)(2,1)} collective-permute-done((bf16[2,2,192,384]{3,2,1,0:T(8,128)(2,1)}, bf16[2,2,192,384]{3,2,1,0:T(8,128)(2,1)}, u32[]{:S(2)}, u32[]{:S(2)}) %collective-permute-start.9) | collective-permute-done | bytes 589856 | tf_op jit(solution)/shard_map/ppermute | solution.py:625
  61.6 3.0 collective-permute-start.12
  64.6 2.9 collective-permute-done.11.rest_3_
  70.2 14.4 %shard_map.237 = (bf16[2,288,384]{2,1,0:T(8,128)(2,1)}, bf16[2,288,384]{2,1,0:T(8,128)(2,1)}, bf16[2,256,768]{2,1,0:T(8,128)(2,1)}, f32[2,256,384]{2,1,0:T(8,128...) custom-call(s32[5]{0:T(128)} %stack.100.pos, ...), custom_call_target="tpu_custom_call" | custom-call | flops 1811939328 | bytes 11461012 | tf_op jit(solution)/shard_map/pallas_call | solution.py:74
  84.6 10.3 %shard_map.239 = (bf16[2,256,384]{2,1,0:T(8,128)(2,1)}, f32[2,384,256]{2,1,0:T(8,128)}, f32[2,8,256]{2,1,0:T(8,128)}) custom-call(s32[2,2]{1,0:T(2,128)} %pad_add_fusion.bounds, s32[5]{0:T(128)} %stack.100.pos, bf16[2,288,384]{2,1,0:T(8,128)(2,1)} %get-tuple-element.53.q_ext, bf16[2,2,256,768]{3,2,1,0:T(8,128)(2,1)} %copy-done.4, ...), custom_call_target="tpu_custom_call" | custom-call | flops 3221225472 | bytes 4794788 | tf_op jit(solution)/shard_map/pallas_call | solution.py:74
  95.7 32.3 %shard_map.240 = (bf16[512,768]{1,0:T(8,128)(2,1)}, f32[512,768]{1,0:T(8,128)}, bf16[512,384]{1,0:T(8,128)(2,1)}, bf16[512,384]{1,0:T(8,128)(2,1)}, bf16[2,2,5,1...) custom-call(s32[5]{0:T(128)} %stack.100.pos, bf16[512,384]{1,0:T(8,128)(2,1)} %bitcast.170, ...), custom_call_target="tpu_custom_call" | custom-call | flops 5435817984 | bytes 18321428 | tf_op jit(solution)/shard_map/pallas_call | solution.py:74
  128.1 12.1 %shard_map.242 = (f32[2,256,384]{2,1,0:T(8,128)}, bf16[2,2,256,768]{3,2,1,0:T(8,128)(2,1)}, bf16[2,2,256,768]{3,2,1,0:T(8,128)(2,1)}) custom-call(s32[2,2]{1,0:T(2,128)} %pad_add_fusion.bounds, s32[5]{0:T(128)} %stack.100.pos, bf16[2,288,384]{2,1,0:T(8,128)(2,1)} %get-tuple-element.53.q_ext, bf16[2,256,384]{2,1,0:T(8,128)(2,1)} %bitcast.169, ...), custom_call_target="tpu_custom_call" | custom-call | flops 8053063680 | bytes 8726948 | tf_op jit(solution)/shard_map/pallas_call | solution.py:74
  144.1 3.3 %collective-permute-done.17 = bf16[2,16,384]{2,1,0:T(8,128)(2,1)S(1)} collective-permute-done((bf16[2,16,384]{2,1,0:T(8,128)(2,1)S(1)}, bf16[2,16,384]{2,1,0:T(8,128)(2,1)S(1)}, u32[]{:S(2)}, u32[]{:S(2)}) %collective-permute-start.17) | collective-permute-done | bytes 24608 | tf_op jit(solution)/shard_map/ppermute | solution.py:684
  148.2 17.8 %shard_map.241 = (bf16[2,256,384]{2,1,0:T(8,128)(2,1)}, f32[2,256,384]{2,1,0:T(8,128)}, f32[2,256,768]{2,1,0:T(8,128)}, f32[384,128]{1,0:T(8,128)}, f32[768,384]{1,0:T(8,128)}, /*index=5*/f32[72,768]{1,0:T(8,128)}) custom-call(bf16[2,288,384]{2,1,0:T(8,128)(2,1)} %pad_maximum_fusion.5.grad_ext, f32[2,288,128]{2,1,0:T(8,128)} %get-tuple-element.59.kern_ext, ...), custom_call_target="tpu_custom_call" | custom-call | flops 2717908992 | bytes 14376960 | tf_op jit(solution)/shard_map/pallas_call | solution.py:74
  166.1 5.0 %shard_map.243 = (bf16[512,384]{1,0:T(8,128)(2,1)}, bf16[2,2,112,1152]{3,2,1,0:T(8,128)(2,1)}, bf16[2,2,112,1152]{3,2,1,0:T(8,128)(2,1)}) custom-call(s32[5]{0:T(128)} %stack.100.pos, bf16[512,768]{1,0:T(8,128)(2,1)} %bitcast.137, f32[512,384]{1,0:T(8,128)} %bitcast.145, f32[512,384]{1,0:T(8,128)} %bitcast.146, bf16[512,384]{1,0:T(8,128)(2,1)} %bitcast.141, ...), custom_call_target="tpu_custom_call" | custom-call | flops 603979776 | bytes 6832148 | tf_op jit(solution)/shard_map/pallas_call | solution.py:74
  171.0 2.5 collective-permute-start.27
  173.6 3.0 fusion.1
  176.6 12.1 %collective-permute-start.21 = (bf16[2,5,192,384]{3,2,1,0:T(8,128)(2,1)}, bf16[2,5,192,384]{3,2,1,0:T(8,128)(2,1)}, u32[]{:S(2)}, u32[]{:S(2)}) collective-permute-start(bf16[2,5,192,384]{3,2,1,0:T(8,128)(2,1)} %fusion.1), channel_id=1, source_target_pairs={{0,16},{16,0},{1,17},{17,1},{2,18},{18,2},{3,19},{19,3},{4,20},{20... | collective-permute-start | bytes 4423688 | tf_op jit(solution)/shard_map/ppermute | solution.py:625
  188.7 2.7 fusion.5
  191.4 19.3 %collective-permute-done.19 = bf16[2,256,768]{2,1,0:T(8,128)(2,1)} collective-permute-done((bf16[2,256,768]{2,1,0:T(8,128)(2,1)S(1)}, bf16[2,256,768]{2,1,0:T(8,128)(2,1)}, u32[]{:S(2)}, u32[]{:S(2)}) %collective-permute-start.19) | collective-permute-done | bytes 786464 | tf_op jit(solution)/shard_map/ppermute | solution.py:625
  210.6 3.5 %shard_map.244 = (bf16[512,768]{1,0:T(8,128)(2,1)}, bf16[2,2,96,768]{3,2,1,0:T(8,128)(2,1)}, bf16[2,2,96,768]{3,2,1,0:T(8,128)(2,1)}) custom-call(s32[5]{0:T(128)} %stack.100.pos, bf16[512,768]{1,0:T(8,128)(2,1)} %bitcast.138, bf16[512,768]{1,0:T(8,128)(2,1)} %bitcast.140, bf16[512,768]{1,0:T(8,128)(2,1)} %bitcast.33.arrived), custom_call_target="tpu_custom_call" | custom-call | flops 603979776 | bytes 4325396 | tf_op jit(solution)/shard_map/pallas_call | solution.py:74
  215.7 6.4 %collective-permute-done.21 = bf16[2,5,192,384]{3,2,1,0:T(8,128)(2,1)} collective-permute-done((bf16[2,5,192,384]{3,2,1,0:T(8,128)(2,1)}, bf16[2,5,192,384]{3,2,1,0:T(8,128)(2,1)}, u32[]{:S(2)}, u32[]{:S(2)}) %collective-permute-start.21) | collective-permute-done | bytes 1474592 | tf_op jit(solution)/shard_map/ppermute | solution.py:625
  226.0 7.1 %collective-permute-done.28 = bf16[2,112,1152]{2,1,0:T(8,128)(2,1)S(1)} collective-permute-done((bf16[2,112,1152]{2,1,0:T(8,128)(2,1)S(1)}, bf16[2,112,1152]{2,1,0:T(8,128)(2,1)S(1)}, u32[]{:S(2)}, u32[]{:S(2)}) %collective-permute-start.28) | collective-permute-done | bytes 516128 | tf_op jit(solution)/shard_map/ppermute | solution.py:625
  234.2 4.5 %collective-permute-done.35 = bf16[2,96,768]{2,1,0:T(8,128)(2,1)S(1)} collective-permute-done((bf16[2,96,768]{2,1,0:T(8,128)(2,1)S(1)}, bf16[2,96,768]{2,1,0:T(8,128)(2,1)S(1)}, u32[]{:S(2)}, u32[]{:S(2)}) %collective-permute-start.35) | collective-permute-done | bytes 294944 | tf_op jit(solution)/shard_map/ppermute | solution.py:625
  239.2 3.9 %collective-permute-done.22 = bf16[5,192,384]{2,1,0:T(8,128)(2,1)S(1)} collective-permute-done((bf16[5,192,384]{2,1,0:T(8,128)(2,1)S(1)}, bf16[5,192,384]{2,1,0:T(8,128)(2,1)S(1)}, u32[]{:S(2)}, u32[]{:S(2)}) %collective-permute-start.22) | collective-permute-done | bytes 737312 | tf_op jit(solution)/shard_map/ppermute | solution.py:625
  245.1 3.0 collective-permute-done.29
  251.4 9.3 %collective-permute-done.23 = bf16[3,192,384]{2,1,0:T(8,128)(2,1)S(1)} collective-permute-done((bf16[3,192,384]{2,1,0:T(8,128)(2,1)S(1)}, bf16[3,192,384]{2,1,0:T(8,128)(2,1)S(1)}, u32[]{:S(2)}, u32[]{:S(2)}) %collective-permute-start.23) | collective-permute-done | bytes 442400 | tf_op jit(solution)/shard_map/ppermute | solution.py:625
  260.9 5.3 %collective-permute-done.30 = bf16[112,1152]{1,0:T(8,128)(2,1)S(1)} collective-permute-done((bf16[112,1152]{1,0:T(8,128)(2,1)S(1)}, bf16[112,1152]{1,0:T(8,128)(2,1)S(1)}, u32[]{:S(2)}, u32[]{:S(2)}) %collective-permute-start.30) | collective-permute-done | bytes 258080 | tf_op jit(solution)/shard_map/ppermute | solution.py:625
  269.4 11.4 %collective-permute-done.24 = bf16[2,192,384]{2,1,0:T(8,128)(2,1)S(1)} collective-permute-done((bf16[2,192,384]{2,1,0:T(8,128)(2,1)S(1)}, bf16[2,192,384]{2,1,0:T(8,128)(2,1)S(1)}, u32[]{:S(2)}, u32[]{:S(2)}) %collective-permute-start.24) | collective-permute-done | bytes 294944 | tf_op jit(solution)/shard_map/ppermute | solution.py:625
  281.0 2.9 collective-permute-start.25
  284.0 2.6 collective-permute-start.32
  289.6 2.6 collective-permute-done.32
  293.9 5.0 %shard_map.245 = bf16[2,256,768]{2,1,0:T(8,128)(2,1)} custom-call(f32[2,256,768]{2,1,0:T(8,128)} %get-tuple-element.67.direct, bf16[2,256,384]{2,1,0:T(8,128)(2,1)} %bitcast.155, bf16[2,256,768]{2,1,0:T(8,128)(2,1)} %bitcast.149, bf16[2,256,384]{2,1,0:T(8,128)(2,1)} %get-tuple-element.73.grad_c, bf16[768,768]{1,0:T(8,128)(2,1)} %get-tuple-element.82.w_kv, ...), custom_call_target="tpu_custom_call" | custom-call | flops 1207959552 | bytes 6881280 | tf_op jit(solution)/shard_map/pallas_call | solution.py:74
  300.7 4.1 %shard_map.246 = (f32[384,1536]{1,0:T(8,128)}, f32[384,768]{1,0:T(8,128)}, f32[384,384]{1,0:T(8,128)}, f32[64,1152]{1,0:T(8,128)}) custom-call(s32[5]{0:T(128)} %stack.100.pos, bf16[2,2,192,384]{3,2,1,0:T(8,128)(2,1)} %copy-done.2, bf16[2,2,192,384]{3,2,1,0:T(8,128)(2,1)} %copy-done.6, bf16[2,112,1152]{2,1,0:T(8,128)(2,1)} %copy-done.3, ...), custom_call_target="tpu_custom_call" | custom-call | bytes 7225364 | tf_op jit(solution)/shard_map/pallas_call | solution.py:74
  (212 shorter events, 69.0 us)
Async XLA Ops:
  2.2 55.1 %collective-permute-start = (bf16[2,16,768]{2,1,0:T(8,128)(2,1)}, bf16[2,16,768]{2,1,0:T(8,128)(2,1)S(1)}, u32[]{:S(2)}, u32[]{:S(2)}) collective-permute-start(bf16[2,16,768]{2,1,0:T(8,128)(2,1)} %get-tuple-element.148), channel_id=1, source_target_pairs={{0,4},{4,8},{8,12},{1,5},{5,9},{9,13},{2,6},{6,10},{10,14},{3,7},{... | collective-permute-start | bytes 147464 | tf_op jit(solution)/shard_map/ppermute | solution.py:683
  5.6 9.3 %collective-permute-start.4 = (bf16[192,768]{1,0:T(8,128)(2,1)S(1)}, bf16[192,768]{1,0:T(8,128)(2,1)S(1)}, u32[]{:S(2)}, u32[]{:S(2)}) collective-permute-start(bf16[192,768]{1,0:T(8,128)(2,1)S(1)} %dynamic-slice.3), channel_id=1, source_target_pairs={{0,16},{16,0},{1,17},{17,1},{2,18},{18,2},{3,19},{19,3},{4,20},{20... | collective-permute-start | bytes 884744 | tf_op jit(solution)/shard_map/ppermute | solution.py:625
  10.2 12.8 %collective-permute-start.8 = (bf16[1,2,192,384]{3,2,1,0:T(8,128)(2,1)S(1)}, bf16[1,2,192,384]{3,2,1,0:T(8,128)(2,1)S(1)}, u32[]{:S(2)}, u32[]{:S(2)}) collective-permute-start(bf16[1,2,192,384]{3,2,1,0:T(8,128)(2,1)S(1)} %maximum_bitcast_fusion), channel_id=1, source_target_pairs={{0,1},{1,0},{2,3},{3,2},{4,5},{5,4},{6,7},{7,6},{8,9},{9,8},{10,11... | collective-permute-start | bytes 884744 | tf_op jit(solution)/shard_map/ppermute | solution.py:625
  14.2 20.2 %collective-permute-start.2 = (bf16[192,2048]{1,0:T(8,128)(2,1)S(1)}, bf16[192,2048]{1,0:T(8,128)(2,1)S(1)}, u32[]{:S(2)}, u32[]{:S(2)}) collective-permute-start(bf16[192,2048]{1,0:T(8,128)(2,1)S(1)} %select_dynamic-update-slice_fusion), channel_id=1, source_target_pairs={{0,16},{16,0},{1,17},{17,1},{2,18},{18,2},{3,19},{19,3},{4,20},{20... | collective-permute-start | bytes 2359304 | tf_op jit(solution)/shard_map/ppermute | solution.py:625
  21.9 32.5 %collective-permute-start.6 = (bf16[1,2,256,768]{3,2,1,0:T(8,128)(2,1)}, bf16[1,2,256,768]{3,2,1,0:T(8,128)(2,1)}, u32[]{:S(2)}, u32[]{:S(2)}) collective-permute-start(bf16[1,2,256,768]{3,2,1,0:T(8,128)(2,1)} %bitcast.147), channel_id=1, source_target_pairs={{0,8},{4,12},{8,0},{12,4},{1,9},{5,13},{9,1},{13,5},{2,10},{6,14},... | collective-permute-start | bytes 2359304 | tf_op jit(solution)/shard_map/ppermute | solution.py:625
  23.9 28.9 %collective-permute-start.9 = (bf16[2,2,192,384]{3,2,1,0:T(8,128)(2,1)}, bf16[2,2,192,384]{3,2,1,0:T(8,128)(2,1)}, u32[]{:S(2)}, u32[]{:S(2)}) collective-permute-start(bf16[2,2,192,384]{3,2,1,0:T(8,128)(2,1)} %pad_maximum_fusion.3.rest_0_), channel_id=1, source_target_pairs={{0,2},{1,3},{2,0},{3,1},{4,6},{5,7},{6,4},{7,5},{8,10},{9,11},{10,... | collective-permute-start | bytes 1769480 | tf_op jit(solution)/shard_map/ppermute | solution.py:625
  34.4 33.1 %collective-permute-start.3 = (bf16[192,2048]{1,0:T(8,128)(2,1)S(1)}, bf16[192,2048]{1,0:T(8,128)(2,1)}, u32[]{:S(2)}, u32[]{:S(2)}) collective-permute-start(bf16[192,2048]{1,0:T(8,128)(2,1)S(1)} %collective-permute-done.2.mine.mine_out), channel_id=1, source_target_pairs={{0,4},{4,0},{8,12},{12,8},{1,5},{5,1},{9,13},{13,9},{2,6},{6,2},{1... | collective-permute-start | bytes 2359304 | tf_op jit(solution)/shard_map/ppermute | solution.py:625
  35.0 29.6 %collective-permute-start.10 = (bf16[2,2,192,384]{3,2,1,0:T(8,128)(2,1)}, bf16[2,2,192,384]{3,2,1,0:T(8,128)(2,1)}, u32[]{:S(2)}, u32[]{:S(2)}) collective-permute-start(bf16[2,2,192,384]{3,2,1,0:T(8,128)(2,1)} %pad_maximum_fusion.3.rest_0_), channel_id=1, source_target_pairs={{0,16},{16,0},{1,17},{17,1},{2,18},{18,2},{3,19},{19,3},{4,20},{20... | collective-permute-start | bytes 1769480 | tf_op jit(solution)/shard_map/ppermute | solution.py:625
  52.9 14.6 %collective-permute-start.11 = (bf16[2,2,192,384]{3,2,1,0:T(8,128)(2,1)}, bf16[2,2,192,384]{3,2,1,0:T(8,128)(2,1)}, u32[]{:S(2)}, u32[]{:S(2)}) collective-permute-start(bf16[2,2,192,384]{3,2,1,0:T(8,128)(2,1)} %collective-permute-done.9.rest_1_), channel_id=1, source_target_pairs={{0,16},{16,0},{1,17},{17,1},{2,18},{18,2},{3,19},{19,3},{4,20},{20... | collective-permute-start | bytes 1769480 | tf_op jit(solution)/shard_map/ppermute | solution.py:625
  55.9 28.7 %collective-permute-start.7 = (bf16[2,2,256,768]{3,2,1,0:T(8,128)(2,1)S(1)}, bf16[2,2,256,768]{3,2,1,0:T(8,128)(2,1)}, u32[]{:S(2)}, u32[]{:S(2)}) collective-permute-start(bf16[2,2,256,768]{3,2,1,0:T(8,128)(2,1)S(1)} %pad_maximum_fusion.kv_near), channel_id=1, source_target_pairs={{0,4},{4,0},{8,12},{12,8},{1,5},{5,1},{9,13},{13,9},{2,6},{6,2},{1... | collective-permute-start | bytes 4718600 | tf_op jit(solution)/shard_map/ppermute | solution.py:625
  61.6 33.3 %collective-permute-start.12 = (bf16[2,2,192,384]{3,2,1,0:T(8,128)(2,1)}, bf16[2,2,192,384]{3,2,1,0:T(8,128)(2,1)S(1)}, u32[]{:S(2)}, u32[]{:S(2)}) collective-permute-start(bf16[2,2,192,384]{3,2,1,0:T(8,128)(2,1)} %pad_maximum_fusion.3.rest_0_), channel_id=1, source_target_pairs={{0,4},{4,0},{8,12},{12,8},{1,5},{5,1},{9,13},{13,9},{2,6},{6,2},{1... | collective-permute-start | bytes 1769480 | tf_op jit(solution)/shard_map/ppermute | solution.py:625
  64.6 30.3 %collective-permute-start.13 = (bf16[2,2,192,384]{3,2,1,0:T(8,128)(2,1)}, bf16[2,2,192,384]{3,2,1,0:T(8,128)(2,1)}, u32[]{:S(2)}, u32[]{:S(2)}) collective-permute-start(bf16[2,2,192,384]{3,2,1,0:T(8,128)(2,1)} %collective-permute-done.9.rest_1_), channel_id=1, source_target_pairs={{0,4},{4,0},{8,12},{12,8},{1,5},{5,1},{9,13},{13,9},{2,6},{6,2},{1... | collective-permute-start | bytes 1769480 | tf_op jit(solution)/shard_map/ppermute | solution.py:625
  67.5 27.4 %collective-permute-start.14 = (bf16[2,2,192,384]{3,2,1,0:T(8,128)(2,1)}, bf16[2,2,192,384]{3,2,1,0:T(8,128)(2,1)}, u32[]{:S(2)}, u32[]{:S(2)}) collective-permute-start(bf16[2,2,192,384]{3,2,1,0:T(8,128)(2,1)} %collective-permute-done.10.rest_2_), channel_id=1, source_target_pairs={{0,4},{4,0},{8,12},{12,8},{1,5},{5,1},{9,13},{13,9},{2,6},{6,2},{1... | collective-permute-start | bytes 1769480 | tf_op jit(solution)/shard_map/ppermute | solution.py:625
  67.5 27.4 %collective-permute-start.15 = (bf16[2,2,192,384]{3,2,1,0:T(8,128)(2,1)}, bf16[2,2,192,384]{3,2,1,0:T(8,128)(2,1)}, u32[]{:S(2)}, u32[]{:S(2)}) collective-permute-start(bf16[2,2,192,384]{3,2,1,0:T(8,128)(2,1)} %collective-permute-done.11.rest_3_), channel_id=1, source_target_pairs={{0,4},{4,0},{8,12},{12,8},{1,5},{5,1},{9,13},{13,9},{2,6},{6,2},{1... | collective-permute-start | bytes 1769480 | tf_op jit(solution)/shard_map/ppermute | solution.py:625
  128.0 45.6 %collective-permute-start.20 = (bf16[2,2,5,192,384]{4,3,2,1,0:T(8,128)(2,1)}, bf16[2,2,5,192,384]{4,3,2,1,0:T(8,128)(2,1)}, u32[]{:S(2)}, u32[]{:S(2)}) collective-permute-start(bf16[2,2,5,192,384]{4,3,2,1,0:T(8,128)(2,1)} %get-tuple-element.84), channel_id=1, source_target_pairs={{0,4},{4,0},{8,12},{12,8},{1,5},{5,1},{9,13},{13,9},{2,6},{6,2},{1... | collective-permute-start | bytes 8847368 | tf_op jit(solution)/shard_map/ppermute | solution.py:625
  140.2 48.5 %collective-permute-start.18 = (bf16[2,2,256,768]{3,2,1,0:T(8,128)(2,1)}, bf16[2,2,256,768]{3,2,1,0:T(8,128)(2,1)}, u32[]{:S(2)}, u32[]{:S(2)}) collective-permute-start(bf16[2,2,256,768]{3,2,1,0:T(8,128)(2,1)} %get-tuple-element.80), channel_id=1, source_target_pairs={{0,4},{4,0},{8,12},{12,8},{1,5},{5,1},{9,13},{13,9},{2,6},{6,2},{1... | collective-permute-start | bytes 4718600 | tf_op jit(solution)/shard_map/ppermute | solution.py:625
  171.0 43.1 %collective-permute-start.27 = (bf16[2,2,112,1152]{3,2,1,0:T(8,128)(2,1)}, bf16[2,2,112,1152]{3,2,1,0:T(8,128)(2,1)}, u32[]{:S(2)}, u32[]{:S(2)}) collective-permute-start(bf16[2,2,112,1152]{3,2,1,0:T(8,128)(2,1)} %get-tuple-element.86), channel_id=1, source_target_pairs={{0,4},{4,0},{8,12},{12,8},{1,5},{5,1},{9,13},{13,9},{2,6},{6,2},{1... | collective-permute-start | bytes 3096584 | tf_op jit(solution)/shard_map/ppermute | solution.py:625
  176.6 45.6 %collective-permute-start.21 = (bf16[2,5,192,384]{3,2,1,0:T(8,128)(2,1)}, bf16[2,5,192,384]{3,2,1,0:T(8,128)(2,1)}, u32[]{:S(2)}, u32[]{:S(2)}) collective-permute-start(bf16[2,5,192,384]{3,2,1,0:T(8,128)(2,1)} %fusion.1), channel_id=1, source_target_pairs={{0,16},{16,0},{1,17},{17,1},{2,18},{18,2},{3,19},{19,3},{4,20},{20... | collective-permute-start | bytes 4423688 | tf_op jit(solution)/shard_map/ppermute | solution.py:625
  191.4 19.3 %collective-permute-start.19 = (bf16[2,256,768]{2,1,0:T(8,128)(2,1)S(1)}, bf16[2,256,768]{2,1,0:T(8,128)(2,1)}, u32[]{:S(2)}, u32[]{:S(2)}) collective-permute-start(bf16[2,256,768]{2,1,0:T(8,128)(2,1)S(1)} %get-tuple-element.138), channel_id=1, source_target_pairs={{0,8},{4,12},{8,0},{12,4},{1,9},{5,13},{9,1},{13,5},{2,10},{6,14},... | collective-permute-start | bytes 2359304 | tf_op jit(solution)/shard_map/ppermute | solution.py:625
  214.2 9.7 %collective-permute-start.34 = (bf16[2,2,96,768]{3,2,1,0:T(8,128)(2,1)}, bf16[2,2,96,768]{3,2,1,0:T(8,128)(2,1)S(1)}, u32[]{:S(2)}, u32[]{:S(2)}) collective-permute-start(bf16[2,2,96,768]{3,2,1,0:T(8,128)(2,1)} %get-tuple-element.88), channel_id=1, source_target_pairs={{0,4},{4,0},{8,12},{12,8},{1,5},{5,1},{9,13},{13,9},{2,6},{6,2},{1... | collective-permute-start | bytes 1769480 | tf_op jit(solution)/shard_map/ppermute | solution.py:625
  215.4 17.7 %collective-permute-start.28 = (bf16[2,112,1152]{2,1,0:T(8,128)(2,1)S(1)}, bf16[2,112,1152]{2,1,0:T(8,128)(2,1)S(1)}, u32[]{:S(2)}, u32[]{:S(2)}) collective-permute-start(bf16[2,112,1152]{2,1,0:T(8,128)(2,1)S(1)} %fusion.6), channel_id=1, source_target_pairs={{0,16},{16,0},{1,17},{17,1},{2,18},{18,2},{3,19},{19,3},{4,20},{20... | collective-permute-start | bytes 1548296 | tf_op jit(solution)/shard_map/ppermute | solution.py:625
  223.7 19.4 %collective-permute-start.22 = (bf16[5,192,384]{2,1,0:T(8,128)(2,1)S(1)}, bf16[5,192,384]{2,1,0:T(8,128)(2,1)S(1)}, u32[]{:S(2)}, u32[]{:S(2)}) collective-permute-start(bf16[5,192,384]{2,1,0:T(8,128)(2,1)S(1)} %fusion.2), channel_id=1, source_target_pairs={{0,8},{4,12},{8,0},{12,4},{1,9},{5,13},{9,1},{13,5},{2,10},{6,14},... | collective-permute-start | bytes 2211848 | tf_op jit(solution)/shard_map/ppermute | solution.py:625
  223.9 14.8 %collective-permute-start.35 = (bf16[2,96,768]{2,1,0:T(8,128)(2,1)S(1)}, bf16[2,96,768]{2,1,0:T(8,128)(2,1)S(1)}, u32[]{:S(2)}, u32[]{:S(2)}) collective-permute-start(bf16[2,96,768]{2,1,0:T(8,128)(2,1)S(1)} %fusion.10), channel_id=1, source_target_pairs={{0,16},{16,0},{1,17},{17,1},{2,18},{18,2},{3,19},{19,3},{4,20},{20... | collective-permute-start | bytes 884744 | tf_op jit(solution)/shard_map/ppermute | solution.py:625
  234.1 14.0 %collective-permute-start.29 = (bf16[112,1152]{1,0:T(8,128)(2,1)S(1)}, bf16[112,1152]{1,0:T(8,128)(2,1)S(1)}, u32[]{:S(2)}, u32[]{:S(2)}) collective-permute-start(bf16[112,1152]{1,0:T(8,128)(2,1)S(1)} %fusion.7), channel_id=1, source_target_pairs={{0,8},{4,12},{8,0},{12,4},{1,9},{5,13},{9,1},{13,5},{2,10},{6,14},... | collective-permute-start | bytes 774152 | tf_op jit(solution)/shard_map/ppermute | solution.py:625
  238.8 10.9 %collective-permute-start.36 = (bf16[96,768]{1,0:T(8,128)(2,1)S(1)}, bf16[96,768]{1,0:T(8,128)(2,1)S(1)}, u32[]{:S(2)}, u32[]{:S(2)}) collective-permute-start(bf16[96,768]{1,0:T(8,128)(2,1)S(1)} %fusion.12), channel_id=1, source_target_pairs={{0,8},{4,12},{8,0},{12,4},{1,9},{5,13},{9,1},{13,5},{2,10},{6,14},... | collective-permute-start | bytes 442376 | tf_op jit(solution)/shard_map/ppermute | solution.py:625
  245.0 15.7 %collective-permute-start.23 = (bf16[3,192,384]{2,1,0:T(8,128)(2,1)S(1)}, bf16[3,192,384]{2,1,0:T(8,128)(2,1)S(1)}, u32[]{:S(2)}, u32[]{:S(2)}) collective-permute-start(bf16[3,192,384]{2,1,0:T(8,128)(2,1)S(1)} %pad_maximum_fusion.6), channel_id=1, source_target_pairs={{0,1},{1,0},{2,3},{3,2},{4,5},{5,4},{6,7},{7,6},{8,9},{9,8},{10,11... | collective-permute-start | bytes 1327112 | tf_op jit(solution)/shard_map/ppermute | solution.py:625
  249.2 17.1 %collective-permute-start.30 = (bf16[112,1152]{1,0:T(8,128)(2,1)S(1)}, bf16[112,1152]{1,0:T(8,128)(2,1)S(1)}, u32[]{:S(2)}, u32[]{:S(2)}) collective-permute-start(bf16[112,1152]{1,0:T(8,128)(2,1)S(1)} %fusion.9), channel_id=1, source_target_pairs={{0,1},{1,0},{2,3},{3,2},{4,5},{5,4},{6,7},{7,6},{8,9},{9,8},{10,11... | collective-permute-start | bytes 774152 | tf_op jit(solution)/shard_map/ppermute | solution.py:625
  249.7 19.1 %collective-permute-start.37 = (bf16[96,768]{1,0:T(8,128)(2,1)S(1)}, bf16[96,768]{1,0:T(8,128)(2,1)S(1)}, u32[]{:S(2)}, u32[]{:S(2)}) collective-permute-start(bf16[96,768]{1,0:T(8,128)(2,1)S(1)} %fusion.14), channel_id=1, source_target_pairs={{0,1},{1,0},{2,3},{3,2},{4,5},{5,4},{6,7},{7,6},{8,9},{9,8},{10,11... | collective-permute-start | bytes 442376 | tf_op jit(solution)/shard_map/ppermute | solution.py:625
  260.8 20.0 %collective-permute-start.24 = (bf16[2,192,384]{2,1,0:T(8,128)(2,1)S(1)}, bf16[2,192,384]{2,1,0:T(8,128)(2,1)S(1)}, u32[]{:S(2)}, u32[]{:S(2)}) collective-permute-start(bf16[2,192,384]{2,1,0:T(8,128)(2,1)S(1)} %pad_maximum_fusion.7), channel_id=1, source_target_pairs={{0,2},{1,3},{2,0},{3,1},{4,6},{5,7},{6,4},{7,5},{8,10},{9,11},{10,... | collective-permute-start | bytes 884744 | tf_op jit(solution)/shard_map/ppermute | solution.py:625
  266.3 17.6 %collective-permute-start.31 = (bf16[112,1152]{1,0:T(8,128)(2,1)S(1)}, bf16[112,1152]{1,0:T(8,128)(2,1)S(1)}, u32[]{:S(2)}, u32[]{:S(2)}) collective-permute-start(bf16[112,1152]{1,0:T(8,128)(2,1)S(1)} %add_convert_fusion.6), channel_id=1, source_target_pairs={{0,2},{1,3},{2,0},{3,1},{4,6},{5,7},{6,4},{7,5},{8,10},{9,11},{10,... | collective-permute-start | bytes 774152 | tf_op jit(solution)/shard_map/ppermute | solution.py:625
  268.9 17.7 %collective-permute-start.38 = (bf16[96,768]{1,0:T(8,128)(2,1)S(1)}, bf16[96,768]{1,0:T(8,128)(2,1)S(1)}, u32[]{:S(2)}, u32[]{:S(2)}) collective-permute-start(bf16[96,768]{1,0:T(8,128)(2,1)S(1)} %add_convert_fusion.8), channel_id=1, source_target_pairs={{0,2},{1,3},{2,0},{3,1},{4,6},{5,7},{6,4},{7,5},{8,10},{9,11},{10,... | collective-permute-start | bytes 442376 | tf_op jit(solution)/shard_map/ppermute | solution.py:625
  289.5 9.5 %collective-permute-start.26 = (bf16[2,2,192,384]{3,2,1,0:T(8,128)(2,1)S(1)}, bf16[2,2,192,384]{3,2,1,0:T(8,128)(2,1)S(1)}, u32[]{:S(2)}, u32[]{:S(2)}) collective-permute-start(bf16[2,2,192,384]{3,2,1,0:T(8,128)(2,1)S(1)} %pad_maximum_fusion.2.f_own), channel_id=1, source_target_pairs={{0,4},{4,0},{8,12},{12,8},{1,5},{5,1},{9,13},{13,9},{2,6},{6,2},{1... | collective-permute-start | bytes 1769480 | tf_op jit(solution)/shard_map/ppermute | solution.py:625
  (39 other events, 292.6 us)
